TPU v7x, 128 devices: a whole 4x4x4 slice. The times are simulated.
128 devices in a mesh: row: 16 (over y, x), col: 8 (over z, core).
Axes of the slice: x: 4, y: 4, z: 4, core: 2. Of those that a mesh axis runs over, the one named last changes fastest.
Arguments:
- tokens: bfloat16 [16384, 1280], P(('row', 'col')), may hold values from -6 to 6
- image_sizes: int32 [16, 8], replicated, may hold values from 1 to 48, 256 in all within a row
- slot_of: int32 [128], replicated, may hold values from 0 to 127, as said below
- ln_gain: float32 [1, 2, 1280], replicated, may hold values from 0.25 to 1.75
- ln_bias: float32 [1, 2, 1280], replicated, may hold values from -3 to 3
- w_qkv: bfloat16 [1, 1280, 3840], P(None, 'row', 'col')
- w_out: bfloat16 [1, 1280, 1280], P(None, 'col', 'row'), may hold values from -0.15625 to 0.15625
- w_up: bfloat16 [1, 1280, 5120], P(None, 'row', 'col'), may hold values from -0.15625 to 0.15625
- w_down: bfloat16 [1, 5120, 1280], P(None, 'col', 'row'), may hold values from -0.078125 to 0.078125
- merge_gain: float32 [1280], replicated, may hold values from 0.25 to 1.75
- merge_bias: float32 [1280], replicated, may hold values from -3 to 3
- w_merge: bfloat16 [5120, 4096], P('row', 'col'), may hold values from -0.078125 to 0.078125
Outputs:
- merged_out: bfloat16 [6144, 4096], P('row', 'col')
- req_norm: float32 [128], P('row')
- req_max: float32 [128], P('row')
Inputs may be any that keep to these rules, and one draw needn't show every extreme that they name: Each row of image_sizes sums to 256 and holds 48 at least once. A permutation of the slots. Request g * 8 + j goes to the row group slot_of // 8, which holds 8 slots. No row group sends more than one request to any row group.
All inputs are finite; a program needn't handle non-finite values.
Results may differ from a plain program's by a relative error of at most 0.018.
The roundings to bfloat16 on the way count: a program that leaves them out, or rounds other values in their place, can miss the bound.
Values may be sent and summed in bfloat16 or wider, within the bound.
A program may use at most 64 MiB of HBM per device.

v0:
```python
import jax
import jax.numpy as jnp
from jax import lax
from jax.sharding import PartitionSpec as P

D = 1280
HEAD_DIM = 80
OUT = 4096
IMG_ROW = 8


def layer_norm(values, gain, bias):
    center = jnp.mean(values, axis=-1, keepdims=True)
    shifted = values - center
    spread = jnp.mean(shifted * shifted, axis=-1, keepdims=True)
    return shifted * lax.rsqrt(spread + 1e-06) * gain + bias


def segment_ids(sizes_row, count):
    bounds = jnp.cumsum(sizes_row)
    merged_index = jnp.arange(count, dtype=jnp.int32) // 4
    return jnp.sum((merged_index[:, None] >= bounds[None, :]).astype(jnp.int32), axis=1)


def attend(qkv, segments):
    count = qkv.shape[0]
    width = min(512, count)
    query = qkv[:, :, 0]
    keys = qkv[:, :, 1]
    values = qkv[:, :, 2]
    results = []
    for offset in range(0, count, width):
        scores = jnp.einsum(
            "qhd,khd->hqk", query[offset : offset + width], keys, preferred_element_type=jnp.float32
        ) * HEAD_DIM ** (-0.5)
        same = segments[offset : offset + width, None] == segments[None, :]
        scores = jnp.where(same[None], scores, -1e30)
        peak = jnp.max(scores, axis=-1, keepdims=True)
        expo = jnp.exp(scores - peak)
        weights = (expo / jnp.sum(expo, axis=-1, keepdims=True)).astype(jnp.bfloat16)
        context = jnp.einsum("hqk,khd->qhd", weights, values, preferred_element_type=jnp.float32)
        results.append(context.astype(jnp.bfloat16).reshape(width, -1))
    return jnp.concatenate(results, axis=0)


def row_gather(block):
    n_row = lax.axis_size("row")
    send = jnp.broadcast_to(block[None], (n_row,) + block.shape)
    received = lax.all_to_all(send, "row", 0, 0, tiled=True)
    return received.reshape((n_row * block.shape[0],) + block.shape[1:])


def local(
    tokens,
    image_sizes,
    slot_of,
    ln_gain,
    ln_bias,
    w_qkv,
    w_out,
    w_up,
    w_down,
    merge_gain,
    merge_bias,
    w_merge,
):
    n_col = lax.axis_size("col")
    n_row = lax.axis_size("row")
    row_index = lax.axis_index("row")
    tok_dev = tokens.shape[0]
    tok_row = tok_dev * n_col
    merged_row = tok_row // 4
    most = merged_row * 3 // 16
    sizes_here = lax.dynamic_index_in_dim(image_sizes, row_index, 0, keepdims=False)
    segments = segment_ids(sizes_here, tok_row)

    qkv_cols = w_qkv.shape[2]
    first = row_gather(jnp.concatenate([w_qkv[0], w_out[0].T], axis=1))
    up_cols = w_up.shape[2]
    second = row_gather(jnp.concatenate([w_up[0], w_down[0].T], axis=1))
    merge_full = row_gather(w_merge)
    qkv_full = first[:, :qkv_cols]
    out_t = first[:, qkv_cols:]
    up_full = second[:, :up_cols]
    down_t = second[:, up_cols:]
    contract_t = (((1,), (1,)), ((), ()))

    stream = tokens
    normed = layer_norm(stream.astype(jnp.float32), ln_gain[0, 0], ln_bias[0, 0]).astype(
        jnp.bfloat16
    )
    normed_all = lax.all_gather(normed, "col", axis=0, tiled=True)
    qkv = jnp.dot(normed_all, qkv_full, preferred_element_type=jnp.float32)
    qkv = qkv.astype(jnp.bfloat16).reshape(tok_row, -1, 3, HEAD_DIM)
    context = attend(qkv, segments)
    attn_terms = lax.dot_general(
        context, out_t, contract_t, preferred_element_type=jnp.float32
    )
    attn_out = lax.psum_scatter(
        attn_terms.astype(jnp.bfloat16), "col", scatter_dimension=0, tiled=True
    ).astype(jnp.float32)
    stream = (stream.astype(jnp.float32) + attn_out).astype(jnp.bfloat16)
    normed = layer_norm(stream.astype(jnp.float32), ln_gain[0, 1], ln_bias[0, 1]).astype(
        jnp.bfloat16
    )
    normed_mlp = lax.all_gather(normed, "col", axis=0, tiled=True)
    up_value = jnp.dot(normed_mlp, up_full, preferred_element_type=jnp.float32)
    hidden = jax.nn.gelu(up_value, approximate=False).astype(jnp.bfloat16)
    mlp_terms = lax.dot_general(
        hidden, down_t, contract_t, preferred_element_type=jnp.float32
    )
    mlp_out = lax.psum_scatter(
        mlp_terms.astype(jnp.bfloat16), "col", scatter_dimension=0, tiled=True
    ).astype(jnp.float32)
    stream = (stream.astype(jnp.float32) + mlp_out).astype(jnp.bfloat16)
    merged = layer_norm(stream.astype(jnp.float32), merge_gain, merge_bias).astype(jnp.bfloat16)
    merged = merged.reshape(tok_dev // 4, 4 * D)
    merged_all = lax.all_gather(merged, "col", axis=0, tiled=True)
    out_dev = w_merge.shape[1]
    projected = jnp.dot(merged_all, merge_full, preferred_element_type=jnp.float32).astype(
        jnp.bfloat16
    )

    reqs = slot_of.shape[0]
    numbers = jnp.arange(reqs, dtype=jnp.int32)
    req_at_slot = jnp.sum(
        jnp.where(slot_of[None, :] == numbers[:, None], numbers[None, :], 0), axis=1
    )
    starts = jnp.cumsum(image_sizes, axis=1) - image_sizes
    sizes_flat = image_sizes.reshape(-1)
    inner = jnp.arange(most, dtype=jnp.int32)
    groups = jnp.arange(n_row, dtype=jnp.int32)
    my_dest = lax.dynamic_slice_in_dim(slot_of, row_index * IMG_ROW, IMG_ROW) // IMG_ROW
    my_starts = lax.dynamic_index_in_dim(starts, row_index, 0, keepdims=False)
    match = my_dest[None, :] == groups[:, None]
    start_to = jnp.sum(jnp.where(match, my_starts[None, :], 0), axis=1)
    padded = jnp.concatenate([projected, jnp.zeros((most, out_dev), projected.dtype)], axis=0)
    rows = jnp.clip(start_to[:, None] + inner[None, :], 0, padded.shape[0] - 1)
    send = jnp.take(padded, rows.reshape(-1), axis=0).reshape(n_row, most, out_dev)
    recv = lax.all_to_all(send, "row", 0, 0, tiled=True)

    request = lax.dynamic_slice_in_dim(req_at_slot, row_index * IMG_ROW, IMG_ROW)
    source = request // IMG_ROW
    taken = jnp.take(recv, source, axis=0)
    valid = inner[None, :] < sizes_flat[request][:, None]
    blocks = jnp.where(valid[:, :, None], taken, jnp.zeros_like(taken)).astype(jnp.float32)
    squares = jnp.sum(blocks * blocks, axis=(1, 2))
    peaks = jnp.max(jnp.abs(blocks), axis=(1, 2))
    stats = lax.all_gather(jnp.concatenate([squares, peaks]), "col", axis=0, tiled=False)
    squares = jnp.sum(stats[:, :IMG_ROW], axis=0)
    peaks = jnp.max(stats[:, IMG_ROW:], axis=0)
    slot_size = sizes_flat[request].astype(jnp.float32)
    req_norm = jnp.sqrt(squares / (slot_size * OUT) + 1e-06)
    merged_out = (
        (blocks / req_norm[:, None, None]).astype(jnp.bfloat16).reshape(IMG_ROW * most, out_dev)
    )
    return (merged_out, req_norm, peaks)


def solution(mesh):
    in_specs = (
        P(("row", "col"), None),
        P(),
        P(),
        P(),
        P(),
        P(None, "row", "col"),
        P(None, "col", "row"),
        P(None, "row", "col"),
        P(None, "col", "row"),
        P(),
        P(),
        P("row", "col"),
    )
    out_specs = (P("row", "col"), P("row"), P("row"))
    return jax.shard_map(local, mesh=mesh, in_specs=in_specs, out_specs=out_specs, check_vma=False)
```

profile of v0, /device:TPU:1, one launch (start us, length us, event | category | flops | bytes accessed | tf_op | source)
XLA Modules:
  0.0 304.0 jit_solution(12602921384670411688)
XLA Ops:
  7.2 1.1 convert_reduce_fusion.1
  8.3 1.2 fusion.74
  10.4 2.0 fusion.77
  13.3 1.0 pad_maximum_fusion.1
  14.2 1.3 broadcast_in_dim.155
  15.5 7.6 %all-to-all-start = ((bf16[16,80,640]{2,1,0:T(8,128)(2,1)}), bf16[16,80,640]{2,1,0:T(8,128)(2,1)S(1)}, u32[]{:S(2)}, u32[]{:S(2)}) async-start(bf16[16,80,640]{2,1,0:T(8,128)(2,1)} %broadcast_in_dim.155), calls=%async_computation | async-start | bytes 3276800 | tf_op jit(solution)/shard_map/all_to_all | solution.py:49
  24.4 22.7 %all-to-all-done = bf16[16,80,640]{2,1,0:T(8,128)(2,1)S(1)} async-done(((bf16[16,80,640]{2,1,0:T(8,128)(2,1)}), bf16[16,80,640]{2,1,0:T(8,128)(2,1)S(1)}, u32[]{:S(2)}, u32[]{:S(2)}) %all-to-all-start) | async-done | bytes 1638432 | tf_op jit(solution)/shard_map/all_to_all | solution.py:49
  47.1 4.3 %convolution_convert_fusion.2 = bf16[1024,480]{0,1:T(8,128)(2,1)} fusion(bf16[1024,1280]{1,0:T(8,128)(2,1)} %all-gather.5.cloned.1.call-done, bf16[1280,640]{1,0:T(8,128)(2,1)S(1)} %bitcast.87), kind=kOutput, calls=%fused_computation.45 | convolution fusion | flops 1258782720 | bytes 4915200 | tf_op jit(solution)/shard_map/dot_general | solution.py:93
  51.3 4.7 %fusion.137 = (f32[2,512]{1,0:T(2,128)S(1)}, f32[2,512,1024]{2,1,0:T(8,128)}) fusion(pred[512,1024]{1,0:T(8,128)(4,1)S(1)} %get-tuple-element.15, bf16[1024,2,3,80]{0,3,2,1:T(8,128)(2,1)} %bitcast.98), kind=kOutput, calls=%fused_computation.219 | convolution fusion | flops 171967488 | bytes 5214208 | tf_op jit(solution)/shard_map/sub | solution.py:39
  56.1 4.7 %fusion.136 = (f32[2,512]{1,0:T(2,128)S(1)}, f32[2,512,1024]{2,1,0:T(8,128)}) fusion(pred[512,1024]{1,0:T(8,128)(4,1)S(1)} %get-tuple-element.16, bf16[1024,2,3,80]{0,3,2,1:T(8,128)(2,1)} %bitcast.99), kind=kOutput, calls=%fused_computation.218 | convolution fusion | flops 171967488 | bytes 5214208 | tf_op jit(solution)/shard_map/sub | solution.py:39
  60.8 3.3 %fusion.61 = bf16[2,80,512]{2,1,0:T(8,128)(2,1)S(1)} fusion(f32[2,512,1024]{2,1,0:T(8,128)} %get-tuple-element.22, f32[2,512]{1,0:T(2,128)S(1)} %get-tuple-element.21, bf16[1024,2,3,80]{0,3,2,1:T(8,128)(2,1)} %bitcast.100), kind=kOutput, calls=%fused_computation.79 | convolution fusion | flops 169951232 | bytes 4689920 | tf_op jit(solution)/shard_map/hqk,khd->qhd/dot_general | solution.py:41
  64.3 1.8 fusion.60
  66.1 2.7 convolution_convert_fusion.1
  68.9 32.1 %reduce-scatter.3.cloned.1.call-done = bf16[128,1280]{1,0:T(8,128)(2,1)} async-done(((bf16[1024,1280]{1,0:T(8,128)(2,1)}), bf16[128,1280]{1,0:T(8,128)(2,1)}) %reduce-scatter.3.cloned.1.call-update) | async-done | bytes 327696 | tf_op jit(solution)/shard_map/reduce_scatter | solution.py:99
  101.0 1.1 convert_reduce_fusion
  102.4 1.0 fusion.73
  103.7 43.5 %all_to_all.20 = bf16[16,80,1280]{2,1,0:T(8,128)(2,1)} all-to-all(bf16[16,80,1280]{2,1,0:T(8,128)(2,1)S(1)} %broadcast_in_dim.159), channel_id=1, replica_groups=mesh['row'=16,'col'=8] {'row'}, dimensions={0} | all-to-all | bytes 6553600 | tf_op jit(solution)/shard_map/all_to_all | solution.py:49
  147.2 13.0 %convolution_convert_fusion = bf16[1024,1280]{1,0:T(8,128)(2,1)} fusion(bf16[1280,1280]{1,0:T(8,128)(2,1)} %bitcast.86, bf16[1024,1280]{1,0:T(8,128)(2,1)} %all-gather.7.cloned.1.call-done), kind=kOutput, calls=%fused_computation.12 | convolution fusion | flops 3399352320 | bytes 8519680 | tf_op jit(solution)/shard_map/dot_general | solution.py:109
  161.2 2.9 broadcast_in_dim.160
  164.1 4.7 %all-to-all-start.2 = ((bf16[16,320,512]{2,1,0:T(8,128)(2,1)}), bf16[16,320,512]{2,1,0:T(8,128)(2,1)}, u32[]{:S(2)}, u32[]{:S(2)}) async-start(bf16[16,320,512]{2,1,0:T(8,128)(2,1)} %broadcast_in_dim.160), calls=%async_computation.4 | async-start | bytes 10485760 | tf_op jit(solution)/shard_map/all_to_all | solution.py:49
  168.9 29.2 %reduce-scatter.5.cloned.1.call-done = bf16[128,1280]{1,0:T(8,128)(2,1)} async-done(((bf16[1024,1280]{1,0:T(8,128)(2,1)}), bf16[128,1280]{1,0:T(8,128)(2,1)}) %reduce-scatter.5.cloned.1.call-update) | async-done | bytes 327696 | tf_op jit(solution)/shard_map/reduce_scatter | solution.py:112
  198.0 1.1 convert_reduce_fusion.2
  199.2 1.2 fusion.78
  200.4 1.2 fusion.81
  203.1 30.9 %all-to-all-done.2 = bf16[16,320,512]{2,1,0:T(8,128)(2,1)} async-done(((bf16[16,320,512]{2,1,0:T(8,128)(2,1)}), bf16[16,320,512]{2,1,0:T(8,128)(2,1)}, u32[]{:S(2)}, u32[]{:S(2)}) %all-to-all-start.2) | async-done | bytes 5242912 | tf_op jit(solution)/shard_map/all_to_all | solution.py:49
  234.0 4.8 %convolution_convert_fusion.3 = bf16[256,512]{1,0:T(8,128)(2,1)S(1)} fusion(bf16[256,5120]{1,0:T(8,128)(2,1)} %all-gather.9.cloned.1.call-done, bf16[5120,512]{1,0:T(8,128)(2,1)} %bitcast.18), kind=kOutput, calls=%fused_computation.77 | convolution fusion | flops 1342308352 | bytes 8126464 | tf_op jit(solution)/shard_map/dot_general | solution.py:120
  238.8 2.7 gather_fusion.1
  241.5 1.1 broadcast_select_fusion
  242.6 8.0 %all-to-all-start.3 = ((bf16[16,48,512]{2,1,0:T(8,128)(2,1)}), bf16[16,48,512]{2,1,0:T(8,128)(2,1)S(1)}, u32[]{:S(2)}, u32[]{:S(2)}) async-start(bf16[16,48,512]{2,1,0:T(8,128)(2,1)} %broadcast_select_fusion), calls=%async_computation.5 | async-start | bytes 1572864 | tf_op jit(solution)/shard_map/all_to_all | solution.py:140
  253.1 9.3 %all-to-all-done.3 = bf16[16,48,512]{2,1,0:T(8,128)(2,1)S(1)} async-done(((bf16[16,48,512]{2,1,0:T(8,128)(2,1)}), bf16[16,48,512]{2,1,0:T(8,128)(2,1)S(1)}, u32[]{:S(2)}, u32[]{:S(2)}) %all-to-all-start.3) | async-done | bytes 786464 | tf_op jit(solution)/shard_map/all_to_all | solution.py:140
  263.5 32.1 %all-reduce.1 = f32[128]{0:T(128)S(1)} all-reduce(f32[128]{0:T(128)S(1)} %maximum_dynamic-update-slice_fusion), channel_id=2, replica_groups=mesh['row'=16,'col'=8] {'col'}, use_global_device_ids=true, to_apply=%add.1 | all-reduce | flops 128 | bytes 1024
  296.5 1.0 divide_convert_fusion.8
  (84 shorter events, 10.2 us)
Async XLA Ops:
  7.2 39.9 %all-gather.5.cloned.1.call-start = ((), (), s32[]{:S(2)}) async-start(), calls=%async_computation.6 | async-start | bytes 2949120 | tf_op jit(solution)/shard_map/all_gather | solution.py:92
  13.2 9.9 %copy-start.4 = (s32[16,8]{0,1:T(8,128)S(1)}, s32[16,8]{0,1:T(8,128)}, u32[]{:S(2)}) copy-start(s32[16,8]{0,1:T(8,128)} %param.13) | copy-start | bytes 1540
  15.5 31.6 %all-to-all-start = ((bf16[16,80,640]{2,1,0:T(8,128)(2,1)}), bf16[16,80,640]{2,1,0:T(8,128)(2,1)S(1)}, u32[]{:S(2)}, u32[]{:S(2)}) async-start(bf16[16,80,640]{2,1,0:T(8,128)(2,1)} %broadcast_in_dim.155), calls=%async_computation | async-start | bytes 3276800 | tf_op jit(solution)/shard_map/all_to_all | solution.py:49
  23.1 77.8 %reduce-scatter.3.cloned.1.call-start = ((), (), s32[]{:S(2)}) async-start(), calls=%async_computation.7 | async-start | bytes 2949120 | tf_op jit(solution)/shard_map/reduce_scatter | solution.py:99
  60.8 3.5 %copy-start.10 = (f32[2,512,1024]{2,1,0:T(8,128)S(1)}, f32[2,512,1024]{2,1,0:T(8,128)}, u32[]{:S(2)}) copy-start(f32[2,512,1024]{2,1,0:T(8,128)} %get-tuple-element.20) | copy-start | bytes 12582916
  66.1 34.8 %copy-start = (bf16[128,1280]{1,0:T(8,128)(2,1)S(1)}, bf16[128,1280]{1,0:T(8,128)(2,1)}, u32[]{:S(2)}) copy-start(bf16[128,1280]{1,0:T(8,128)(2,1)} %param.12) | copy-start | bytes 983044
  68.8 34.6 %copy-start.2 = (bf16[1,640,80]{1,2,0:T(8,128)(2,1)S(1)}, bf16[1,640,80]{1,2,0:T(8,128)(2,1)}, u32[]{:S(2)}) copy-start(bf16[1,640,80]{1,2,0:T(8,128)(2,1)} %param.20) | copy-start | bytes 307204
  68.8 34.6 %copy-start.3 = (bf16[1,80,640]{2,1,0:T(8,128)(2,1)S(1)}, bf16[1,80,640]{2,1,0:T(8,128)(2,1)}, u32[]{:S(2)}) copy-start(bf16[1,80,640]{2,1,0:T(8,128)(2,1)} %param.19) | copy-start | bytes 307204
  68.8 78.4 %all-gather.7.cloned.1.call-start = ((), (), s32[]{:S(2)}) async-start(), calls=%async_computation.8 | async-start | bytes 2949120 | tf_op jit(solution)/shard_map/all_gather | solution.py:106
  103.4 94.7 %reduce-scatter.5.cloned.1.call-start = ((), (), s32[]{:S(2)}) async-start(), calls=%async_computation.9 | async-start | bytes 2949120 | tf_op jit(solution)/shard_map/reduce_scatter | solution.py:112
  160.3 1.0 copy-start.1
  164.1 36.3 %copy-start.5 = (f32[1280]{0:T(1024)S(1)}, f32[1280]{0:T(1024)}, u32[]{:S(2)}) copy-start(f32[1280]{0:T(1024)} %param.22) | copy-start | bytes 15364
  164.1 36.3 %copy-start.6 = (f32[1280]{0:T(1024)S(1)}, f32[1280]{0:T(1024)}, u32[]{:S(2)}) copy-start(f32[1280]{0:T(1024)} %param.21) | copy-start | bytes 15364
  164.1 69.9 %all-to-all-start.2 = ((bf16[16,320,512]{2,1,0:T(8,128)(2,1)}), bf16[16,320,512]{2,1,0:T(8,128)(2,1)}, u32[]{:S(2)}, u32[]{:S(2)}) async-start(bf16[16,320,512]{2,1,0:T(8,128)(2,1)} %broadcast_in_dim.160), calls=%async_computation.4 | async-start | bytes 10485760 | tf_op jit(solution)/shard_map/all_to_all | solution.py:49
  168.8 33.7 %copy-start.7 = (s32[128]{0:T(128)S(1)}, s32[128]{0:T(128)}, u32[]{:S(2)}) copy-start(s32[128]{0:T(128)} %param.14) | copy-start | bytes 1540
  168.8 65.2 %all-gather.9.cloned.1.call-start = ((), (), s32[]{:S(2)}) async-start(), calls=%async_computation.10 | async-start | bytes 2949120 | tf_op jit(solution)/shard_map/all_gather | solution.py:118
  241.5 10.3 %copy-start.9 = (u32[128]{0:T(128)S(1)}, u32[128]{0:T(128)}, u32[]{:S(2)}) copy-start(u32[128]{0:T(128)} %constant.178) | copy-start | bytes 1540
  242.6 19.8 %all-to-all-start.3 = ((bf16[16,48,512]{2,1,0:T(8,128)(2,1)}), bf16[16,48,512]{2,1,0:T(8,128)(2,1)S(1)}, u32[]{:S(2)}, u32[]{:S(2)}) async-start(bf16[16,48,512]{2,1,0:T(8,128)(2,1)} %broadcast_select_fusion), calls=%async_computation.5 | async-start | bytes 1572864 | tf_op jit(solution)/shard_map/all_to_all | solution.py:140
  296.3 1.1 copy-start.8
Sparse Core Ops, SparseCore 0:
  12.5 29.6 all-gather.4
  68.9 31.9 reduce-scatter.2
  103.5 28.2 all-gather.6
  160.4 37.5 reduce-scatter.4
  202.6 28.5 all-gather.8
where the time goes:
time: 305 us; the launch traced here: 304 us
  waiting for transfers between devices  124 us (41%)
  blocking collectives  75.7 us (25%)
  matrix products  39.2 us (13%)
  starting transfers between devices  20.5 us (7%)
  other arithmetic  16 us (5%)
  between operations  14.7 us (5%)
  local copies, waits for them, and re-layouts  13.7 us (4%)
    all_to_all x2, waiting for transfers between devices, row_gather(): received = lax.all_to_all(send, 'row', 0, 0, tiled=True)  53.6 us
    all_to_all x1, blocking collectives, row_gather(): received = lax.all_to_all(send, 'row', 0, 0, tiled=True)  43.5 us
    unnamed x1, blocking collectives  32.1 us
    reduce_scatter x1, waiting for transfers between devices, local(): lax.psum_scatter(attn_terms.astype(jnp.bfloat16), 'col', scatter_dimensio...  32.1 us
    reduce_scatter x1, waiting for transfers between devices, local(): lax.psum_scatter(mlp_terms.astype(jnp.bfloat16), 'col', scatter_dimension...  29.2 us
    dot_general x1, matrix products, local(): lax.dot_general(hidden, down_t, contract_t, preferred_element_type=jnp.fl...  13 us
    all_to_all x2, starting transfers between devices, row_gather(): received = lax.all_to_all(send, 'row', 0, 0, tiled=True)  12.3 us
    sub x2, matrix products, attend(): expo = jnp.exp(scores - peak)  9.41 us
  transfers between devices with their start and end apart: 8, of which 5 were waited for; matrix products, arithmetic and copies ran while one was open for 5% of the time, Pallas kernels for 0%

commit v1 on v0

--- a/solution.py
+++ b/solution.py
@@ -77,12 +77,14 @@
     qkv_cols = w_qkv.shape[2]
     first = row_gather(jnp.concatenate([w_qkv[0], w_out[0].T], axis=1))
     up_cols = w_up.shape[2]
-    second = row_gather(jnp.concatenate([w_up[0], w_down[0].T], axis=1))
-    merge_full = row_gather(w_merge)
+    down_cols = w_down.shape[1]
+    rest = w_merge.reshape(w_up.shape[1], -1)
+    second = row_gather(jnp.concatenate([w_up[0], w_down[0].T, rest], axis=1))
     qkv_full = first[:, :qkv_cols]
     out_t = first[:, qkv_cols:]
     up_full = second[:, :up_cols]
-    down_t = second[:, up_cols:]
+    down_t = second[:, up_cols : up_cols + down_cols]
+    merge_full = second[:, up_cols + down_cols :].reshape(-1, w_merge.shape[1])
     contract_t = (((1,), (1,)), ((), ()))
 
     stream = tokens
@@ -139,16 +141,26 @@
     send = jnp.take(padded, rows.reshape(-1), axis=0).reshape(n_row, most, out_dev)
     recv = lax.all_to_all(send, "row", 0, 0, tiled=True)
 
+    owner = segment_ids(sizes_here, merged_row * 4)[::4]
+    own = owner[:, None] == jnp.arange(IMG_ROW, dtype=jnp.int32)[None, :]
+    proj32 = projected.astype(jnp.float32)
+    row_sq = jnp.sum(proj32 * proj32, axis=1)
+    row_peak = jnp.max(jnp.abs(proj32), axis=1)
+    part_sq = jnp.sum(jnp.where(own, row_sq[:, None], 0.0), axis=0)
+    part_peak = jnp.max(jnp.where(own, row_peak[:, None], 0.0), axis=0)
+    stats = lax.all_gather(
+        jnp.concatenate([part_sq, part_peak]), ("row", "col"), axis=0, tiled=False
+    ).reshape(n_row, n_col, 2, IMG_ROW)
+    req_sq = jnp.sum(stats[:, :, 0], axis=1).reshape(-1)
+    req_peak = jnp.max(stats[:, :, 1], axis=1).reshape(-1)
+
     request = lax.dynamic_slice_in_dim(req_at_slot, row_index * IMG_ROW, IMG_ROW)
     source = request // IMG_ROW
     taken = jnp.take(recv, source, axis=0)
     valid = inner[None, :] < sizes_flat[request][:, None]
     blocks = jnp.where(valid[:, :, None], taken, jnp.zeros_like(taken)).astype(jnp.float32)
-    squares = jnp.sum(blocks * blocks, axis=(1, 2))
-    peaks = jnp.max(jnp.abs(blocks), axis=(1, 2))
-    stats = lax.all_gather(jnp.concatenate([squares, peaks]), "col", axis=0, tiled=False)
-    squares = jnp.sum(stats[:, :IMG_ROW], axis=0)
-    peaks = jnp.max(stats[:, IMG_ROW:], axis=0)
+    squares = req_sq[request]
+    peaks = req_peak[request]
     slot_size = sizes_flat[request].astype(jnp.float32)
     req_norm = jnp.sqrt(squares / (slot_size * OUT) + 1e-06)
     merged_out = (

time: 305 us -> 377 us (1.24)
  waiting for transfers between devices: 124 us -> 190 us
  local copies, waits for them, and re-layouts: 13.7 us -> 30.4 us
  blocking collectives: 75.7 us -> 67.6 us
    all_to_all x2, waiting for transfers between devices: 53.6 us -> 119 us  [row_gather(): received = lax.all_to_all(send, 'row', 0, 0, tiled=True)]
    all_to_all x1 -> x0, blocking collectives: 43.5 us -> none  [row_gather(): received = lax.all_to_all(send, 'row', 0, 0, tiled=True)]
    unnamed x1, blocking collectives: 32.1 us -> 67.6 us
    all_gather x1, waiting for transfers between devices: 0.01 us -> 11.9 us  [local(): merged_all = lax.all_gather(merged, 'col', axis=0, tiled=True)]
    reshape x0 -> x5, local copies, waits for them, and re-layouts: none -> 9.82 us  [the longest x1 9.22 us: local(): merge_full = second[:, up_cols + down_cols:].reshape(-1, w_merge.shape[1])]
    all_to_all x1, waiting for transfers between devices: 9.3 us -> 0.01 us  [local(): recv = lax.all_to_all(send, 'row', 0, 0, tiled=True)]
    reduce_scatter x1, waiting for transfers between devices: 32.1 us -> 23.8 us  [local(): lax.psum_scatter(attn_terms.astype(jnp.bfloat16), 'col', scatter_dimensio...]
    slice x0 -> x2, local copies, waits for them, and re-layouts: none -> 5.94 us  [the longest x1 5.72 us: local(): merge_full = second[:, up_cols + down_cols:].reshape(-1, w_merge.shape[1])]
  transfers between devices with their start and end apart: 8 -> 8, of which waited for: 5 -> 5; matrix products, arithmetic and copies ran while one was open for 5% -> 8% of each run, Pallas kernels for 0% -> 0%
where the time goes in v1:
time: 377 us; the launch traced here: 376 us
  waiting for transfers between devices  190 us (50%)
  blocking collectives  67.6 us (18%)
  matrix products  39.3 us (10%)
  local copies, waits for them, and re-layouts  30.4 us (8%)
  starting transfers between devices  19.4 us (5%)
  other arithmetic  15.3 us (4%)
  between operations  14.1 us (4%)
    all_to_all x2, waiting for transfers between devices, row_gather(): received = lax.all_to_all(send, 'row', 0, 0, tiled=True)  119 us
    unnamed x1, blocking collectives  67.6 us
    reduce_scatter x1, waiting for transfers between devices, local(): lax.psum_scatter(mlp_terms.astype(jnp.bfloat16), 'col', scatter_dimension...  34.9 us
    reduce_scatter x1, waiting for transfers between devices, local(): lax.psum_scatter(attn_terms.astype(jnp.bfloat16), 'col', scatter_dimensio...  23.8 us
    dot_general x1, matrix products, local(): lax.dot_general(hidden, down_t, contract_t, preferred_element_type=jnp.fl...  13 us
    all_to_all x2, starting transfers between devices, row_gather(): received = lax.all_to_all(send, 'row', 0, 0, tiled=True)  12.4 us
    all_gather x1, waiting for transfers between devices, local(): merged_all = lax.all_gather(merged, 'col', axis=0, tiled=True)  11.9 us
    sub x2, matrix products, attend(): expo = jnp.exp(scores - peak)  9.41 us
  transfers between devices with their start and end apart: 8, of which 5 were waited for; matrix products, arithmetic and copies ran while one was open for 8% of the time, Pallas kernels for 0%

profile of v1, /device:TPU:1, one launch (start us, length us, event | category | flops | bytes accessed | tf_op | source)
XLA Modules:
  0.0 375.7 jit_solution(475856465096609004)
XLA Ops:
  7.2 1.1 convert_reduce_fusion.1
  8.3 1.2 fusion.72
  10.4 2.0 fusion.75
  14.2 1.3 broadcast_in_dim.167
  15.5 7.6 %all-to-all-start = ((bf16[16,80,640]{2,1,0:T(8,128)(2,1)}), bf16[16,80,640]{2,1,0:T(8,128)(2,1)S(1)}, u32[]{:S(2)}, u32[]{:S(2)}) async-start(bf16[16,80,640]{2,1,0:T(8,128)(2,1)} %broadcast_in_dim.167), calls=%async_computation | async-start | bytes 3276800 | tf_op jit(solution)/shard_map/all_to_all | solution.py:49
  24.4 22.7 %all-to-all-done = bf16[16,80,640]{2,1,0:T(8,128)(2,1)S(1)} async-done(((bf16[16,80,640]{2,1,0:T(8,128)(2,1)}), bf16[16,80,640]{2,1,0:T(8,128)(2,1)S(1)}, u32[]{:S(2)}, u32[]{:S(2)}) %all-to-all-start) | async-done | bytes 1638432 | tf_op jit(solution)/shard_map/all_to_all | solution.py:49
  47.1 4.3 %convolution_convert_fusion.2 = bf16[1024,480]{0,1:T(8,128)(2,1)} fusion(bf16[1024,1280]{1,0:T(8,128)(2,1)} %all-gather.5.cloned.1.call-done, bf16[1280,640]{1,0:T(8,128)(2,1)S(1)} %bitcast.84), kind=kOutput, calls=%fused_computation.47 | convolution fusion | flops 1258782720 | bytes 4915200 | tf_op jit(solution)/shard_map/dot_general | solution.py:95
  51.3 4.7 %fusion.136 = (f32[2,512]{1,0:T(2,128)S(1)}, f32[2,512,1024]{2,1,0:T(8,128)}) fusion(pred[512,1024]{1,0:T(8,128)(4,1)S(1)} %get-tuple-element.18, bf16[1024,2,3,80]{0,3,2,1:T(8,128)(2,1)} %bitcast.95), kind=kOutput, calls=%fused_computation.222 | convolution fusion | flops 171967488 | bytes 5214208 | tf_op jit(solution)/shard_map/sub | solution.py:39
  56.0 4.7 %fusion.137 = (f32[2,512]{1,0:T(2,128)S(1)}, f32[2,512,1024]{2,1,0:T(8,128)}) fusion(pred[512,1024]{1,0:T(8,128)(4,1)S(1)} %get-tuple-element.17, bf16[1024,2,3,80]{0,3,2,1:T(8,128)(2,1)} %bitcast.96), kind=kOutput, calls=%fused_computation.223 | convolution fusion | flops 171967488 | bytes 5214208 | tf_op jit(solution)/shard_map/sub | solution.py:39
  60.8 3.3 fusion.60
  64.3 1.8 fusion.61
  66.2 2.7 convolution_convert_fusion.1
  69.1 3.8 %broadcast_in_dim.171 = bf16[16,80,3328]{2,1,0:T(8,128)(2,1)} broadcast(bf16[80,3328]{1,0:T(8,128)(2,1)S(1)} %pad_maximum_fusion), dimensions={1,2} | broadcast | bytes 9052160 | tf_op jit(solution)/shard_map/broadcast_in_dim | solution.py:48
  73.0 4.9 %all-to-all-start.1 = ((bf16[16,80,3328]{2,1,0:T(8,128)(2,1)}), bf16[16,80,3328]{2,1,0:T(8,128)(2,1)}, u32[]{:S(2)}, u32[]{:S(2)}) async-start(bf16[16,80,3328]{2,1,0:T(8,128)(2,1)} %broadcast_in_dim.171), calls=%async_computation.2 | async-start | bytes 17039360 | tf_op jit(solution)/shard_map/all_to_all | solution.py:49
  77.9 23.8 %reduce-scatter.3.cloned.1.call-done = bf16[128,1280]{1,0:T(8,128)(2,1)} async-done(((bf16[1024,1280]{1,0:T(8,128)(2,1)}), bf16[128,1280]{1,0:T(8,128)(2,1)}) %reduce-scatter.3.cloned.1.call-update) | async-done | bytes 327696 | tf_op jit(solution)/shard_map/reduce_scatter | solution.py:101
  101.7 1.1 convert_reduce_fusion
  103.1 1.0 fusion.71
  104.3 96.2 %all-to-all-done.1 = bf16[16,80,3328]{2,1,0:T(8,128)(2,1)} async-done(((bf16[16,80,3328]{2,1,0:T(8,128)(2,1)}), bf16[16,80,3328]{2,1,0:T(8,128)(2,1)}, u32[]{:S(2)}, u32[]{:S(2)}) %all-to-all-start.1) | async-done | bytes 8519712 | tf_op jit(solution)/shard_map/all_to_all | solution.py:49
  200.5 13.0 %convolution_convert_fusion = bf16[1024,1280]{1,0:T(8,128)(2,1)} fusion(bf16[1280,3328]{1,0:T(8,128)(2,1)} %bitcast.17, bf16[1024,1280]{1,0:T(8,128)(2,1)} %all-gather.7.cloned.1.call-done), kind=kOutput, calls=%fused_computation.14 | convolution fusion | flops 3399352320 | bytes 8519680 | tf_op jit(solution)/shard_map/dot_general | solution.py:111
  213.6 34.9 %reduce-scatter.5.cloned.1.call-done = bf16[128,1280]{1,0:T(8,128)(2,1)} async-done(((bf16[1024,1280]{1,0:T(8,128)(2,1)}), bf16[128,1280]{1,0:T(8,128)(2,1)}) %reduce-scatter.5.cloned.1.call-update) | async-done | bytes 327696 | tf_op jit(solution)/shard_map/reduce_scatter | solution.py:114
  248.5 1.1 convert_reduce_fusion.2
  249.6 1.2 fusion.76
  250.9 1.2 fusion.79
  254.4 5.7 %slice.101 = bf16[1280,2048]{1,0:T(8,128)(2,1)} slice(bf16[1280,3328]{1,0:T(8,128)(2,1)} %bitcast.17), slice={[0:1280], [1280:3328]} | slice | bytes 10485760 | tf_op jit(solution)/shard_map/slice | solution.py:87
  260.2 9.2 %reshape.286 = bf16[5120,512]{1,0:T(8,128)(2,1)} reshape(bf16[1280,2048]{1,0:T(8,128)(2,1)} %slice.101) | data formatting | bytes 10485760 | tf_op jit(solution)/shard_map/reshape | solution.py:87
  269.4 11.9 %all-gather.9.cloned.1.call-done = bf16[256,5120]{1,0:T(8,128)(2,1)} async-done(((bf16[32,5120]{1,0:T(8,128)(2,1)}), bf16[256,5120]{1,0:T(8,128)(2,1)}) %all-gather.9.cloned.1.call-update) | async-done | bytes 2621456 | tf_op jit(solution)/shard_map/all_gather | solution.py:120
  281.3 4.9 %fusion.83 = (f32[256]{0:T(256)S(1)}, f32[256]{0:T(256)S(1)}, bf16[256,512]{1,0:T(8,128)(2,1)S(1)}) fusion(bf16[256,5120]{1,0:T(8,128)(2,1)} %all-gather.9.cloned.1.call-done, bf16[5120,512]{1,0:T(8,128)(2,1)} %reshape.286), kind=kOutput, calls=%fused_computation.118 | convolution fusion | flops 1342963200 | bytes 8128512 | tf_op jit(solution)/shard_map/dot_general | solution.py:122
  286.3 2.7 gather_fusion.1
  289.0 1.1 broadcast_select_fusion
  290.0 6.5 %all-to-all-start.2 = ((bf16[16,48,512]{2,1,0:T(8,128)(2,1)}), bf16[16,48,512]{2,1,0:T(8,128)(2,1)S(1)}, u32[]{:S(2)}, u32[]{:S(2)}) async-start(bf16[16,48,512]{2,1,0:T(8,128)(2,1)} %broadcast_select_fusion), calls=%async_computation.4 | async-start | bytes 1572864 | tf_op jit(solution)/shard_map/all_to_all | solution.py:142
  297.5 67.6 %all-reduce.1 = f32[2048]{0:T(1024)S(1)} all-reduce(f32[2048]{0:T(1024)S(1)} %maximum_dynamic-update-slice_fusion), channel_id=2, replica_groups=mesh['row'=16,'col'=8] {'row','col'}, use_global_device_ids=true, to_apply=%add.1 | all-reduce | flops 2048 | bytes 16384
  366.5 1.2 gather_fusion.4
  (87 shorter events, 11.4 us)
Async XLA Ops:
  7.2 39.9 %all-gather.5.cloned.1.call-start = ((), (), s32[]{:S(2)}) async-start(), calls=%async_computation.5 | async-start | bytes 2949120 | tf_op jit(solution)/shard_map/all_gather | solution.py:94
  13.2 9.9 %copy-start.4 = (s32[16,8]{0,1:T(8,128)S(1)}, s32[16,8]{0,1:T(8,128)}, u32[]{:S(2)}) copy-start(s32[16,8]{0,1:T(8,128)} %param.13) | copy-start | bytes 1540
  15.5 31.6 %all-to-all-start = ((bf16[16,80,640]{2,1,0:T(8,128)(2,1)}), bf16[16,80,640]{2,1,0:T(8,128)(2,1)S(1)}, u32[]{:S(2)}, u32[]{:S(2)}) async-start(bf16[16,80,640]{2,1,0:T(8,128)(2,1)} %broadcast_in_dim.167), calls=%async_computation | async-start | bytes 3276800 | tf_op jit(solution)/shard_map/all_to_all | solution.py:49
  23.1 78.6 %reduce-scatter.3.cloned.1.call-start = ((), (), s32[]{:S(2)}) async-start(), calls=%async_computation.6 | async-start | bytes 2949120 | tf_op jit(solution)/shard_map/reduce_scatter | solution.py:101
  60.8 3.5 copy-start.9
  66.1 2.7 copy-start.1
  66.1 2.9 copy-start.2
  66.1 2.9 copy-start.3
  73.0 28.7 %copy-start = (bf16[128,1280]{1,0:T(8,128)(2,1)S(1)}, bf16[128,1280]{1,0:T(8,128)(2,1)}, u32[]{:S(2)}) copy-start(bf16[128,1280]{1,0:T(8,128)(2,1)} %param.12) | copy-start | bytes 983044
  73.0 127.6 %all-to-all-start.1 = ((bf16[16,80,3328]{2,1,0:T(8,128)(2,1)}), bf16[16,80,3328]{2,1,0:T(8,128)(2,1)}, u32[]{:S(2)}, u32[]{:S(2)}) async-start(bf16[16,80,3328]{2,1,0:T(8,128)(2,1)} %broadcast_in_dim.171), calls=%async_computation.2 | async-start | bytes 17039360 | tf_op jit(solution)/shard_map/all_to_all | solution.py:49
  77.8 122.7 %all-gather.7.cloned.1.call-start = ((), (), s32[]{:S(2)}) async-start(), calls=%async_computation.7 | async-start | bytes 2949120 | tf_op jit(solution)/shard_map/all_gather | solution.py:108
  104.1 144.4 %reduce-scatter.5.cloned.1.call-start = ((), (), s32[]{:S(2)}) async-start(), calls=%async_computation.8 | async-start | bytes 2949120 | tf_op jit(solution)/shard_map/reduce_scatter | solution.py:114
  213.5 37.3 %copy-start.5 = (f32[1280]{0:T(1024)S(1)}, f32[1280]{0:T(1024)}, u32[]{:S(2)}) copy-start(f32[1280]{0:T(1024)} %param.22) | copy-start | bytes 15364
  213.5 37.3 %copy-start.6 = (f32[1280]{0:T(1024)S(1)}, f32[1280]{0:T(1024)}, u32[]{:S(2)}) copy-start(f32[1280]{0:T(1024)} %param.21) | copy-start | bytes 15364
  213.5 39.5 %copy-start.7 = (s32[128]{0:T(128)S(1)}, s32[128]{0:T(128)}, u32[]{:S(2)}) copy-start(s32[128]{0:T(128)} %param.14) | copy-start | bytes 1540
  213.6 67.8 %all-gather.9.cloned.1.call-start = ((), (), s32[]{:S(2)}) async-start(), calls=%async_computation.9 | async-start | bytes 2949120 | tf_op jit(solution)/shard_map/all_gather | solution.py:120
  290.0 77.6 %all-to-all-start.2 = ((bf16[16,48,512]{2,1,0:T(8,128)(2,1)}), bf16[16,48,512]{2,1,0:T(8,128)(2,1)S(1)}, u32[]{:S(2)}, u32[]{:S(2)}) async-start(bf16[16,48,512]{2,1,0:T(8,128)(2,1)} %broadcast_select_fusion), calls=%async_computation.4 | async-start | bytes 1572864 | tf_op jit(solution)/shard_map/all_to_all | solution.py:142
  366.2 3.0 copy-start.8
Sparse Core Ops, SparseCore 0:
  12.5 29.6 all-gather.4
  69.0 32.6 reduce-scatter.2
  104.2 28.4 all-gather.6
  213.7 34.7 reduce-scatter.4
  253.1 28.1 all-gather.8

commit v2 on v0

--- a/solution.py
+++ b/solution.py
@@ -85,37 +85,30 @@
     down_t = second[:, up_cols:]
     contract_t = (((1,), (1,)), ((), ()))
 
-    stream = tokens
-    normed = layer_norm(stream.astype(jnp.float32), ln_gain[0, 0], ln_bias[0, 0]).astype(
+    stream = lax.all_gather(tokens, "col", axis=0, tiled=True)
+    normed_all = layer_norm(stream.astype(jnp.float32), ln_gain[0, 0], ln_bias[0, 0]).astype(
         jnp.bfloat16
     )
-    normed_all = lax.all_gather(normed, "col", axis=0, tiled=True)
     qkv = jnp.dot(normed_all, qkv_full, preferred_element_type=jnp.float32)
     qkv = qkv.astype(jnp.bfloat16).reshape(tok_row, -1, 3, HEAD_DIM)
     context = attend(qkv, segments)
     attn_terms = lax.dot_general(
         context, out_t, contract_t, preferred_element_type=jnp.float32
     )
-    attn_out = lax.psum_scatter(
-        attn_terms.astype(jnp.bfloat16), "col", scatter_dimension=0, tiled=True
-    ).astype(jnp.float32)
+    attn_out = lax.psum(attn_terms.astype(jnp.bfloat16), "col").astype(jnp.float32)
     stream = (stream.astype(jnp.float32) + attn_out).astype(jnp.bfloat16)
-    normed = layer_norm(stream.astype(jnp.float32), ln_gain[0, 1], ln_bias[0, 1]).astype(
+    normed_mlp = layer_norm(stream.astype(jnp.float32), ln_gain[0, 1], ln_bias[0, 1]).astype(
         jnp.bfloat16
     )
-    normed_mlp = lax.all_gather(normed, "col", axis=0, tiled=True)
     up_value = jnp.dot(normed_mlp, up_full, preferred_element_type=jnp.float32)
     hidden = jax.nn.gelu(up_value, approximate=False).astype(jnp.bfloat16)
     mlp_terms = lax.dot_general(
         hidden, down_t, contract_t, preferred_element_type=jnp.float32
     )
-    mlp_out = lax.psum_scatter(
-        mlp_terms.astype(jnp.bfloat16), "col", scatter_dimension=0, tiled=True
-    ).astype(jnp.float32)
+    mlp_out = lax.psum(mlp_terms.astype(jnp.bfloat16), "col").astype(jnp.float32)
     stream = (stream.astype(jnp.float32) + mlp_out).astype(jnp.bfloat16)
     merged = layer_norm(stream.astype(jnp.float32), merge_gain, merge_bias).astype(jnp.bfloat16)
-    merged = merged.reshape(tok_dev // 4, 4 * D)
-    merged_all = lax.all_gather(merged, "col", axis=0, tiled=True)
+    merged_all = merged.reshape(merged_row, 4 * D)
     out_dev = w_merge.shape[1]
     projected = jnp.dot(merged_all, merge_full, preferred_element_type=jnp.float32).astype(
         jnp.bfloat16

time: 305 us -> 302 us (level)
  blocking collectives: 75.7 us -> 17.6 us
  waiting for transfers between devices: 124 us -> 164 us
  starting transfers between devices: 20.5 us -> 27.9 us
  other arithmetic: 16 us -> 20.5 us
  local copies, waits for them, and re-layouts: 13.7 us -> 17.7 us
    psum x0 -> x2, waiting for transfers between devices: none -> 135 us  [the longest x1 67.8 us: local(): lax.psum(attn_terms.astype(jnp.bfloat16), 'col').astype(jnp.float32)]
    reduce_scatter x2 -> x0, waiting for transfers between devices: 61.3 us -> none  [the longest x1 32.1 us: local(): lax.psum_scatter(attn_terms.astype(jnp.bfloat16), 'col', scatter_dimensio...]
    all_to_all x2 -> x3, waiting for transfers between devices: 53.6 us -> 0.1 us  [row_gather(): received = lax.all_to_all(send, 'row', 0, 0, tiled=True)]
    all_to_all x1 -> x0, blocking collectives: 43.5 us -> none  [row_gather(): received = lax.all_to_all(send, 'row', 0, 0, tiled=True)]
    all_gather x3 -> x1, waiting for transfers between devices: 0.01 us -> 18.5 us  [local(): stream = lax.all_gather(tokens, 'col', axis=0, tiled=True)]
    unnamed x1, blocking collectives: 32.1 us -> 17.6 us
    all_to_all x2 -> x3, starting transfers between devices: 12.3 us -> 21.1 us  [row_gather(): received = lax.all_to_all(send, 'row', 0, 0, tiled=True)]
    reduce_sum x3, other arithmetic: 3.39 us -> 8.3 us  [layer_norm(): center = jnp.mean(values, axis=-1, keepdims=True)]
  transfers between devices with their start and end apart: 8 -> 7, of which waited for: 5 -> 5; matrix products, arithmetic and copies ran while one was open for 5% -> 20% of each run, Pallas kernels for 0% -> 0%
where the time goes in v2:
time: 302 us; the launch traced here: 299 us
  waiting for transfers between devices  164 us (54%)
  matrix products  37 us (12%)
  starting transfers between devices  27.9 us (9%)
  other arithmetic  20.5 us (7%)
  local copies, waits for them, and re-layouts  17.7 us (6%)
  blocking collectives  17.6 us (6%)
  between operations  14.8 us (5%)
    psum x1, waiting for transfers between devices, local(): lax.psum(attn_terms.astype(jnp.bfloat16), 'col').astype(jnp.float32)  67.8 us
    psum x1, waiting for transfers between devices, local(): lax.psum(mlp_terms.astype(jnp.bfloat16), 'col').astype(jnp.float32)  67.3 us
    all_to_all x3, starting transfers between devices, row_gather(): received = lax.all_to_all(send, 'row', 0, 0, tiled=True)  21.1 us
    all_gather x1, waiting for transfers between devices, local(): stream = lax.all_gather(tokens, 'col', axis=0, tiled=True)  18.5 us
    unnamed x1, blocking collectives  17.6 us
    dot_general x1, matrix products, local(): lax.dot_general(hidden, down_t, contract_t, preferred_element_type=jnp.fl...  12.6 us
    all_to_all x1, waiting for transfers between devices, local(): recv = lax.all_to_all(send, 'row', 0, 0, tiled=True)  9.32 us
    sub x2, matrix products, attend(): expo = jnp.exp(scores - peak)  8.6 us
  transfers between devices with their start and end apart: 7, of which 5 were waited for; matrix products, arithmetic and copies ran while one was open for 20% of the time, Pallas kernels for 0%

profile of v2, /device:TPU:1, one launch (start us, length us, event | category | flops | bytes accessed | tf_op | source)
XLA Modules:
  0.0 299.3 jit_solution(13002861895791961807)
XLA Ops:
  7.9 0.9 copy.28
  8.8 1.0 pad_maximum_fusion.1
  9.8 1.3 broadcast_in_dim.155
  11.1 7.6 %all-to-all-start = ((bf16[16,80,640]{2,1,0:T(8,128)(2,1)}), bf16[16,80,640]{2,1,0:T(8,128)(2,1)}, u32[]{:S(2)}, u32[]{:S(2)}) async-start(bf16[16,80,640]{2,1,0:T(8,128)(2,1)} %broadcast_in_dim.155), calls=%async_computation | async-start | bytes 3276800 | tf_op jit(solution)/shard_map/all_to_all | solution.py:49
  19.4 1.4 broadcast_compare_fusion.1
  20.8 18.5 %all-gather.3.cloned.1.call-done = bf16[1024,1280]{1,0:T(8,128)(2,1)} async-done(((bf16[128,1280]{1,0:T(8,128)(2,1)}), bf16[1024,1280]{1,0:T(8,128)(2,1)}) %all-gather.3.cloned.1.call-update) | async-done | bytes 2621456 | tf_op jit(solution)/shard_map/all_gather | solution.py:88
  39.3 2.3 convert_reduce_fusion.1
  42.8 1.9 broadcast_in_dim.159
  44.6 6.9 %all-to-all-start.1 = ((bf16[16,80,1280]{2,1,0:T(8,128)(2,1)}), bf16[16,80,1280]{2,1,0:T(8,128)(2,1)}, u32[]{:S(2)}, u32[]{:S(2)}) async-start(bf16[16,80,1280]{2,1,0:T(8,128)(2,1)} %broadcast_in_dim.159), calls=%async_computation.1 | async-start | bytes 6553600 | tf_op jit(solution)/shard_map/all_to_all | solution.py:49
  51.8 4.0 %fusion.56 = bf16[1024,480]{0,1:T(8,128)(2,1)} fusion(bf16[1024,1280]{1,0:T(8,128)(2,1)S(1)} %copy-done, f32[1280]{0:T(1024)S(1)} %get-tuple-element.8, f32[1280]{0:T(1024)S(1)} %get-tuple-element.27, f32[1024]{0:T(1024)S(1)} %add_rsqrt_fusion.2, f32[1024]{0:T(1024)S(1)} %broadcast_multiply_fusion.2, bf16[1280,640]{1,0:T(8,128)(2,1)} %bitcast.3), kind=kOutput, calls=%fused_computation.82 | convolution fusion | flops 1266647040 | bytes 4933632 | tf_op jit(solution)/shard_map/dot_general | solution.py:92
  55.8 4.9 %fusion.156 = (f32[2,512]{1,0:T(2,128)S(1)}, f32[2,512,1024]{2,1,0:T(8,128)}) fusion(pred[512,1024]{1,0:T(8,128)(4,1)} %get-tuple-element.15, bf16[1024,2,3,80]{0,3,2,1:T(8,128)(2,1)} %bitcast.93), kind=kOutput, calls=%fused_computation.228 | convolution fusion | flops 171967488 | bytes 5214208 | tf_op jit(solution)/shard_map/sub | solution.py:39
  60.8 3.7 %fusion.155 = (f32[2,512]{1,0:T(2,128)S(1)}, f32[2,512,1024]{2,1,0:T(8,128)}) fusion(pred[512,1024]{1,0:T(8,128)(4,1)S(1)} %get-tuple-element.16, bf16[1024,2,3,80]{0,3,2,1:T(8,128)(2,1)S(1)} %bitcast.94), kind=kOutput, calls=%fused_computation.227 | convolution fusion | flops 171967488 | bytes 5214208 | tf_op jit(solution)/shard_map/sub | solution.py:39
  64.4 3.2 %fusion.100 = bf16[2,80,512]{2,1,0:T(8,128)(2,1)S(1)} fusion(f32[2,512,1024]{2,1,0:T(8,128)} %get-tuple-element.22, f32[2,512]{1,0:T(2,128)S(1)} %get-tuple-element.21, bf16[1024,2,3,80]{0,3,2,1:T(8,128)(2,1)S(1)} %bitcast.95), kind=kOutput, calls=%fused_computation.116 | convolution fusion | flops 169951232 | bytes 4689920 | tf_op jit(solution)/shard_map/hqk,khd->qhd/dot_general | solution.py:41
  67.9 0.8 fusion.99
  68.7 3.8 %convolution_convert_fusion.1 = bf16[1024,1280]{1,0:T(8,128)(2,1)} fusion(bf16[1280,640]{1,0:T(8,128)(2,1)} %bitcast.3, bf16[512,160]{0,1:T(8,128)(2,1)S(1)} %bitcast.86, bf16[512,160]{0,1:T(8,128)(2,1)S(1)} %bitcast.85), kind=kOutput, calls=%fused_computation.41 | convolution fusion | flops 421396480 | bytes 3604480 | tf_op jit(solution)/shard_map/dot_general | solution.py:95
  72.5 67.8 %all-reduce.5.cloned.1.call-done = bf16[1024,1280]{1,0:T(8,128)(2,1)} async-done(((bf16[1024,1280]{1,0:T(8,128)(2,1)}), bf16[1024,1280]{1,0:T(8,128)(2,1)}) %all-reduce.5.cloned.1.call-update) | async-done | bytes 2621456 | tf_op jit(solution)/shard_map/psum | solution.py:98
  140.3 3.4 %convert_reduce_fusion = (f32[1024]{0:T(1024)S(1)}, bf16[1024,1280]{1,0:T(8,128)(2,1)S(1)}) fusion(bf16[1024,1280]{1,0:T(8,128)(2,1)} %all-reduce.5.cloned.1.call-done, bf16[1024,1280]{1,0:T(8,128)(2,1)} %all-gather.3.cloned.1.call-done), kind=kLoop, calls=%fused_computation.7 | loop fusion | flops 7863296 | bytes 7868416 | tf_op jit(solution)/shard_map/reduce_sum | solution.py:13
  144.7 2.9 broadcast_in_dim.160
  147.5 6.6 %all-to-all-start.2 = ((bf16[16,320,512]{2,1,0:T(8,128)(2,1)}), bf16[16,320,512]{2,1,0:T(8,128)(2,1)}, u32[]{:S(2)}, u32[]{:S(2)}) async-start(bf16[16,320,512]{2,1,0:T(8,128)(2,1)} %broadcast_in_dim.160), calls=%async_computation.2 | async-start | bytes 10485760 | tf_op jit(solution)/shard_map/all_to_all | solution.py:49
  154.4 12.6 %convolution_convert_fusion = bf16[1024,1280]{1,0:T(8,128)(2,1)} fusion(bf16[1280,1280]{1,0:T(8,128)(2,1)} %bitcast.17, bf16[1024,1280]{1,0:T(8,128)(2,1)S(1)} %get-tuple-element.14, f32[1280]{0:T(1024)S(1)} %get-tuple-element.7, f32[1280]{0:T(1024)S(1)} %get-tuple-element.28, f32[1024]{0:T(1024)S(1)} %add_rsqrt_fusion.1, f32[1024]{0:T(1024)S(1)} %broadcast_multiply_fusion.1), kind=kOutput, calls=%fused_computation.40 | convolution fusion | flops 3407216640 | bytes 8538112 | tf_op jit(solution)/shard_map/dot_general | solution.py:105
  168.2 67.3 %all-reduce.7.cloned.1.call-done = bf16[1024,1280]{1,0:T(8,128)(2,1)} async-done(((bf16[1024,1280]{1,0:T(8,128)(2,1)}), bf16[1024,1280]{1,0:T(8,128)(2,1)}) %all-reduce.7.cloned.1.call-update) | async-done | bytes 2621456 | tf_op jit(solution)/shard_map/psum | solution.py:108
  235.5 2.6 convert_reduce_fusion.2
  238.1 1.1 fusion.16
  239.3 3.0 fusion.19
  242.3 4.0 %reshape.274 = bf16[256,5120]{1,0:T(8,128)(2,1)S(1)} reshape(bf16[1024,1280]{1,0:T(8,128)(2,1)} %fusion.19) | data formatting | bytes 5242880 | tf_op jit(solution)/shard_map/reshape | solution.py:111
  246.3 4.0 %convolution_convert_fusion.2 = bf16[256,512]{1,0:T(8,128)(2,1)S(1)} fusion(bf16[256,5120]{1,0:T(8,128)(2,1)S(1)} %reshape.274, bf16[5120,512]{1,0:T(8,128)(2,1)} %bitcast.18), kind=kOutput, calls=%fused_computation.114 | convolution fusion | flops 1342308352 | bytes 8126464 | tf_op jit(solution)/shard_map/dot_general | solution.py:113
  250.4 2.7 gather_fusion.1
  253.1 1.1 broadcast_select_fusion
  254.1 6.3 %all-to-all-start.3 = ((bf16[16,48,512]{2,1,0:T(8,128)(2,1)}), bf16[16,48,512]{2,1,0:T(8,128)(2,1)S(1)}, u32[]{:S(2)}, u32[]{:S(2)}) async-start(bf16[16,48,512]{2,1,0:T(8,128)(2,1)} %broadcast_select_fusion), calls=%async_computation.3 | async-start | bytes 1572864 | tf_op jit(solution)/shard_map/all_to_all | solution.py:133
  262.9 9.3 %all-to-all-done.3 = bf16[16,48,512]{2,1,0:T(8,128)(2,1)S(1)} async-done(((bf16[16,48,512]{2,1,0:T(8,128)(2,1)}), bf16[16,48,512]{2,1,0:T(8,128)(2,1)S(1)}, u32[]{:S(2)}, u32[]{:S(2)}) %all-to-all-start.3) | async-done | bytes 786464 | tf_op jit(solution)/shard_map/all_to_all | solution.py:133
  273.3 17.6 %all-reduce.1 = f32[128]{0:T(128)S(1)} all-reduce(f32[128]{0:T(128)S(1)} %maximum_dynamic-update-slice_fusion), channel_id=2, replica_groups=mesh['row'=16,'col'=8] {'col'}, use_global_device_ids=true, to_apply=%add.1 | all-reduce | flops 128 | bytes 1024
  291.8 1.0 divide_convert_fusion.8
  (85 shorter events, 9.2 us)
Async XLA Ops:
  7.2 32.2 %all-gather.3.cloned.1.call-start = ((), (), s32[]{:S(2)}) async-start(), calls=%async_computation.4 | async-start | bytes 2949120 | tf_op jit(solution)/shard_map/all_gather | solution.py:88
  8.8 10.0 %copy-start.5 = (s32[16,8]{0,1:T(8,128)S(1)}, s32[16,8]{0,1:T(8,128)}, u32[]{:S(2)}) copy-start(s32[16,8]{0,1:T(8,128)} %param.13) | copy-start | bytes 1540
  8.8 10.5 %copy-start.6 = (f32[1,2,1280]{2,1,0:T(2,128)S(1)}, f32[1,2,1280]{2,1,0:T(2,128)}, u32[]{:S(2)}) copy-start(f32[1,2,1280]{2,1,0:T(2,128)} %param.16) | copy-start | bytes 30724
  8.8 10.5 %copy-start.7 = (f32[1,2,1280]{2,1,0:T(2,128)S(1)}, f32[1,2,1280]{2,1,0:T(2,128)}, u32[]{:S(2)}) copy-start(f32[1,2,1280]{2,1,0:T(2,128)} %param.15) | copy-start | bytes 30724
  9.8 9.6 %copy-start.3 = (bf16[1,640,80]{1,2,0:T(8,128)(2,1)S(1)}, bf16[1,640,80]{1,2,0:T(8,128)(2,1)}, u32[]{:S(2)}) copy-start(bf16[1,640,80]{1,2,0:T(8,128)(2,1)} %param.20) | copy-start | bytes 307204
  9.8 9.6 %copy-start.4 = (bf16[1,80,640]{2,1,0:T(8,128)(2,1)S(1)}, bf16[1,80,640]{2,1,0:T(8,128)(2,1)}, u32[]{:S(2)}) copy-start(bf16[1,80,640]{2,1,0:T(8,128)(2,1)} %param.19) | copy-start | bytes 307204
  11.1 31.7 %all-to-all-start = ((bf16[16,80,640]{2,1,0:T(8,128)(2,1)}), bf16[16,80,640]{2,1,0:T(8,128)(2,1)}, u32[]{:S(2)}, u32[]{:S(2)}) async-start(bf16[16,80,640]{2,1,0:T(8,128)(2,1)} %broadcast_in_dim.155), calls=%async_computation | async-start | bytes 3276800 | tf_op jit(solution)/shard_map/all_to_all | solution.py:49
  39.3 2.5 copy-start
  44.6 99.9 %all-to-all-start.1 = ((bf16[16,80,1280]{2,1,0:T(8,128)(2,1)}), bf16[16,80,1280]{2,1,0:T(8,128)(2,1)}, u32[]{:S(2)}, u32[]{:S(2)}) async-start(bf16[16,80,1280]{2,1,0:T(8,128)(2,1)} %broadcast_in_dim.159), calls=%async_computation.1 | async-start | bytes 6553600 | tf_op jit(solution)/shard_map/all_to_all | solution.py:49
  51.6 88.8 %all-reduce.5.cloned.1.call-start = ((), (), s32[]{:S(2)}) async-start(), calls=%async_computation.5 | async-start | bytes 5242880 | tf_op jit(solution)/shard_map/psum | solution.py:98
  55.8 4.9 %copy-start.12 = (bf16[1024,480]{0,1:T(8,128)(2,1)S(1)}, bf16[1024,480]{0,1:T(8,128)(2,1)}, u32[]{:S(2)}) copy-start(bf16[1024,480]{0,1:T(8,128)(2,1)} %fusion.56) | copy-start | bytes 2949124
  64.4 3.4 %copy-start.14 = (f32[2,512,1024]{2,1,0:T(8,128)S(1)}, f32[2,512,1024]{2,1,0:T(8,128)}, u32[]{:S(2)}) copy-start(f32[2,512,1024]{2,1,0:T(8,128)} %get-tuple-element.20) | copy-start | bytes 12582916
  143.7 1.0 copy-start.2
  147.5 98.8 %all-to-all-start.2 = ((bf16[16,320,512]{2,1,0:T(8,128)(2,1)}), bf16[16,320,512]{2,1,0:T(8,128)(2,1)}, u32[]{:S(2)}, u32[]{:S(2)}) async-start(bf16[16,320,512]{2,1,0:T(8,128)(2,1)} %broadcast_in_dim.160), calls=%async_computation.2 | async-start | bytes 10485760 | tf_op jit(solution)/shard_map/all_to_all | solution.py:49
  154.1 81.3 %all-reduce.7.cloned.1.call-start = ((), (), s32[]{:S(2)}) async-start(), calls=%async_computation.6 | async-start | bytes 5242880 | tf_op jit(solution)/shard_map/psum | solution.py:108
  166.9 0.7 copy-start.10
  235.5 2.7 copy-start.1
  238.1 1.1 copy-start.8
  238.1 1.1 copy-start.9
  253.0 8.6 %copy-start.13 = (u32[128]{0:T(128)S(1)}, u32[128]{0:T(128)}, u32[]{:S(2)}) copy-start(u32[128]{0:T(128)} %constant.178) | copy-start | bytes 1540
  254.1 18.1 %all-to-all-start.3 = ((bf16[16,48,512]{2,1,0:T(8,128)(2,1)}), bf16[16,48,512]{2,1,0:T(8,128)(2,1)S(1)}, u32[]{:S(2)}, u32[]{:S(2)}) async-start(bf16[16,48,512]{2,1,0:T(8,128)(2,1)} %broadcast_select_fusion), calls=%async_computation.3 | async-start | bytes 1572864 | tf_op jit(solution)/shard_map/all_to_all | solution.py:133
  291.6 1.1 copy-start.11
Sparse Core Ops, SparseCore 0:
  9.7 29.6 all-gather.2
  72.7 67.6 all-reduce.4
  167.1 68.3 all-reduce.6

commit v3 on v0

--- a/solution.py
+++ b/solution.py
@@ -93,12 +93,17 @@
     qkv = jnp.dot(normed_all, qkv_full, preferred_element_type=jnp.float32)
     qkv = qkv.astype(jnp.bfloat16).reshape(tok_row, -1, 3, HEAD_DIM)
     context = attend(qkv, segments)
-    attn_terms = lax.dot_general(
-        context, out_t, contract_t, preferred_element_type=jnp.float32
-    )
-    attn_out = lax.psum_scatter(
-        attn_terms.astype(jnp.bfloat16), "col", scatter_dimension=0, tiled=True
-    ).astype(jnp.float32)
+    head_cols = context.shape[1]
+    pieces = lax.all_to_all(context.reshape(n_col, tok_dev, head_cols), "col", 0, 0, tiled=True)
+    out_all = lax.all_gather(out_t.T, "col", axis=0, tiled=True)
+    attn_out = jnp.zeros((tok_dev, D), jnp.float32)
+    for c in range(n_col):
+        term = jnp.dot(
+            pieces[c],
+            out_all[c * head_cols : (c + 1) * head_cols],
+            preferred_element_type=jnp.float32,
+        )
+        attn_out = attn_out + term.astype(jnp.bfloat16).astype(jnp.float32)
     stream = (stream.astype(jnp.float32) + attn_out).astype(jnp.bfloat16)
     normed = layer_norm(stream.astype(jnp.float32), ln_gain[0, 1], ln_bias[0, 1]).astype(
         jnp.bfloat16

time: 305 us -> 279 us (0.915)
  waiting for transfers between devices: 124 us -> 80.8 us
  blocking collectives: 75.7 us -> 106 us
  starting transfers between devices: 20.5 us -> 9.79 us
  other arithmetic: 16 us -> 12.9 us
    reduce_scatter x1 -> x0, waiting for transfers between devices: 32.1 us -> none  [local(): lax.psum_scatter(attn_terms.astype(jnp.bfloat16), 'col', scatter_dimensio...]
    all_to_all x1 -> x2, blocking collectives: 43.5 us -> 74 us  [row_gather(): received = lax.all_to_all(send, 'row', 0, 0, tiled=True)]
    all_to_all x0 -> x1, blocking collectives: none -> 14.5 us  [local(): lax.all_to_all(context.reshape(n_col, tok_dev, head_cols), 'col', 0, 0, t...]
    unnamed x1, blocking collectives: 32.1 us -> 17.8 us
    all_to_all x2 -> x1, starting transfers between devices: 12.3 us -> 4.7 us  [row_gather(): received = lax.all_to_all(send, 'row', 0, 0, tiled=True)]
    reduce_scatter x1, waiting for transfers between devices: 29.2 us -> 23.1 us  [local(): lax.psum_scatter(mlp_terms.astype(jnp.bfloat16), 'col', scatter_dimension...]
    all_to_all x2 -> x1, waiting for transfers between devices: 53.6 us -> 48.5 us  [row_gather(): received = lax.all_to_all(send, 'row', 0, 0, tiled=True)]
    all_to_all x1, starting transfers between devices: 7.99 us -> 4.89 us  [local(): recv = lax.all_to_all(send, 'row', 0, 0, tiled=True)]
  transfers between devices with their start and end apart: 8 -> 7, of which waited for: 5 -> 3; matrix products, arithmetic and copies ran while one was open for 5% -> 10% of each run, Pallas kernels for 0% -> 0%
where the time goes in v3:
time: 279 us; the launch traced here: 278 us
  blocking collectives  106 us (38%)
  waiting for transfers between devices  80.8 us (29%)
  matrix products  39.9 us (14%)
  between operations  14.8 us (5%)
  local copies, waits for them, and re-layouts  14 us (5%)
  other arithmetic  12.9 us (5%)
  starting transfers between devices  9.79 us (4%)
    all_to_all x2, blocking collectives, row_gather(): received = lax.all_to_all(send, 'row', 0, 0, tiled=True)  74 us
    all_to_all x1, waiting for transfers between devices, row_gather(): received = lax.all_to_all(send, 'row', 0, 0, tiled=True)  48.5 us
    reduce_scatter x1, waiting for transfers between devices, local(): lax.psum_scatter(mlp_terms.astype(jnp.bfloat16), 'col', scatter_dimension...  23.1 us
    unnamed x1, blocking collectives  17.8 us
    all_to_all x1, blocking collectives, local(): lax.all_to_all(context.reshape(n_col, tok_dev, head_cols), 'col', 0, 0, t...  14.5 us
    dot_general x1, matrix products, local(): lax.dot_general(hidden, down_t, contract_t, preferred_element_type=jnp.fl...  13 us
    all_to_all x1, waiting for transfers between devices, local(): recv = lax.all_to_all(send, 'row', 0, 0, tiled=True)  9.16 us
    sub x2, matrix products, attend(): expo = jnp.exp(scores - peak)  8.43 us
  transfers between devices with their start and end apart: 7, of which 3 were waited for; matrix products, arithmetic and copies ran while one was open for 10% of the time, Pallas kernels for 0%

profile of v3, /device:TPU:1, one launch (start us, length us, event | category | flops | bytes accessed | tf_op | source)
XLA Modules:
  0.0 278.5 jit_solution(4191222139054245202)
XLA Ops:
  7.2 1.1 convert_reduce_fusion
  8.3 1.2 fusion.86
  10.4 2.0 fusion.89
  12.4 0.9 copy.50
  13.3 1.0 pad_maximum_fusion.1
  14.4 29.9 %all_to_all.25 = bf16[16,80,640]{2,1,0:T(8,128)(2,1)S(1)} all-to-all(bf16[16,80,640]{2,1,0:T(8,128)(2,1)S(1)} %broadcast_in_dim.155), channel_id=1, replica_groups=mesh['row'=16,'col'=8] {'row'}, dimensions={0} | all-to-all | bytes 3276800 | tf_op jit(solution)/shard_map/all_to_all | solution.py:49
  44.6 1.0 copy.56
  46.9 4.2 %convolution_convert_fusion.9 = bf16[1024,480]{0,1:T(8,128)(2,1)} fusion(bf16[1024,1280]{1,0:T(8,128)(2,1)} %all-gather.6.cloned.1.call-done, bf16[1280,640]{1,0:T(8,128)(2,1)S(1)} %bitcast.121), kind=kOutput, calls=%fused_computation.70 | convolution fusion | flops 1258782720 | bytes 4915200 | tf_op jit(solution)/shard_map/dot_general | solution.py:93
  51.1 4.8 %fusion.149 = (f32[2,512]{1,0:T(2,128)S(1)}, f32[2,512,1024]{2,1,0:T(8,128)}) fusion(pred[512,1024]{1,0:T(8,128)(4,1)S(1)} %get-tuple-element.15, bf16[1024,2,3,80]{0,3,2,1:T(8,128)(2,1)} %bitcast.131), kind=kOutput, calls=%fused_computation.249 | convolution fusion | flops 171967488 | bytes 5214208 | tf_op jit(solution)/shard_map/sub | solution.py:39
  55.8 3.7 %fusion.148 = (f32[2,512]{1,0:T(2,128)S(1)}, f32[2,512,1024]{2,1,0:T(8,128)}) fusion(pred[512,1024]{1,0:T(8,128)(4,1)S(1)} %get-tuple-element.16, bf16[1024,2,3,80]{0,3,2,1:T(8,128)(2,1)S(1)} %bitcast.132), kind=kOutput, calls=%fused_computation.248 | convolution fusion | flops 171967488 | bytes 5214208 | tf_op jit(solution)/shard_map/sub | solution.py:39
  59.5 3.2 %fusion.79 = bf16[2,80,512]{2,1,0:T(8,128)(2,1)S(1)} fusion(f32[2,512,1024]{2,1,0:T(8,128)} %get-tuple-element.22, f32[2,512]{1,0:T(2,128)S(1)} %get-tuple-element.21, bf16[1024,2,3,80]{0,3,2,1:T(8,128)(2,1)S(1)} %bitcast.133), kind=kOutput, calls=%fused_computation.104 | convolution fusion | flops 169951232 | bytes 4689920 | tf_op jit(solution)/shard_map/hqk,khd->qhd/dot_general | solution.py:41
  64.0 14.5 %all_to_all.26 = bf16[8,128,160]{1,2,0:T(8,128)(2,1)S(1)} all-to-all(bf16[8,128,160]{1,2,0:T(8,128)(2,1)S(1)} %copy_bitcast_fusion), channel_id=1, replica_groups=mesh['row'=16,'col'=8] {'col'}, dimensions={0} | all-to-all | bytes 655360 | tf_op jit(solution)/shard_map/all_to_all | solution.py:97
  78.5 1.4 fusion.31
  79.9 1.3 fusion.30
  81.2 1.3 fusion.28
  84.4 0.9 add_convert_fusion.1
  85.6 44.0 %all_to_all.27 = bf16[16,80,1280]{2,1,0:T(8,128)(2,1)} all-to-all(bf16[16,80,1280]{2,1,0:T(8,128)(2,1)S(1)} %broadcast_in_dim.159), channel_id=1, replica_groups=mesh['row'=16,'col'=8] {'row'}, dimensions={0} | all-to-all | bytes 6553600 | tf_op jit(solution)/shard_map/all_to_all | solution.py:49
  129.7 13.0 %convolution_convert_fusion = bf16[1024,1280]{1,0:T(8,128)(2,1)} fusion(bf16[1280,1280]{1,0:T(8,128)(2,1)} %bitcast.119, bf16[1024,1280]{1,0:T(8,128)(2,1)} %all-gather.10.cloned.1.call-done), kind=kOutput, calls=%fused_computation.12 | convolution fusion | flops 3399352320 | bytes 8519680 | tf_op jit(solution)/shard_map/dot_general | solution.py:114
  142.7 0.9 copy-done.2
  143.6 2.9 %broadcast_in_dim.160 = bf16[16,320,512]{2,1,0:T(8,128)(2,1)} broadcast(bf16[320,512]{1,0:T(8,128)(2,1)S(1)} %copy-done.2), dimensions={1,2} | broadcast | bytes 5570560 | tf_op jit(solution)/shard_map/broadcast_in_dim | solution.py:48
  146.5 4.7 %all-to-all-start.3 = ((bf16[16,320,512]{2,1,0:T(8,128)(2,1)}), bf16[16,320,512]{2,1,0:T(8,128)(2,1)}, u32[]{:S(2)}, u32[]{:S(2)}) async-start(bf16[16,320,512]{2,1,0:T(8,128)(2,1)} %broadcast_in_dim.160), calls=%async_computation.4 | async-start | bytes 10485760 | tf_op jit(solution)/shard_map/all_to_all | solution.py:49
  151.3 23.1 %reduce-scatter.2.cloned.1.call-done = bf16[128,1280]{1,0:T(8,128)(2,1)} async-done(((bf16[1024,1280]{1,0:T(8,128)(2,1)}), bf16[128,1280]{1,0:T(8,128)(2,1)}) %reduce-scatter.2.cloned.1.call-update) | async-done | bytes 327696 | tf_op jit(solution)/shard_map/reduce_scatter | solution.py:117
  174.3 1.1 convert_reduce_fusion.1
  176.0 0.9 reshape.278
  177.6 48.5 %all-to-all-done.3 = bf16[16,320,512]{2,1,0:T(8,128)(2,1)} async-done(((bf16[16,320,512]{2,1,0:T(8,128)(2,1)}), bf16[16,320,512]{2,1,0:T(8,128)(2,1)}, u32[]{:S(2)}, u32[]{:S(2)}) %all-to-all-start.3) | async-done | bytes 5242912 | tf_op jit(solution)/shard_map/all_to_all | solution.py:49
  226.0 4.8 %convolution_convert_fusion.10 = bf16[256,512]{1,0:T(8,128)(2,1)S(1)} fusion(bf16[256,5120]{1,0:T(8,128)(2,1)} %all-gather.12.cloned.1.call-done, bf16[5120,512]{1,0:T(8,128)(2,1)} %bitcast.27), kind=kOutput, calls=%fused_computation.102 | convolution fusion | flops 1342308352 | bytes 8126464 | tf_op jit(solution)/shard_map/dot_general | solution.py:125
  230.9 2.7 gather_fusion.1
  233.6 1.1 broadcast_select_fusion
  234.6 4.9 %all-to-all-start.4 = ((bf16[16,48,512]{2,1,0:T(8,128)(2,1)}), bf16[16,48,512]{2,1,0:T(8,128)(2,1)S(1)}, u32[]{:S(2)}, u32[]{:S(2)}) async-start(bf16[16,48,512]{2,1,0:T(8,128)(2,1)} %broadcast_select_fusion), calls=%async_computation.5 | async-start | bytes 1572864 | tf_op jit(solution)/shard_map/all_to_all | solution.py:145
  242.0 9.2 %all-to-all-done.4 = bf16[16,48,512]{2,1,0:T(8,128)(2,1)S(1)} async-done(((bf16[16,48,512]{2,1,0:T(8,128)(2,1)}), bf16[16,48,512]{2,1,0:T(8,128)(2,1)S(1)}, u32[]{:S(2)}, u32[]{:S(2)}) %all-to-all-start.4) | async-done | bytes 786464 | tf_op jit(solution)/shard_map/all_to_all | solution.py:145
  252.3 17.8 %all-reduce.1 = f32[128]{0:T(128)S(1)} all-reduce(f32[128]{0:T(128)S(1)} %maximum_dynamic-update-slice_fusion), channel_id=2, replica_groups=mesh['row'=16,'col'=8] {'col'}, use_global_device_ids=true, to_apply=%add.1 | all-reduce | flops 128 | bytes 1024
  270.9 1.0 divide_convert_fusion.8
  (97 shorter events, 10.9 us)
Async XLA Ops:
  7.2 39.8 %all-gather.6.cloned.1.call-start = ((), (), s32[]{:S(2)}) async-start(), calls=%async_computation.6 | async-start | bytes 2949120 | tf_op jit(solution)/shard_map/all_gather | solution.py:92
  12.4 66.2 %all-gather.8.cloned.1.call-start = ((), (), s32[]{:S(2)}) async-start(), calls=%async_computation.7 | async-start | bytes 3686400 | tf_op jit(solution)/shard_map/all_gather | solution.py:98
  14.4 31.3 %copy-start.5 = (s32[16,8]{0,1:T(8,128)S(1)}, s32[16,8]{0,1:T(8,128)}, u32[]{:S(2)}) copy-start(s32[16,8]{0,1:T(8,128)} %param.13) | copy-start | bytes 1540
  45.6 84.0 %all-gather.10.cloned.1.call-start = ((), (), s32[]{:S(2)}) async-start(), calls=%async_computation.8 | async-start | bytes 2949120 | tf_op jit(solution)/shard_map/all_gather | solution.py:111
  51.1 4.8 %copy-start.10 = (bf16[1024,480]{0,1:T(8,128)(2,1)S(1)}, bf16[1024,480]{0,1:T(8,128)(2,1)}, u32[]{:S(2)}) copy-start(bf16[1024,480]{0,1:T(8,128)(2,1)} %convolution_convert_fusion.9) | copy-start | bytes 2949124
  59.5 3.6 %copy-start.12 = (f32[2,512,1024]{2,1,0:T(8,128)S(1)}, f32[2,512,1024]{2,1,0:T(8,128)}, u32[]{:S(2)}) copy-start(f32[2,512,1024]{2,1,0:T(8,128)} %get-tuple-element.20) | copy-start | bytes 12582916
  78.5 4.0 %copy-start.1 = (bf16[1280,1280]{1,0:T(8,128)(2,1)S(1)}, bf16[1280,1280]{1,0:T(8,128)(2,1)}, u32[]{:S(2)}) copy-start(bf16[1280,1280]{1,0:T(8,128)(2,1)} %all-gather.8.cloned.1.call-done) | copy-start | bytes 9830404
  82.8 1.0 copy-start
  83.3 2.0 copy-start.3
  83.4 2.0 copy-start.4
  85.3 89.0 %reduce-scatter.2.cloned.1.call-start = ((), (), s32[]{:S(2)}) async-start(), calls=%async_computation.9 | async-start | bytes 2949120 | tf_op jit(solution)/shard_map/reduce_scatter | solution.py:117
  142.7 1.0 copy-start.2
  146.5 29.2 %copy-start.6 = (f32[1280]{0:T(1024)S(1)}, f32[1280]{0:T(1024)}, u32[]{:S(2)}) copy-start(f32[1280]{0:T(1024)} %param.22) | copy-start | bytes 15364
  146.5 29.2 %copy-start.7 = (f32[1280]{0:T(1024)S(1)}, f32[1280]{0:T(1024)}, u32[]{:S(2)}) copy-start(f32[1280]{0:T(1024)} %param.21) | copy-start | bytes 15364
  146.5 79.5 %all-to-all-start.3 = ((bf16[16,320,512]{2,1,0:T(8,128)(2,1)}), bf16[16,320,512]{2,1,0:T(8,128)(2,1)}, u32[]{:S(2)}, u32[]{:S(2)}) async-start(bf16[16,320,512]{2,1,0:T(8,128)(2,1)} %broadcast_in_dim.160), calls=%async_computation.4 | async-start | bytes 10485760 | tf_op jit(solution)/shard_map/all_to_all | solution.py:49
  151.2 25.8 %copy-start.8 = (s32[128]{0:T(128)S(1)}, s32[128]{0:T(128)}, u32[]{:S(2)}) copy-start(s32[128]{0:T(128)} %param.14) | copy-start | bytes 1540
  151.2 74.8 %all-gather.12.cloned.1.call-start = ((), (), s32[]{:S(2)}) async-start(), calls=%async_computation.10 | async-start | bytes 2949120 | tf_op jit(solution)/shard_map/all_gather | solution.py:123
  233.6 7.2 %copy-start.11 = (u32[128]{0:T(128)S(1)}, u32[128]{0:T(128)}, u32[]{:S(2)}) copy-start(u32[128]{0:T(128)} %constant.178) | copy-start | bytes 1540
  234.6 16.6 %all-to-all-start.4 = ((bf16[16,48,512]{2,1,0:T(8,128)(2,1)}), bf16[16,48,512]{2,1,0:T(8,128)(2,1)S(1)}, u32[]{:S(2)}, u32[]{:S(2)}) async-start(bf16[16,48,512]{2,1,0:T(8,128)(2,1)} %broadcast_select_fusion), calls=%async_computation.5 | async-start | bytes 1572864 | tf_op jit(solution)/shard_map/all_to_all | solution.py:145
  270.8 1.1 copy-start.9
Sparse Core Ops, SparseCore 0:
  12.5 29.6 all-gather.5
  45.7 28.7 all-gather.7
  85.4 24.7 all-gather.9
  142.8 31.4 reduce-scatter.1
  177.1 28.4 all-gather.11

commit v4 on v3

--- a/solution.py
+++ b/solution.py
@@ -94,15 +94,18 @@
     qkv = qkv.astype(jnp.bfloat16).reshape(tok_row, -1, 3, HEAD_DIM)
     context = attend(qkv, segments)
     head_cols = context.shape[1]
-    pieces = lax.all_to_all(context.reshape(n_col, tok_dev, head_cols), "col", 0, 0, tiled=True)
+    col_index = lax.axis_index("col")
     out_all = lax.all_gather(out_t.T, "col", axis=0, tiled=True)
     attn_out = jnp.zeros((tok_dev, D), jnp.float32)
-    for c in range(n_col):
-        term = jnp.dot(
-            pieces[c],
-            out_all[c * head_cols : (c + 1) * head_cols],
-            preferred_element_type=jnp.float32,
-        )
+    for shift in range(n_col):
+        target = (col_index + shift) % n_col
+        block = lax.dynamic_slice_in_dim(context, target * tok_dev, tok_dev, 0)
+        if shift:
+            pairs = [(i, (i + shift) % n_col) for i in range(n_col)]
+            block = lax.ppermute(block, "col", pairs)
+        source = (col_index - shift) % n_col
+        rows = lax.dynamic_slice_in_dim(out_all, source * head_cols, head_cols, 0)
+        term = jnp.dot(block, rows, preferred_element_type=jnp.float32)
         attn_out = attn_out + term.astype(jnp.bfloat16).astype(jnp.float32)
     stream = (stream.astype(jnp.float32) + attn_out).astype(jnp.bfloat16)
     normed = layer_norm(stream.astype(jnp.float32), ln_gain[0, 1], ln_bias[0, 1]).astype(
@@ -144,16 +147,28 @@
     send = jnp.take(padded, rows.reshape(-1), axis=0).reshape(n_row, most, out_dev)
     recv = lax.all_to_all(send, "row", 0, 0, tiled=True)
 
+    owner = segment_ids(sizes_here, merged_row * 4)[::4]
+    own = owner[:, None] == jnp.arange(IMG_ROW, dtype=jnp.int32)[None, :]
+    proj32 = projected.astype(jnp.float32)
+    row_sq = jnp.sum(proj32 * proj32, axis=1)
+    row_peak = jnp.max(jnp.abs(proj32), axis=1)
+    part_sq = jnp.sum(jnp.where(own, row_sq[:, None], 0.0), axis=0)
+    part_peak = jnp.max(jnp.where(own, row_peak[:, None], 0.0), axis=0)
+    col_stats = lax.all_gather(jnp.concatenate([part_sq, part_peak]), "col", axis=0, tiled=False)
+    group_stats = jnp.concatenate(
+        [jnp.sum(col_stats[:, :IMG_ROW], axis=0), jnp.max(col_stats[:, IMG_ROW:], axis=0)]
+    )
+    all_stats = lax.all_gather(group_stats, "row", axis=0, tiled=False)
+    req_sq = all_stats[:, :IMG_ROW].reshape(-1)
+    req_peak = all_stats[:, IMG_ROW:].reshape(-1)
+
     request = lax.dynamic_slice_in_dim(req_at_slot, row_index * IMG_ROW, IMG_ROW)
     source = request // IMG_ROW
     taken = jnp.take(recv, source, axis=0)
     valid = inner[None, :] < sizes_flat[request][:, None]
     blocks = jnp.where(valid[:, :, None], taken, jnp.zeros_like(taken)).astype(jnp.float32)
-    squares = jnp.sum(blocks * blocks, axis=(1, 2))
-    peaks = jnp.max(jnp.abs(blocks), axis=(1, 2))
-    stats = lax.all_gather(jnp.concatenate([squares, peaks]), "col", axis=0, tiled=False)
-    squares = jnp.sum(stats[:, :IMG_ROW], axis=0)
-    peaks = jnp.max(stats[:, IMG_ROW:], axis=0)
+    squares = req_sq[request]
+    peaks = req_peak[request]
     slot_size = sizes_flat[request].astype(jnp.float32)
     req_norm = jnp.sqrt(squares / (slot_size * OUT) + 1e-06)
     merged_out = (

time: 279 us -> 316 us (1.13)
  the two profiles are of different devices: /device:TPU:1 before, /device:TPU:0 now
where the time goes in v4:
time: 316 us; the launch traced here: 315 us
  blocking collectives  140 us (44%)
  waiting for transfers between devices  68.9 us (22%)
  matrix products  40.1 us (13%)
  starting transfers between devices  20.4 us (6%)
  local copies, waits for them, and re-layouts  16.9 us (5%)
  between operations  15.8 us (5%)
  other arithmetic  12.4 us (4%)
    all_to_all x2, blocking collectives, row_gather(): received = lax.all_to_all(send, 'row', 0, 0, tiled=True)  79.5 us
    unnamed x2, blocking collectives  60.9 us
    all_to_all x1, waiting for transfers between devices, row_gather(): received = lax.all_to_all(send, 'row', 0, 0, tiled=True)  42.8 us
    reduce_scatter x1, waiting for transfers between devices, local(): lax.psum_scatter(mlp_terms.astype(jnp.bfloat16), 'col', scatter_dimension...  24.6 us
    dot_general x1, matrix products, local(): lax.dot_general(hidden, down_t, contract_t, preferred_element_type=jnp.fl...  13 us
    ppermute x7, starting transfers between devices, local(): block = lax.ppermute(block, 'col', pairs)  10.9 us
    sub x2, matrix products, attend(): expo = jnp.exp(scores - peak)  8.43 us
  transfers between devices with their start and end apart: 14, of which 3 were waited for; matrix products, arithmetic and copies ran while one was open for 12% of the time, Pallas kernels for 0%

profile of v4, /device:TPU:0, one launch (start us, length us, event | category | flops | bytes accessed | tf_op | source)
XLA Modules:
  0.0 315.0 jit_solution(14802638217029475223)
XLA Ops:
  7.2 1.1 convert_reduce_fusion
  8.3 1.2 fusion.84
  10.4 2.0 fusion.87
  13.3 1.0 pad_maximum_fusion.1
  14.4 30.4 %all_to_all.20 = bf16[16,80,640]{2,1,0:T(8,128)(2,1)S(1)} all-to-all(bf16[16,80,640]{2,1,0:T(8,128)(2,1)S(1)} %broadcast_in_dim.173), channel_id=1, replica_groups=mesh['row'=16,'col'=8] {'row'}, dimensions={0} | all-to-all | bytes 3276800 | tf_op jit(solution)/shard_map/all_to_all | solution.py:49
  47.7 4.2 %convolution_convert_fusion.9 = bf16[1024,480]{0,1:T(8,128)(2,1)} fusion(bf16[1024,1280]{1,0:T(8,128)(2,1)} %all-gather.7.cloned.1.call-done, bf16[1280,640]{1,0:T(8,128)(2,1)S(1)} %bitcast.98), kind=kOutput, calls=%fused_computation.72 | convolution fusion | flops 1258782720 | bytes 4915200 | tf_op jit(solution)/shard_map/dot_general | solution.py:93
  51.9 4.8 %fusion.170 = (f32[2,512]{1,0:T(2,128)S(1)}, f32[2,512,1024]{2,1,0:T(8,128)}) fusion(pred[512,1024]{1,0:T(8,128)(4,1)S(1)} %get-tuple-element.25, bf16[1024,2,3,80]{0,3,2,1:T(8,128)(2,1)} %bitcast.112), kind=kOutput, calls=%fused_computation.280 | convolution fusion | flops 171967488 | bytes 5214208 | tf_op jit(solution)/shard_map/sub | solution.py:39
  56.6 3.7 %fusion.169 = (f32[2,512]{1,0:T(2,128)S(1)}, f32[2,512,1024]{2,1,0:T(8,128)}) fusion(pred[512,1024]{1,0:T(8,128)(4,1)S(1)} %get-tuple-element.26, bf16[1024,2,3,80]{0,3,2,1:T(8,128)(2,1)S(1)} %bitcast.113), kind=kOutput, calls=%fused_computation.279 | convolution fusion | flops 171967488 | bytes 5214208 | tf_op jit(solution)/shard_map/sub | solution.py:39
  60.3 3.3 %fusion.78 = bf16[2,80,512]{2,1,0:T(8,128)(2,1)S(1)} fusion(f32[2,512,1024]{2,1,0:T(8,128)} %get-tuple-element.32, f32[2,512]{1,0:T(2,128)S(1)} %get-tuple-element.31, bf16[1024,2,3,80]{0,3,2,1:T(8,128)(2,1)S(1)} %bitcast.114), kind=kOutput, calls=%fused_computation.105 | convolution fusion | flops 169951232 | bytes 4689920 | tf_op jit(solution)/shard_map/hqk,khd->qhd/dot_general | solution.py:41
  65.0 3.6 %collective-permute-start.2 = (bf16[128,160]{0,1:T(8,128)(2,1)S(1)}, bf16[128,160]{0,1:T(8,128)(2,1)S(1)}, u32[]{:S(2)}, u32[]{:S(2)}) collective-permute-start(bf16[128,160]{0,1:T(8,128)(2,1)S(1)} %get-tuple-element.19), channel_id=1, source_target_pairs={{0,3},{1,4},{2,5},{3,6},{4,7},{5,0},{6,1},{7,2},{8,11},{9,12},{10,... | collective-permute-start | bytes 122888 | tf_op jit(solution)/shard_map/ppermute | solution.py:105
  69.4 2.5 collective-permute-start.4
  72.8 1.5 all-gather.9.cloned.1.call-done
  74.3 1.4 fusion.31
  75.7 1.0 collective-permute-start.1
  76.8 1.3 fusion.30
  78.1 2.0 collective-permute-start.6
  80.1 1.3 fusion.18
  84.5 49.1 %all_to_all.21 = bf16[16,80,1280]{2,1,0:T(8,128)(2,1)} all-to-all(bf16[16,80,1280]{2,1,0:T(8,128)(2,1)S(1)} %broadcast_in_dim.177), channel_id=1, replica_groups=mesh['row'=16,'col'=8] {'row'}, dimensions={0} | all-to-all | bytes 6553600 | tf_op jit(solution)/shard_map/all_to_all | solution.py:49
  133.6 13.0 %convolution_convert_fusion = bf16[1024,1280]{1,0:T(8,128)(2,1)} fusion(bf16[1280,1280]{1,0:T(8,128)(2,1)} %bitcast.96, bf16[1024,1280]{1,0:T(8,128)(2,1)} %all-gather.11.cloned.1.call-done), kind=kOutput, calls=%fused_computation.14 | convolution fusion | flops 3399352320 | bytes 8519680 | tf_op jit(solution)/shard_map/dot_general | solution.py:117
  147.6 2.9 broadcast_in_dim.178
  150.5 4.7 %all-to-all-start.2 = ((bf16[16,320,512]{2,1,0:T(8,128)(2,1)}), bf16[16,320,512]{2,1,0:T(8,128)(2,1)}, u32[]{:S(2)}, u32[]{:S(2)}) async-start(bf16[16,320,512]{2,1,0:T(8,128)(2,1)} %broadcast_in_dim.178), calls=%async_computation.3 | async-start | bytes 10485760 | tf_op jit(solution)/shard_map/all_to_all | solution.py:49
  155.3 24.6 %reduce-scatter.2.cloned.1.call-done = bf16[128,1280]{1,0:T(8,128)(2,1)} async-done(((bf16[1024,1280]{1,0:T(8,128)(2,1)}), bf16[128,1280]{1,0:T(8,128)(2,1)}) %reduce-scatter.2.cloned.1.call-update) | async-done | bytes 327696 | tf_op jit(solution)/shard_map/reduce_scatter | solution.py:120
  179.8 1.1 convert_reduce_fusion.1
  187.0 42.8 %all-to-all-done.2 = bf16[16,320,512]{2,1,0:T(8,128)(2,1)} async-done(((bf16[16,320,512]{2,1,0:T(8,128)(2,1)}), bf16[16,320,512]{2,1,0:T(8,128)(2,1)}, u32[]{:S(2)}, u32[]{:S(2)}) %all-to-all-start.2) | async-done | bytes 5242912 | tf_op jit(solution)/shard_map/all_to_all | solution.py:49
  229.8 4.9 %fusion.92 = (f32[256]{0:T(256)S(1)}, f32[256]{0:T(256)S(1)}, bf16[256,512]{1,0:T(8,128)(2,1)S(1)}) fusion(bf16[256,5120]{1,0:T(8,128)(2,1)} %all-gather.13.cloned.1.call-done, bf16[5120,512]{1,0:T(8,128)(2,1)} %bitcast.19), kind=kOutput, calls=%fused_computation.149 | convolution fusion | flops 1342963200 | bytes 8128512 | tf_op jit(solution)/shard_map/dot_general | solution.py:128
  234.7 2.7 gather_fusion.1
  237.4 1.1 broadcast_select_fusion
  238.4 4.6 %all-to-all-start.3 = ((bf16[16,48,512]{2,1,0:T(8,128)(2,1)}), bf16[16,48,512]{2,1,0:T(8,128)(2,1)S(1)}, u32[]{:S(2)}, u32[]{:S(2)}) async-start(bf16[16,48,512]{2,1,0:T(8,128)(2,1)} %broadcast_select_fusion), calls=%async_computation.4 | async-start | bytes 1572864 | tf_op jit(solution)/shard_map/all_to_all | solution.py:148
  243.4 20.8 %all-reduce.1 = f32[128]{0:T(128)S(1)} all-reduce(f32[128]{0:T(128)S(1)} %maximum_dynamic-update-slice_fusion), channel_id=2, replica_groups=mesh['row'=16,'col'=8] {'col'}, use_global_device_ids=true, to_apply=%add.1 | all-reduce | flops 128 | bytes 1024
  264.5 40.1 %all-reduce.2 = f32[256]{0:T(256)S(1)} all-reduce(f32[256]{0:T(256)S(1)} %maximum_dynamic-update-slice_fusion.1), channel_id=3, replica_groups=mesh['row'=16,'col'=8] {'row'}, use_global_device_ids=true, to_apply=%add.2 | all-reduce | flops 256 | bytes 2048
  305.8 1.2 gather_fusion.4
  307.5 1.0 divide_convert_fusion.8
  (124 shorter events, 18.7 us)
Async XLA Ops:
  7.2 40.5 %all-gather.7.cloned.1.call-start = ((), (), s32[]{:S(2)}) async-start(), calls=%async_computation.5 | async-start | bytes 2949120 | tf_op jit(solution)/shard_map/all_gather | solution.py:92
  12.4 61.9 %all-gather.9.cloned.1.call-start = ((), (), s32[]{:S(2)}) async-start(), calls=%async_computation.6 | async-start | bytes 3686400 | tf_op jit(solution)/shard_map/all_gather | solution.py:98
  14.4 32.0 %copy-start.5 = (s32[16,8]{0,1:T(8,128)S(1)}, s32[16,8]{0,1:T(8,128)}, u32[]{:S(2)}) copy-start(s32[16,8]{0,1:T(8,128)} %param.13) | copy-start | bytes 1540
  46.1 87.5 %all-gather.11.cloned.1.call-start = ((), (), s32[]{:S(2)}) async-start(), calls=%async_computation.7 | async-start | bytes 2949120 | tf_op jit(solution)/shard_map/all_gather | solution.py:114
  51.9 4.8 %copy-start.10 = (bf16[1024,480]{0,1:T(8,128)(2,1)S(1)}, bf16[1024,480]{0,1:T(8,128)(2,1)}, u32[]{:S(2)}) copy-start(bf16[1024,480]{0,1:T(8,128)(2,1)} %convolution_convert_fusion.9) | copy-start | bytes 2949124
  60.3 3.6 %copy-start.13 = (f32[2,512,1024]{2,1,0:T(8,128)S(1)}, f32[2,512,1024]{2,1,0:T(8,128)}, u32[]{:S(2)}) copy-start(f32[2,512,1024]{2,1,0:T(8,128)} %get-tuple-element.30) | copy-start | bytes 12582916
  64.9 10.8 %collective-permute-start = (bf16[128,160]{0,1:T(8,128)(2,1)S(1)}, bf16[128,160]{0,1:T(8,128)(2,1)S(1)}, u32[]{:S(2)}, u32[]{:S(2)}) collective-permute-start(bf16[128,160]{0,1:T(8,128)(2,1)S(1)} %get-tuple-element.18), channel_id=1, source_target_pairs={{0,1},{1,2},{2,3},{3,4},{4,5},{5,6},{6,7},{7,0},{8,9},{9,10},{10,1... | collective-permute-start | bytes 122888 | tf_op jit(solution)/shard_map/ppermute | solution.py:105
  65.0 13.1 %collective-permute-start.2 = (bf16[128,160]{0,1:T(8,128)(2,1)S(1)}, bf16[128,160]{0,1:T(8,128)(2,1)S(1)}, u32[]{:S(2)}, u32[]{:S(2)}) collective-permute-start(bf16[128,160]{0,1:T(8,128)(2,1)S(1)} %get-tuple-element.19), channel_id=1, source_target_pairs={{0,3},{1,4},{2,5},{3,6},{4,7},{5,0},{6,1},{7,2},{8,11},{9,12},{10,... | collective-permute-start | bytes 122888 | tf_op jit(solution)/shard_map/ppermute | solution.py:105
  68.5 12.9 %collective-permute-start.3 = (bf16[128,160]{0,1:T(8,128)(2,1)S(1)}, bf16[128,160]{0,1:T(8,128)(2,1)S(1)}, u32[]{:S(2)}, u32[]{:S(2)}) collective-permute-start(bf16[128,160]{0,1:T(8,128)(2,1)S(1)} %get-tuple-element.20), channel_id=1, source_target_pairs={{0,4},{1,5},{2,6},{3,7},{4,0},{5,1},{6,2},{7,3},{8,12},{9,13},{10,... | collective-permute-start | bytes 122888 | tf_op jit(solution)/shard_map/ppermute | solution.py:105
  69.4 12.3 %collective-permute-start.4 = (bf16[128,160]{0,1:T(8,128)(2,1)S(1)}, bf16[128,160]{0,1:T(8,128)(2,1)S(1)}, u32[]{:S(2)}, u32[]{:S(2)}) collective-permute-start(bf16[128,160]{0,1:T(8,128)(2,1)S(1)} %get-tuple-element.21), channel_id=1, source_target_pairs={{0,5},{1,6},{2,7},{3,0},{4,1},{5,2},{6,3},{7,4},{8,13},{9,14},{10,... | collective-permute-start | bytes 122888 | tf_op jit(solution)/shard_map/ppermute | solution.py:105
  71.9 10.1 %collective-permute-start.5 = (bf16[128,160]{0,1:T(8,128)(2,1)S(1)}, bf16[128,160]{0,1:T(8,128)(2,1)S(1)}, u32[]{:S(2)}, u32[]{:S(2)}) collective-permute-start(bf16[128,160]{0,1:T(8,128)(2,1)S(1)} %get-tuple-element.22), channel_id=1, source_target_pairs={{0,6},{1,7},{2,0},{3,1},{4,2},{5,3},{6,4},{7,5},{8,14},{9,15},{10,... | collective-permute-start | bytes 122888 | tf_op jit(solution)/shard_map/ppermute | solution.py:105
  74.3 7.1 %copy-start.1 = (bf16[1280,1280]{1,0:T(8,128)(2,1)S(1)}, bf16[1280,1280]{1,0:T(8,128)(2,1)}, u32[]{:S(2)}) copy-start(bf16[1280,1280]{1,0:T(8,128)(2,1)} %all-gather.9.cloned.1.call-done) | copy-start | bytes 9830404
  75.7 6.8 %collective-permute-start.1 = (bf16[128,160]{0,1:T(8,128)(2,1)S(1)}, bf16[128,160]{0,1:T(8,128)(2,1)S(1)}, u32[]{:S(2)}, u32[]{:S(2)}) collective-permute-start(bf16[128,160]{0,1:T(8,128)(2,1)S(1)} %get-tuple-element.17), channel_id=1, source_target_pairs={{0,2},{1,3},{2,4},{3,5},{4,6},{5,7},{6,0},{7,1},{8,10},{9,11},{10,... | collective-permute-start | bytes 122888 | tf_op jit(solution)/shard_map/ppermute | solution.py:105
  78.1 4.5 %copy-start = (bf16[128,1280]{1,0:T(8,128)(2,1)S(1)}, bf16[128,1280]{1,0:T(8,128)(2,1)}, u32[]{:S(2)}) copy-start(bf16[128,1280]{1,0:T(8,128)(2,1)} %param.12) | copy-start | bytes 983044
  78.1 4.2 %collective-permute-start.6 = (bf16[128,160]{0,1:T(8,128)(2,1)S(1)}, bf16[128,160]{0,1:T(8,128)(2,1)S(1)}, u32[]{:S(2)}, u32[]{:S(2)}) collective-permute-start(bf16[128,160]{0,1:T(8,128)(2,1)S(1)} %fusion.109), channel_id=1, source_target_pairs={{0,7},{1,0},{2,1},{3,2},{4,3},{5,4},{6,5},{7,6},{8,15},{9,8},{10,9... | collective-permute-start | bytes 122888 | tf_op jit(solution)/shard_map/ppermute | solution.py:105
  82.5 1.8 copy-start.3
  82.5 1.8 copy-start.4
  84.2 95.6 %reduce-scatter.2.cloned.1.call-start = ((), (), s32[]{:S(2)}) async-start(), calls=%async_computation.8 | async-start | bytes 2949120 | tf_op jit(solution)/shard_map/reduce_scatter | solution.py:120
  146.6 1.0 copy-start.2
  150.5 30.7 %copy-start.6 = (f32[1280]{0:T(1024)S(1)}, f32[1280]{0:T(1024)}, u32[]{:S(2)}) copy-start(f32[1280]{0:T(1024)} %param.22) | copy-start | bytes 15364
  150.5 30.8 %copy-start.7 = (f32[1280]{0:T(1024)S(1)}, f32[1280]{0:T(1024)}, u32[]{:S(2)}) copy-start(f32[1280]{0:T(1024)} %param.21) | copy-start | bytes 15364
  150.5 79.3 %all-to-all-start.2 = ((bf16[16,320,512]{2,1,0:T(8,128)(2,1)}), bf16[16,320,512]{2,1,0:T(8,128)(2,1)}, u32[]{:S(2)}, u32[]{:S(2)}) async-start(bf16[16,320,512]{2,1,0:T(8,128)(2,1)} %broadcast_in_dim.178), calls=%async_computation.3 | async-start | bytes 10485760 | tf_op jit(solution)/shard_map/all_to_all | solution.py:49
  155.2 27.6 %copy-start.12 = (u32[128]{0:T(128)S(1)}, u32[128]{0:T(128)}, u32[]{:S(2)}) copy-start(u32[128]{0:T(128)} %constant.279) | copy-start | bytes 1540
  155.2 28.1 %copy-start.11 = (u32[128]{0:T(128)S(1)}, u32[128]{0:T(128)}, u32[]{:S(2)}) copy-start(u32[128]{0:T(128)} %constant.284) | copy-start | bytes 1540
  155.2 30.1 %copy-start.8 = (s32[128]{0:T(128)S(1)}, s32[128]{0:T(128)}, u32[]{:S(2)}) copy-start(s32[128]{0:T(128)} %param.14) | copy-start | bytes 1540
  155.2 74.5 %all-gather.13.cloned.1.call-start = ((), (), s32[]{:S(2)}) async-start(), calls=%async_computation.9 | async-start | bytes 2949120 | tf_op jit(solution)/shard_map/all_gather | solution.py:126
  238.4 68.5 %all-to-all-start.3 = ((bf16[16,48,512]{2,1,0:T(8,128)(2,1)}), bf16[16,48,512]{2,1,0:T(8,128)(2,1)S(1)}, u32[]{:S(2)}, u32[]{:S(2)}) async-start(bf16[16,48,512]{2,1,0:T(8,128)(2,1)} %broadcast_select_fusion), calls=%async_computation.4 | async-start | bytes 1572864 | tf_op jit(solution)/shard_map/all_to_all | solution.py:148
  305.5 3.0 copy-start.9
Sparse Core Ops, SparseCore 0:
  12.5 28.5 all-gather.6
  46.3 28.0 all-gather.8
  84.3 28.4 all-gather.10
  146.8 32.9 reduce-scatter.1
  182.6 24.7 all-gather.12

commit v5 on v3

--- a/solution.py
+++ b/solution.py
@@ -2,6 +2,7 @@
 import jax.numpy as jnp
 from jax import lax
 from jax.sharding import PartitionSpec as P
+
 
 D = 1280
 HEAD_DIM = 80
@@ -94,15 +95,18 @@
     qkv = qkv.astype(jnp.bfloat16).reshape(tok_row, -1, 3, HEAD_DIM)
     context = attend(qkv, segments)
     head_cols = context.shape[1]
-    pieces = lax.all_to_all(context.reshape(n_col, tok_dev, head_cols), "col", 0, 0, tiled=True)
+    col_index = lax.axis_index("col")
     out_all = lax.all_gather(out_t.T, "col", axis=0, tiled=True)
     attn_out = jnp.zeros((tok_dev, D), jnp.float32)
-    for c in range(n_col):
-        term = jnp.dot(
-            pieces[c],
-            out_all[c * head_cols : (c + 1) * head_cols],
-            preferred_element_type=jnp.float32,
-        )
+    for shift in range(n_col):
+        target = (col_index + shift) % n_col
+        block = lax.dynamic_slice_in_dim(context, target * tok_dev, tok_dev, 0)
+        if shift:
+            pairs = [(i, (i + shift) % n_col) for i in range(n_col)]
+            block = lax.ppermute(block, "col", pairs)
+        source = (col_index - shift) % n_col
+        rows = lax.dynamic_slice_in_dim(out_all, source * head_cols, head_cols, 0)
+        term = jnp.dot(block, rows, preferred_element_type=jnp.float32)
         attn_out = attn_out + term.astype(jnp.bfloat16).astype(jnp.float32)
     stream = (stream.astype(jnp.float32) + attn_out).astype(jnp.bfloat16)
     normed = layer_norm(stream.astype(jnp.float32), ln_gain[0, 1], ln_bias[0, 1]).astype(

time: 279 us -> 287 us (1.029)
  starting transfers between devices: 9.79 us -> 20 us
  blocking collectives: 106 us -> 102 us
    all_to_all x1 -> x0, blocking collectives: 14.5 us -> none  [local(): lax.all_to_all(context.reshape(n_col, tok_dev, head_cols), 'col', 0, 0, t...]
    ppermute x0 -> x7, starting transfers between devices: none -> 10.7 us  [local(): block = lax.ppermute(block, 'col', pairs)]
    unnamed x1, blocking collectives: 17.8 us -> 24.6 us
    all_to_all x2, blocking collectives: 74 us -> 77.7 us  [row_gather(): received = lax.all_to_all(send, 'row', 0, 0, tiled=True)]
  transfers between devices with their start and end apart: 7 -> 14, of which waited for: 3 -> 5; matrix products, arithmetic and copies ran while one was open for 10% -> 12% of each run, Pallas kernels for 0% -> 0%
where the time goes in v5:
time: 287 us; the launch traced here: 286 us
  blocking collectives  102 us (36%)
  waiting for transfers between devices  81.4 us (28%)
  matrix products  40 us (14%)
  starting transfers between devices  20 us (7%)
  between operations  15.2 us (5%)
  local copies, waits for them, and re-layouts  13.9 us (5%)
  other arithmetic  13 us (5%)
    all_to_all x2, blocking collectives, row_gather(): received = lax.all_to_all(send, 'row', 0, 0, tiled=True)  77.7 us
    all_to_all x1, waiting for transfers between devices, row_gather(): received = lax.all_to_all(send, 'row', 0, 0, tiled=True)  47.5 us
    unnamed x1, blocking collectives  24.6 us
    reduce_scatter x1, waiting for transfers between devices, local(): lax.psum_scatter(mlp_terms.astype(jnp.bfloat16), 'col', scatter_dimension...  23 us
    dot_general x1, matrix products, local(): lax.dot_general(hidden, down_t, contract_t, preferred_element_type=jnp.fl...  13 us
    ppermute x7, starting transfers between devices, local(): block = lax.ppermute(block, 'col', pairs)  10.7 us
    sub x2, matrix products, attend(): expo = jnp.exp(scores - peak)  8.43 us
    all_to_all x1, waiting for transfers between devices, local(): recv = lax.all_to_all(send, 'row', 0, 0, tiled=True)  8.42 us
  transfers between devices with their start and end apart: 14, of which 5 were waited for; matrix products, arithmetic and copies ran while one was open for 12% of the time, Pallas kernels for 0%

profile of v5, /device:TPU:1, one launch (start us, length us, event | category | flops | bytes accessed | tf_op | source)
XLA Modules:
  0.0 285.8 jit_solution(5875028441375833626)
XLA Ops:
  7.2 1.1 convert_reduce_fusion
  8.3 1.2 fusion.86
  10.4 2.0 fusion.89
  13.3 1.0 pad_maximum_fusion.1
  14.4 29.9 %all_to_all.20 = bf16[16,80,640]{2,1,0:T(8,128)(2,1)S(1)} all-to-all(bf16[16,80,640]{2,1,0:T(8,128)(2,1)S(1)} %broadcast_in_dim.155), channel_id=1, replica_groups=mesh['row'=16,'col'=8] {'row'}, dimensions={0} | all-to-all | bytes 3276800 | tf_op jit(solution)/shard_map/all_to_all | solution.py:50
  44.6 1.0 copy.47
  47.2 4.2 %convolution_convert_fusion.9 = bf16[1024,480]{0,1:T(8,128)(2,1)} fusion(bf16[1024,1280]{1,0:T(8,128)(2,1)} %all-gather.6.cloned.1.call-done, bf16[1280,640]{1,0:T(8,128)(2,1)S(1)} %bitcast.97), kind=kOutput, calls=%fused_computation.70 | convolution fusion | flops 1258782720 | bytes 4915200 | tf_op jit(solution)/shard_map/dot_general | solution.py:94
  51.3 4.8 %fusion.169 = (f32[2,512]{1,0:T(2,128)S(1)}, f32[2,512,1024]{2,1,0:T(8,128)}) fusion(pred[512,1024]{1,0:T(8,128)(4,1)S(1)} %get-tuple-element.21, bf16[1024,2,3,80]{0,3,2,1:T(8,128)(2,1)} %bitcast.111), kind=kOutput, calls=%fused_computation.274 | convolution fusion | flops 171967488 | bytes 5214208 | tf_op jit(solution)/shard_map/sub | solution.py:40
  56.1 3.7 %fusion.168 = (f32[2,512]{1,0:T(2,128)S(1)}, f32[2,512,1024]{2,1,0:T(8,128)}) fusion(pred[512,1024]{1,0:T(8,128)(4,1)S(1)} %get-tuple-element.22, bf16[1024,2,3,80]{0,3,2,1:T(8,128)(2,1)S(1)} %bitcast.112), kind=kOutput, calls=%fused_computation.273 | convolution fusion | flops 171967488 | bytes 5214208 | tf_op jit(solution)/shard_map/sub | solution.py:40
  59.8 3.2 %fusion.78 = bf16[2,80,512]{2,1,0:T(8,128)(2,1)S(1)} fusion(f32[2,512,1024]{2,1,0:T(8,128)} %get-tuple-element.28, f32[2,512]{1,0:T(2,128)S(1)} %get-tuple-element.27, bf16[1024,2,3,80]{0,3,2,1:T(8,128)(2,1)S(1)} %bitcast.113), kind=kOutput, calls=%fused_computation.103 | convolution fusion | flops 169951232 | bytes 4689920 | tf_op jit(solution)/shard_map/hqk,khd->qhd/dot_general | solution.py:42
  64.4 3.4 %collective-permute-start = (bf16[128,160]{0,1:T(8,128)(2,1)S(1)}, bf16[128,160]{0,1:T(8,128)(2,1)S(1)}, u32[]{:S(2)}, u32[]{:S(2)}) collective-permute-start(bf16[128,160]{0,1:T(8,128)(2,1)S(1)} %get-tuple-element.16), channel_id=1, source_target_pairs={{0,1},{1,2},{2,3},{3,4},{4,5},{5,6},{6,7},{7,0},{8,9},{9,10},{10,1... | collective-permute-start | bytes 122888 | tf_op jit(solution)/shard_map/ppermute | solution.py:106
  67.8 2.1 collective-permute-start.2
  69.9 1.2 collective-permute-start.3
  71.2 2.6 collective-permute-start.4
  73.8 1.6 all-gather.8.cloned.1.call-done
  75.4 1.4 fusion.31
  77.6 1.3 fusion.30
  79.5 1.3 fusion.18
  84.6 47.8 %all_to_all.21 = bf16[16,80,1280]{2,1,0:T(8,128)(2,1)} all-to-all(bf16[16,80,1280]{2,1,0:T(8,128)(2,1)S(1)} %broadcast_in_dim.159), channel_id=1, replica_groups=mesh['row'=16,'col'=8] {'row'}, dimensions={0} | all-to-all | bytes 6553600 | tf_op jit(solution)/shard_map/all_to_all | solution.py:50
  132.5 13.0 %convolution_convert_fusion = bf16[1024,1280]{1,0:T(8,128)(2,1)} fusion(bf16[1280,1280]{1,0:T(8,128)(2,1)} %bitcast.95, bf16[1024,1280]{1,0:T(8,128)(2,1)} %all-gather.10.cloned.1.call-done), kind=kOutput, calls=%fused_computation.12 | convolution fusion | flops 3399352320 | bytes 8519680 | tf_op jit(solution)/shard_map/dot_general | solution.py:118
  146.4 2.9 broadcast_in_dim.160
  149.3 4.7 %all-to-all-start.2 = ((bf16[16,320,512]{2,1,0:T(8,128)(2,1)}), bf16[16,320,512]{2,1,0:T(8,128)(2,1)}, u32[]{:S(2)}, u32[]{:S(2)}) async-start(bf16[16,320,512]{2,1,0:T(8,128)(2,1)} %broadcast_in_dim.160), calls=%async_computation.3 | async-start | bytes 10485760 | tf_op jit(solution)/shard_map/all_to_all | solution.py:50
  154.1 23.0 %reduce-scatter.2.cloned.1.call-done = bf16[128,1280]{1,0:T(8,128)(2,1)} async-done(((bf16[1024,1280]{1,0:T(8,128)(2,1)}), bf16[128,1280]{1,0:T(8,128)(2,1)}) %reduce-scatter.2.cloned.1.call-update) | async-done | bytes 327696 | tf_op jit(solution)/shard_map/reduce_scatter | solution.py:121
  177.1 1.1 convert_reduce_fusion.1
  180.3 47.5 %all-to-all-done.2 = bf16[16,320,512]{2,1,0:T(8,128)(2,1)} async-done(((bf16[16,320,512]{2,1,0:T(8,128)(2,1)}), bf16[16,320,512]{2,1,0:T(8,128)(2,1)}, u32[]{:S(2)}, u32[]{:S(2)}) %all-to-all-start.2) | async-done | bytes 5242912 | tf_op jit(solution)/shard_map/all_to_all | solution.py:50
  227.8 4.8 %convolution_convert_fusion.10 = bf16[256,512]{1,0:T(8,128)(2,1)S(1)} fusion(bf16[256,5120]{1,0:T(8,128)(2,1)} %all-gather.12.cloned.1.call-done, bf16[5120,512]{1,0:T(8,128)(2,1)} %bitcast.19), kind=kOutput, calls=%fused_computation.102 | convolution fusion | flops 1342308352 | bytes 8126464 | tf_op jit(solution)/shard_map/dot_general | solution.py:129
  232.6 2.7 gather_fusion.1
  235.3 1.1 broadcast_select_fusion
  236.4 4.3 %all-to-all-start.3 = ((bf16[16,48,512]{2,1,0:T(8,128)(2,1)}), bf16[16,48,512]{2,1,0:T(8,128)(2,1)S(1)}, u32[]{:S(2)}, u32[]{:S(2)}) async-start(bf16[16,48,512]{2,1,0:T(8,128)(2,1)} %broadcast_select_fusion), calls=%async_computation.4 | async-start | bytes 1572864 | tf_op jit(solution)/shard_map/all_to_all | solution.py:149
  243.2 8.4 %all-to-all-done.3 = bf16[16,48,512]{2,1,0:T(8,128)(2,1)S(1)} async-done(((bf16[16,48,512]{2,1,0:T(8,128)(2,1)}), bf16[16,48,512]{2,1,0:T(8,128)(2,1)S(1)}, u32[]{:S(2)}, u32[]{:S(2)}) %all-to-all-start.3) | async-done | bytes 786464 | tf_op jit(solution)/shard_map/all_to_all | solution.py:149
  252.8 24.6 %all-reduce.1 = f32[128]{0:T(128)S(1)} all-reduce(f32[128]{0:T(128)S(1)} %maximum_dynamic-update-slice_fusion), channel_id=2, replica_groups=mesh['row'=16,'col'=8] {'col'}, use_global_device_ids=true, to_apply=%add.1 | all-reduce | flops 128 | bytes 1024
  278.3 1.0 divide_convert_fusion.8
  (111 shorter events, 16.8 us)
Async XLA Ops:
  7.2 40.0 %all-gather.6.cloned.1.call-start = ((), (), s32[]{:S(2)}) async-start(), calls=%async_computation.5 | async-start | bytes 2949120 | tf_op jit(solution)/shard_map/all_gather | solution.py:93
  12.4 63.0 %all-gather.8.cloned.1.call-start = ((), (), s32[]{:S(2)}) async-start(), calls=%async_computation.6 | async-start | bytes 3686400 | tf_op jit(solution)/shard_map/all_gather | solution.py:99
  14.4 31.5 %copy-start.5 = (s32[16,8]{0,1:T(8,128)S(1)}, s32[16,8]{0,1:T(8,128)}, u32[]{:S(2)}) copy-start(s32[16,8]{0,1:T(8,128)} %param.13) | copy-start | bytes 1540
  45.6 86.8 %all-gather.10.cloned.1.call-start = ((), (), s32[]{:S(2)}) async-start(), calls=%async_computation.7 | async-start | bytes 2949120 | tf_op jit(solution)/shard_map/all_gather | solution.py:115
  51.3 4.8 %copy-start.10 = (bf16[1024,480]{0,1:T(8,128)(2,1)S(1)}, bf16[1024,480]{0,1:T(8,128)(2,1)}, u32[]{:S(2)}) copy-start(bf16[1024,480]{0,1:T(8,128)(2,1)} %convolution_convert_fusion.9) | copy-start | bytes 2949124
  59.8 3.6 %copy-start.12 = (f32[2,512,1024]{2,1,0:T(8,128)S(1)}, f32[2,512,1024]{2,1,0:T(8,128)}, u32[]{:S(2)}) copy-start(f32[2,512,1024]{2,1,0:T(8,128)} %get-tuple-element.26) | copy-start | bytes 12582916
  64.4 12.5 %collective-permute-start = (bf16[128,160]{0,1:T(8,128)(2,1)S(1)}, bf16[128,160]{0,1:T(8,128)(2,1)S(1)}, u32[]{:S(2)}, u32[]{:S(2)}) collective-permute-start(bf16[128,160]{0,1:T(8,128)(2,1)S(1)} %get-tuple-element.16), channel_id=1, source_target_pairs={{0,1},{1,2},{2,3},{3,4},{4,5},{5,6},{6,7},{7,0},{8,9},{9,10},{10,1... | collective-permute-start | bytes 122888 | tf_op jit(solution)/shard_map/ppermute | solution.py:106
  67.8 11.1 %collective-permute-start.2 = (bf16[128,160]{0,1:T(8,128)(2,1)S(1)}, bf16[128,160]{0,1:T(8,128)(2,1)S(1)}, u32[]{:S(2)}, u32[]{:S(2)}) collective-permute-start(bf16[128,160]{0,1:T(8,128)(2,1)S(1)} %get-tuple-element.17), channel_id=1, source_target_pairs={{0,3},{1,4},{2,5},{3,6},{4,7},{5,0},{6,1},{7,2},{8,11},{9,12},{10,... | collective-permute-start | bytes 122888 | tf_op jit(solution)/shard_map/ppermute | solution.py:106
  69.9 10.8 %collective-permute-start.3 = (bf16[128,160]{0,1:T(8,128)(2,1)S(1)}, bf16[128,160]{0,1:T(8,128)(2,1)S(1)}, u32[]{:S(2)}, u32[]{:S(2)}) collective-permute-start(bf16[128,160]{0,1:T(8,128)(2,1)S(1)} %get-tuple-element.18), channel_id=1, source_target_pairs={{0,4},{1,5},{2,6},{3,7},{4,0},{5,1},{6,2},{7,3},{8,12},{9,13},{10,... | collective-permute-start | bytes 122888 | tf_op jit(solution)/shard_map/ppermute | solution.py:106
  71.2 9.9 %collective-permute-start.4 = (bf16[128,160]{0,1:T(8,128)(2,1)S(1)}, bf16[128,160]{0,1:T(8,128)(2,1)S(1)}, u32[]{:S(2)}, u32[]{:S(2)}) collective-permute-start(bf16[128,160]{0,1:T(8,128)(2,1)S(1)} %get-tuple-element.19), channel_id=1, source_target_pairs={{0,5},{1,6},{2,7},{3,0},{4,1},{5,2},{6,3},{7,4},{8,13},{9,14},{10,... | collective-permute-start | bytes 122888 | tf_op jit(solution)/shard_map/ppermute | solution.py:106
  73.8 7.6 %collective-permute-start.5 = (bf16[128,160]{0,1:T(8,128)(2,1)S(1)}, bf16[128,160]{0,1:T(8,128)(2,1)S(1)}, u32[]{:S(2)}, u32[]{:S(2)}) collective-permute-start(bf16[128,160]{0,1:T(8,128)(2,1)S(1)} %get-tuple-element.20), channel_id=1, source_target_pairs={{0,6},{1,7},{2,0},{3,1},{4,2},{5,3},{6,4},{7,5},{8,14},{9,15},{10,... | collective-permute-start | bytes 122888 | tf_op jit(solution)/shard_map/ppermute | solution.py:106
  75.4 5.3 %copy-start.1 = (bf16[1280,1280]{1,0:T(8,128)(2,1)S(1)}, bf16[1280,1280]{1,0:T(8,128)(2,1)}, u32[]{:S(2)}) copy-start(bf16[1280,1280]{1,0:T(8,128)(2,1)} %all-gather.8.cloned.1.call-done) | copy-start | bytes 9830404
  76.9 5.8 %collective-permute-start.1 = (bf16[128,160]{0,1:T(8,128)(2,1)S(1)}, bf16[128,160]{0,1:T(8,128)(2,1)S(1)}, u32[]{:S(2)}, u32[]{:S(2)}) collective-permute-start(bf16[128,160]{0,1:T(8,128)(2,1)S(1)} %get-tuple-element.15), channel_id=1, source_target_pairs={{0,2},{1,3},{2,4},{3,5},{4,6},{5,7},{6,0},{7,1},{8,10},{9,11},{10,... | collective-permute-start | bytes 122888 | tf_op jit(solution)/shard_map/ppermute | solution.py:106
  78.9 3.8 %copy-start = (bf16[128,1280]{1,0:T(8,128)(2,1)S(1)}, bf16[128,1280]{1,0:T(8,128)(2,1)}, u32[]{:S(2)}) copy-start(bf16[128,1280]{1,0:T(8,128)(2,1)} %param.12) | copy-start | bytes 983044
  78.9 3.4 %collective-permute-start.6 = (bf16[128,160]{0,1:T(8,128)(2,1)S(1)}, bf16[128,160]{0,1:T(8,128)(2,1)S(1)}, u32[]{:S(2)}, u32[]{:S(2)}) collective-permute-start(bf16[128,160]{0,1:T(8,128)(2,1)S(1)} %fusion.109), channel_id=1, source_target_pairs={{0,7},{1,0},{2,1},{3,2},{4,3},{5,4},{6,5},{7,6},{8,15},{9,8},{10,9... | collective-permute-start | bytes 122888 | tf_op jit(solution)/shard_map/ppermute | solution.py:106
  82.6 1.8 copy-start.3
  82.6 1.8 copy-start.4
  84.3 92.8 %reduce-scatter.2.cloned.1.call-start = ((), (), s32[]{:S(2)}) async-start(), calls=%async_computation.8 | async-start | bytes 2949120 | tf_op jit(solution)/shard_map/reduce_scatter | solution.py:121
  145.5 1.0 copy-start.2
  149.3 29.2 %copy-start.6 = (f32[1280]{0:T(1024)S(1)}, f32[1280]{0:T(1024)}, u32[]{:S(2)}) copy-start(f32[1280]{0:T(1024)} %param.22) | copy-start | bytes 15364
  149.3 29.2 %copy-start.7 = (f32[1280]{0:T(1024)S(1)}, f32[1280]{0:T(1024)}, u32[]{:S(2)}) copy-start(f32[1280]{0:T(1024)} %param.21) | copy-start | bytes 15364
  149.3 78.5 %all-to-all-start.2 = ((bf16[16,320,512]{2,1,0:T(8,128)(2,1)}), bf16[16,320,512]{2,1,0:T(8,128)(2,1)}, u32[]{:S(2)}, u32[]{:S(2)}) async-start(bf16[16,320,512]{2,1,0:T(8,128)(2,1)} %broadcast_in_dim.160), calls=%async_computation.3 | async-start | bytes 10485760 | tf_op jit(solution)/shard_map/all_to_all | solution.py:50
  154.0 25.7 %copy-start.8 = (s32[128]{0:T(128)S(1)}, s32[128]{0:T(128)}, u32[]{:S(2)}) copy-start(s32[128]{0:T(128)} %param.14) | copy-start | bytes 1540
  154.0 73.8 %all-gather.12.cloned.1.call-start = ((), (), s32[]{:S(2)}) async-start(), calls=%async_computation.9 | async-start | bytes 2949120 | tf_op jit(solution)/shard_map/all_gather | solution.py:127
  235.3 6.7 %copy-start.11 = (u32[128]{0:T(128)S(1)}, u32[128]{0:T(128)}, u32[]{:S(2)}) copy-start(u32[128]{0:T(128)} %constant.276) | copy-start | bytes 1540
  236.4 15.3 %all-to-all-start.3 = ((bf16[16,48,512]{2,1,0:T(8,128)(2,1)}), bf16[16,48,512]{2,1,0:T(8,128)(2,1)S(1)}, u32[]{:S(2)}, u32[]{:S(2)}) async-start(bf16[16,48,512]{2,1,0:T(8,128)(2,1)} %broadcast_select_fusion), calls=%async_computation.4 | async-start | bytes 1572864 | tf_op jit(solution)/shard_map/all_to_all | solution.py:149
  278.1 1.1 copy-start.9
Sparse Core Ops, SparseCore 0:
  12.5 29.6 all-gather.5
  45.7 29.6 all-gather.7
  84.5 29.4 all-gather.9
  145.6 31.4 reduce-scatter.1
  179.8 28.5 all-gather.11

commit v6 on v5

--- a/solution.py
+++ b/solution.py
@@ -118,9 +118,21 @@
     mlp_terms = lax.dot_general(
         hidden, down_t, contract_t, preferred_element_type=jnp.float32
     )
-    mlp_out = lax.psum_scatter(
-        mlp_terms.astype(jnp.bfloat16), "col", scatter_dimension=0, tiled=True
+    mlp_terms = mlp_terms.astype(jnp.bfloat16)
+    split = D // 2
+    head_sum = lax.psum_scatter(
+        mlp_terms[:, :split], "col", scatter_dimension=0, tiled=True
     ).astype(jnp.float32)
+    tail_terms = mlp_terms[:, split:]
+    tail_sum = jnp.zeros((tok_dev, D - split), jnp.float32)
+    for shift in range(n_col):
+        target = (col_index + shift) % n_col
+        block = lax.dynamic_slice_in_dim(tail_terms, target * tok_dev, tok_dev, 0)
+        if shift:
+            pairs = [(i, (i + shift) % n_col) for i in range(n_col)]
+            block = lax.ppermute(block, "col", pairs)
+        tail_sum = tail_sum + block.astype(jnp.float32)
+    mlp_out = jnp.concatenate([head_sum, tail_sum], axis=1)
     stream = (stream.astype(jnp.float32) + mlp_out).astype(jnp.bfloat16)
     merged = layer_norm(stream.astype(jnp.float32), merge_gain, merge_bias).astype(jnp.bfloat16)
     merged = merged.reshape(tok_dev // 4, 4 * D)

time: 287 us -> 302 us (1.052)
  starting transfers between devices: 20 us -> 30.2 us
  blocking collectives: 102 us -> 93 us
  waiting for transfers between devices: 81.4 us -> 89.7 us
  local copies, waits for them, and re-layouts: 13.9 us -> 17.5 us
    all_to_all x1, waiting for transfers between devices: 47.5 us -> 63.8 us  [row_gather(): received = lax.all_to_all(send, 'row', 0, 0, tiled=True)]
    reduce_scatter x1, waiting for transfers between devices: 23 us -> 7.31 us  [local(): lax.psum_scatter(mlp_terms[:, :split], 'col', scatter_dimension=0, tiled=...]
    ppermute x7 -> x14, starting transfers between devices: 10.7 us -> 20.1 us  [local(): block = lax.ppermute(block, 'col', pairs)]
    unnamed x1, blocking collectives: 24.6 us -> 15.9 us
    ppermute x7 -> x14, waiting for transfers between devices: 0.76 us -> 8.33 us  [local(): block = lax.ppermute(block, 'col', pairs)]
  transfers between devices with their start and end apart: 14 -> 21, of which waited for: 5 -> 8; matrix products, arithmetic and copies ran while one was open for 12% -> 12% of each run, Pallas kernels for 0% -> 0%
where the time goes in v6:
time: 302 us; the launch traced here: 301 us
  blocking collectives  93 us (31%)
  waiting for transfers between devices  89.7 us (30%)
  matrix products  41.1 us (14%)
  starting transfers between devices  30.2 us (10%)
  local copies, waits for them, and re-layouts  17.5 us (6%)
  between operations  15.2 us (5%)
  other arithmetic  14.1 us (5%)
    all_to_all x2, blocking collectives, row_gather(): received = lax.all_to_all(send, 'row', 0, 0, tiled=True)  77.1 us
    all_to_all x1, waiting for transfers between devices, row_gather(): received = lax.all_to_all(send, 'row', 0, 0, tiled=True)  63.8 us
    ppermute x14, starting transfers between devices, local(): block = lax.ppermute(block, 'col', pairs)  20.1 us
    unnamed x1, blocking collectives  15.9 us
    dot_general x1, matrix products, local(): lax.dot_general(hidden, down_t, contract_t, preferred_element_type=jnp.fl...  13 us
    all_to_all x1, waiting for transfers between devices, local(): recv = lax.all_to_all(send, 'row', 0, 0, tiled=True)  10.1 us
    sub x2, matrix products, attend(): expo = jnp.exp(scores - peak)  8.43 us
    ppermute x14, waiting for transfers between devices, local(): block = lax.ppermute(block, 'col', pairs)  8.33 us
  transfers between devices with their start and end apart: 21, of which 8 were waited for; matrix products, arithmetic and copies ran while one was open for 12% of the time, Pallas kernels for 0%

profile of v6, /device:TPU:1, one launch (start us, length us, event | category | flops | bytes accessed | tf_op | source)
XLA Modules:
  0.0 300.8 jit_solution(2069461289175335523)
XLA Ops:
  10.4 2.0 fusion.89
  14.4 29.9 %all_to_all.20 = bf16[16,80,640]{2,1,0:T(8,128)(2,1)S(1)} all-to-all(bf16[16,80,640]{2,1,0:T(8,128)(2,1)S(1)} %broadcast_in_dim.155), channel_id=1, replica_groups=mesh['row'=16,'col'=8] {'row'}, dimensions={0} | all-to-all | bytes 3276800 | tf_op jit(solution)/shard_map/all_to_all | solution.py:50
  47.2 4.2 %convolution_convert_fusion.9 = bf16[1024,480]{0,1:T(8,128)(2,1)} fusion(bf16[1024,1280]{1,0:T(8,128)(2,1)} %all-gather.6.cloned.1.call-done, bf16[1280,640]{1,0:T(8,128)(2,1)S(1)} %bitcast.97), kind=kOutput, calls=%fused_computation.70 | convolution fusion | flops 1258782720 | bytes 4915200 | tf_op jit(solution)/shard_map/dot_general | solution.py:94
  51.4 4.8 %fusion.172 = (f32[2,512]{1,0:T(2,128)S(1)}, f32[2,512,1024]{2,1,0:T(8,128)}) fusion(pred[512,1024]{1,0:T(8,128)(4,1)S(1)} %get-tuple-element.30, bf16[1024,2,3,80]{0,3,2,1:T(8,128)(2,1)} %bitcast.111), kind=kOutput, calls=%fused_computation.284 | convolution fusion | flops 171967488 | bytes 5214208 | tf_op jit(solution)/shard_map/sub | solution.py:40
  56.2 3.6 %fusion.171 = (f32[2,512]{1,0:T(2,128)S(1)}, f32[2,512,1024]{2,1,0:T(8,128)}) fusion(pred[512,1024]{1,0:T(8,128)(4,1)S(1)} %get-tuple-element.31, bf16[1024,2,3,80]{0,3,2,1:T(8,128)(2,1)S(1)} %bitcast.114), kind=kOutput, calls=%fused_computation.283 | convolution fusion | flops 171967488 | bytes 5214208 | tf_op jit(solution)/shard_map/sub | solution.py:40
  59.8 3.3 %fusion.78 = bf16[2,80,512]{2,1,0:T(8,128)(2,1)S(1)} fusion(f32[2,512,1024]{2,1,0:T(8,128)} %get-tuple-element.37, f32[2,512]{1,0:T(2,128)S(1)} %get-tuple-element.36, bf16[1024,2,3,80]{0,3,2,1:T(8,128)(2,1)} %bitcast.112), kind=kOutput, calls=%fused_computation.103 | convolution fusion | flops 169951232 | bytes 4689920 | tf_op jit(solution)/shard_map/hqk,khd->qhd/dot_general | solution.py:42
  63.5 1.8 fusion.79
  65.5 3.4 %collective-permute-start = (bf16[128,160]{0,1:T(8,128)(2,1)S(1)}, bf16[128,160]{0,1:T(8,128)(2,1)S(1)}, u32[]{:S(2)}, u32[]{:S(2)}) collective-permute-start(bf16[128,160]{0,1:T(8,128)(2,1)S(1)} %get-tuple-element.25), channel_id=1, source_target_pairs={{0,1},{1,2},{2,3},{3,4},{4,5},{5,6},{6,7},{7,0},{8,9},{9,10},{10,1... | collective-permute-start | bytes 122888 | tf_op jit(solution)/shard_map/ppermute | solution.py:106
  68.9 2.2 collective-permute-start.2
  71.0 1.2 collective-permute-start.3
  72.3 2.6 collective-permute-start.4
  75.0 1.4 fusion.31
  76.4 1.7 collective-permute-start.1
  78.1 1.3 fusion.30
  79.5 1.3 fusion.18
  81.6 1.2 collective-permute-done.6
  85.2 47.2 %all_to_all.21 = bf16[16,80,1280]{2,1,0:T(8,128)(2,1)} all-to-all(bf16[16,80,1280]{2,1,0:T(8,128)(2,1)S(1)} %broadcast_in_dim.159), channel_id=1, replica_groups=mesh['row'=16,'col'=8] {'row'}, dimensions={0} | all-to-all | bytes 6553600 | tf_op jit(solution)/shard_map/all_to_all | solution.py:50
  132.3 13.0 %convolution_convert_fusion = bf16[1024,1280]{1,0:T(8,128)(2,1)} fusion(bf16[1280,1280]{1,0:T(8,128)(2,1)} %bitcast.95, bf16[1024,1280]{1,0:T(8,128)(2,1)} %all-gather.10.cloned.1.call-done), kind=kOutput, calls=%fused_computation.12 | convolution fusion | flops 3399352320 | bytes 8519680 | tf_op jit(solution)/shard_map/dot_general | solution.py:118
  145.3 3.0 %fusion.169 = (bf16[1024,640]{1,0:T(8,128)(2,1)}, bf16[1024,640]{1,0:T(8,128)(2,1)S(1)}) fusion(bf16[1024,1280]{1,0:T(8,128)(2,1)} %convolution_convert_fusion), kind=kLoop, calls=%fused_computation.281 | loop fusion | bytes 5242880 | tf_op jit(solution)/shard_map/slice | solution.py:124
  149.3 3.4 %collective-permute-start.10 = (bf16[128,640]{1,0:T(8,128)(2,1)S(1)}, bf16[128,640]{1,0:T(8,128)(2,1)S(1)}, u32[]{:S(2)}, u32[]{:S(2)}) collective-permute-start(bf16[128,640]{1,0:T(8,128)(2,1)S(1)} %get-tuple-element.21), channel_id=1, source_target_pairs={{0,4},{1,5},{2,6},{3,7},{4,0},{5,1},{6,2},{7,3},{8,12},{9,13},{10,... | collective-permute-start | bytes 491528 | tf_op jit(solution)/shard_map/ppermute | solution.py:133
  152.7 1.4 collective-permute-start.11
  155.3 1.7 collective-permute-start.13
  158.1 5.9 %collective-permute-done.11 = bf16[128,640]{1,0:T(8,128)(2,1)S(1)} collective-permute-done((bf16[128,640]{1,0:T(8,128)(2,1)S(1)}, bf16[128,640]{1,0:T(8,128)(2,1)S(1)}, u32[]{:S(2)}, u32[]{:S(2)}) %collective-permute-start.11) | collective-permute-done | bytes 163872 | tf_op jit(solution)/shard_map/ppermute | solution.py:133
  164.1 2.9 broadcast_in_dim.160
  166.9 4.6 %all-to-all-start.2 = ((bf16[16,320,512]{2,1,0:T(8,128)(2,1)}), bf16[16,320,512]{2,1,0:T(8,128)(2,1)}, u32[]{:S(2)}, u32[]{:S(2)}) async-start(bf16[16,320,512]{2,1,0:T(8,128)(2,1)} %broadcast_in_dim.160), calls=%async_computation.3 | async-start | bytes 10485760 | tf_op jit(solution)/shard_map/all_to_all | solution.py:50
  174.8 7.3 %reduce-scatter.2.cloned.1.call-done = bf16[128,640]{1,0:T(8,128)(2,1)} async-done(((bf16[1024,640]{1,0:T(8,128)(2,1)}), bf16[128,640]{1,0:T(8,128)(2,1)}) %reduce-scatter.2.cloned.1.call-update) | async-done | bytes 163856 | tf_op jit(solution)/shard_map/reduce_scatter | solution.py:123
  185.3 63.8 %all-to-all-done.2 = bf16[16,320,512]{2,1,0:T(8,128)(2,1)} async-done(((bf16[16,320,512]{2,1,0:T(8,128)(2,1)}), bf16[16,320,512]{2,1,0:T(8,128)(2,1)}, u32[]{:S(2)}, u32[]{:S(2)}) %all-to-all-start.2) | async-done | bytes 5242912 | tf_op jit(solution)/shard_map/all_to_all | solution.py:50
  249.1 4.8 %convolution_convert_fusion.10 = bf16[256,512]{1,0:T(8,128)(2,1)S(1)} fusion(bf16[256,5120]{1,0:T(8,128)(2,1)} %all-gather.12.cloned.1.call-done, bf16[5120,512]{1,0:T(8,128)(2,1)} %bitcast.19), kind=kOutput, calls=%fused_computation.102 | convolution fusion | flops 1342308352 | bytes 8126464 | tf_op jit(solution)/shard_map/dot_general | solution.py:141
  253.9 2.7 gather_fusion.1
  257.7 5.1 %all-to-all-start.3 = ((bf16[16,48,512]{2,1,0:T(8,128)(2,1)}), bf16[16,48,512]{2,1,0:T(8,128)(2,1)S(1)}, u32[]{:S(2)}, u32[]{:S(2)}) async-start(bf16[16,48,512]{2,1,0:T(8,128)(2,1)} %broadcast_select_fusion), calls=%async_computation.4 | async-start | bytes 1572864 | tf_op jit(solution)/shard_map/all_to_all | solution.py:161
  265.3 10.1 %all-to-all-done.3 = bf16[16,48,512]{2,1,0:T(8,128)(2,1)S(1)} async-done(((bf16[16,48,512]{2,1,0:T(8,128)(2,1)}), bf16[16,48,512]{2,1,0:T(8,128)(2,1)S(1)}, u32[]{:S(2)}, u32[]{:S(2)}) %all-to-all-start.3) | async-done | bytes 786464 | tf_op jit(solution)/shard_map/all_to_all | solution.py:161
  276.5 15.9 %all-reduce.1 = f32[128]{0:T(128)S(1)} all-reduce(f32[128]{0:T(128)S(1)} %maximum_dynamic-update-slice_fusion), channel_id=2, replica_groups=mesh['row'=16,'col'=8] {'col'}, use_global_device_ids=true, to_apply=%add.1 | all-reduce | flops 128 | bytes 1024
  (131 shorter events, 26.9 us)
Async XLA Ops:
  7.2 40.0 %all-gather.6.cloned.1.call-start = ((), (), s32[]{:S(2)}) async-start(), calls=%async_computation.5 | async-start | bytes 2949120 | tf_op jit(solution)/shard_map/all_gather | solution.py:93
  12.4 62.6 %all-gather.8.cloned.1.call-start = ((), (), s32[]{:S(2)}) async-start(), calls=%async_computation.6 | async-start | bytes 3686400 | tf_op jit(solution)/shard_map/all_gather | solution.py:99
  14.4 31.5 %copy-start.6 = (s32[16,8]{0,1:T(8,128)S(1)}, s32[16,8]{0,1:T(8,128)}, u32[]{:S(2)}) copy-start(s32[16,8]{0,1:T(8,128)} %param.13) | copy-start | bytes 1540
  45.6 86.7 %all-gather.10.cloned.1.call-start = ((), (), s32[]{:S(2)}) async-start(), calls=%async_computation.7 | async-start | bytes 2949120 | tf_op jit(solution)/shard_map/all_gather | solution.py:115
  51.4 4.8 %copy-start.11 = (bf16[1024,480]{0,1:T(8,128)(2,1)S(1)}, bf16[1024,480]{0,1:T(8,128)(2,1)}, u32[]{:S(2)}) copy-start(bf16[1024,480]{0,1:T(8,128)(2,1)} %convolution_convert_fusion.9) | copy-start | bytes 2949124
  59.8 3.7 %copy-start.13 = (f32[2,512,1024]{2,1,0:T(8,128)S(1)}, f32[2,512,1024]{2,1,0:T(8,128)}, u32[]{:S(2)}) copy-start(f32[2,512,1024]{2,1,0:T(8,128)} %get-tuple-element.35) | copy-start | bytes 12582916
  65.5 11.0 %collective-permute-start = (bf16[128,160]{0,1:T(8,128)(2,1)S(1)}, bf16[128,160]{0,1:T(8,128)(2,1)S(1)}, u32[]{:S(2)}, u32[]{:S(2)}) collective-permute-start(bf16[128,160]{0,1:T(8,128)(2,1)S(1)} %get-tuple-element.25), channel_id=1, source_target_pairs={{0,1},{1,2},{2,3},{3,4},{4,5},{5,6},{6,7},{7,0},{8,9},{9,10},{10,1... | collective-permute-start | bytes 122888 | tf_op jit(solution)/shard_map/ppermute | solution.py:106
  68.9 10.5 %collective-permute-start.2 = (bf16[128,160]{0,1:T(8,128)(2,1)S(1)}, bf16[128,160]{0,1:T(8,128)(2,1)S(1)}, u32[]{:S(2)}, u32[]{:S(2)}) collective-permute-start(bf16[128,160]{0,1:T(8,128)(2,1)S(1)} %get-tuple-element.26), channel_id=1, source_target_pairs={{0,3},{1,4},{2,5},{3,6},{4,7},{5,0},{6,1},{7,2},{8,11},{9,12},{10,... | collective-permute-start | bytes 122888 | tf_op jit(solution)/shard_map/ppermute | solution.py:106
  71.0 9.7 %collective-permute-start.3 = (bf16[128,160]{0,1:T(8,128)(2,1)S(1)}, bf16[128,160]{0,1:T(8,128)(2,1)S(1)}, u32[]{:S(2)}, u32[]{:S(2)}) collective-permute-start(bf16[128,160]{0,1:T(8,128)(2,1)S(1)} %get-tuple-element.27), channel_id=1, source_target_pairs={{0,4},{1,5},{2,6},{3,7},{4,0},{5,1},{6,2},{7,3},{8,12},{9,13},{10,... | collective-permute-start | bytes 122888 | tf_op jit(solution)/shard_map/ppermute | solution.py:106
  72.3 8.8 %collective-permute-start.4 = (bf16[128,160]{0,1:T(8,128)(2,1)S(1)}, bf16[128,160]{0,1:T(8,128)(2,1)S(1)}, u32[]{:S(2)}, u32[]{:S(2)}) collective-permute-start(bf16[128,160]{0,1:T(8,128)(2,1)S(1)} %get-tuple-element.28), channel_id=1, source_target_pairs={{0,5},{1,6},{2,7},{3,0},{4,1},{5,2},{6,3},{7,4},{8,13},{9,14},{10,... | collective-permute-start | bytes 122888 | tf_op jit(solution)/shard_map/ppermute | solution.py:106
  74.9 6.5 %collective-permute-start.5 = (bf16[128,160]{0,1:T(8,128)(2,1)S(1)}, bf16[128,160]{0,1:T(8,128)(2,1)S(1)}, u32[]{:S(2)}, u32[]{:S(2)}) collective-permute-start(bf16[128,160]{0,1:T(8,128)(2,1)S(1)} %get-tuple-element.29), channel_id=1, source_target_pairs={{0,6},{1,7},{2,0},{3,1},{4,2},{5,3},{6,4},{7,5},{8,14},{9,15},{10,... | collective-permute-start | bytes 122888 | tf_op jit(solution)/shard_map/ppermute | solution.py:106
  75.0 5.8 %copy-start.1 = (bf16[1280,1280]{1,0:T(8,128)(2,1)S(1)}, bf16[1280,1280]{1,0:T(8,128)(2,1)}, u32[]{:S(2)}) copy-start(bf16[1280,1280]{1,0:T(8,128)(2,1)} %all-gather.8.cloned.1.call-done) | copy-start | bytes 9830404
  76.4 6.7 %collective-permute-start.1 = (bf16[128,160]{0,1:T(8,128)(2,1)S(1)}, bf16[128,160]{0,1:T(8,128)(2,1)S(1)}, u32[]{:S(2)}, u32[]{:S(2)}) collective-permute-start(bf16[128,160]{0,1:T(8,128)(2,1)S(1)} %get-tuple-element.24), channel_id=1, source_target_pairs={{0,2},{1,3},{2,4},{3,5},{4,6},{5,7},{6,0},{7,1},{8,10},{9,11},{10,... | collective-permute-start | bytes 122888 | tf_op jit(solution)/shard_map/ppermute | solution.py:106
  79.4 3.8 %copy-start = (bf16[128,1280]{1,0:T(8,128)(2,1)S(1)}, bf16[128,1280]{1,0:T(8,128)(2,1)}, u32[]{:S(2)}) copy-start(bf16[128,1280]{1,0:T(8,128)(2,1)} %param.12) | copy-start | bytes 983044
  79.4 3.4 %collective-permute-start.6 = (bf16[128,160]{0,1:T(8,128)(2,1)S(1)}, bf16[128,160]{0,1:T(8,128)(2,1)S(1)}, u32[]{:S(2)}, u32[]{:S(2)}) collective-permute-start(bf16[128,160]{0,1:T(8,128)(2,1)S(1)} %fusion.110), channel_id=1, source_target_pairs={{0,7},{1,0},{2,1},{3,2},{4,3},{5,4},{6,5},{7,6},{8,15},{9,8},{10,9... | collective-permute-start | bytes 122888 | tf_op jit(solution)/shard_map/ppermute | solution.py:106
  83.1 1.8 copy-start.4
  84.9 97.3 %reduce-scatter.2.cloned.1.call-start = ((), (), s32[]{:S(2)}) async-start(), calls=%async_computation.8 | async-start | bytes 1474560 | tf_op jit(solution)/shard_map/reduce_scatter | solution.py:123
  148.3 15.7 %copy-start.2 = (bf16[320,512]{1,0:T(8,128)(2,1)S(1)}, bf16[320,512]{1,0:T(8,128)(2,1)}, u32[]{:S(2)}) copy-start(bf16[320,512]{1,0:T(8,128)(2,1)} %param.23) | copy-start | bytes 983044
  149.3 7.7 %collective-permute-start.10 = (bf16[128,640]{1,0:T(8,128)(2,1)S(1)}, bf16[128,640]{1,0:T(8,128)(2,1)S(1)}, u32[]{:S(2)}, u32[]{:S(2)}) collective-permute-start(bf16[128,640]{1,0:T(8,128)(2,1)S(1)} %get-tuple-element.21), channel_id=1, source_target_pairs={{0,4},{1,5},{2,6},{3,7},{4,0},{5,1},{6,2},{7,3},{8,12},{9,13},{10,... | collective-permute-start | bytes 491528 | tf_op jit(solution)/shard_map/ppermute | solution.py:133
  152.7 11.3 %collective-permute-start.11 = (bf16[128,640]{1,0:T(8,128)(2,1)S(1)}, bf16[128,640]{1,0:T(8,128)(2,1)S(1)}, u32[]{:S(2)}, u32[]{:S(2)}) collective-permute-start(bf16[128,640]{1,0:T(8,128)(2,1)S(1)} %get-tuple-element.20), channel_id=1, source_target_pairs={{0,5},{1,6},{2,7},{3,0},{4,1},{5,2},{6,3},{7,4},{8,13},{9,14},{10,... | collective-permute-start | bytes 491528 | tf_op jit(solution)/shard_map/ppermute | solution.py:133
  154.1 17.7 %collective-permute-start.12 = (bf16[128,640]{1,0:T(8,128)(2,1)}, bf16[128,640]{1,0:T(8,128)(2,1)S(1)}, u32[]{:S(2)}, u32[]{:S(2)}) collective-permute-start(bf16[128,640]{1,0:T(8,128)(2,1)} %get-tuple-element.19), channel_id=1, source_target_pairs={{0,6},{1,7},{2,0},{3,1},{4,2},{5,3},{6,4},{7,5},{8,14},{9,15},{10,... | collective-permute-start | bytes 491528 | tf_op jit(solution)/shard_map/ppermute | solution.py:133
  155.3 17.4 %collective-permute-start.13 = (bf16[128,640]{1,0:T(8,128)(2,1)}, bf16[128,640]{1,0:T(8,128)(2,1)S(1)}, u32[]{:S(2)}, u32[]{:S(2)}) collective-permute-start(bf16[128,640]{1,0:T(8,128)(2,1)} %get-tuple-element.18), channel_id=1, source_target_pairs={{0,7},{1,0},{2,1},{3,2},{4,3},{5,4},{6,5},{7,6},{8,15},{9,8},{10,9... | collective-permute-start | bytes 491528 | tf_op jit(solution)/shard_map/ppermute | solution.py:133
  157.0 15.7 %collective-permute-start.7 = (bf16[128,640]{1,0:T(8,128)(2,1)}, bf16[128,640]{1,0:T(8,128)(2,1)S(1)}, u32[]{:S(2)}, u32[]{:S(2)}) collective-permute-start(bf16[128,640]{1,0:T(8,128)(2,1)} %get-tuple-element.17), channel_id=1, source_target_pairs={{0,1},{1,2},{2,3},{3,4},{4,5},{5,6},{6,7},{7,0},{8,9},{9,10},{10,1... | collective-permute-start | bytes 491528 | tf_op jit(solution)/shard_map/ppermute | solution.py:133
  157.0 15.7 %collective-permute-start.8 = (bf16[128,640]{1,0:T(8,128)(2,1)}, bf16[128,640]{1,0:T(8,128)(2,1)S(1)}, u32[]{:S(2)}, u32[]{:S(2)}) collective-permute-start(bf16[128,640]{1,0:T(8,128)(2,1)} %get-tuple-element.23), channel_id=1, source_target_pairs={{0,2},{1,3},{2,4},{3,5},{4,6},{5,7},{6,0},{7,1},{8,10},{9,11},{10,... | collective-permute-start | bytes 491528 | tf_op jit(solution)/shard_map/ppermute | solution.py:133
  164.0 9.6 %collective-permute-start.9 = (bf16[128,640]{1,0:T(8,128)(2,1)S(1)}, bf16[128,640]{1,0:T(8,128)(2,1)}, u32[]{:S(2)}, u32[]{:S(2)}) collective-permute-start(bf16[128,640]{1,0:T(8,128)(2,1)S(1)} %get-tuple-element.22), channel_id=1, source_target_pairs={{0,3},{1,4},{2,5},{3,6},{4,7},{5,0},{6,1},{7,2},{8,11},{9,12},{10,... | collective-permute-start | bytes 491528 | tf_op jit(solution)/shard_map/ppermute | solution.py:133
  166.9 82.2 %all-to-all-start.2 = ((bf16[16,320,512]{2,1,0:T(8,128)(2,1)}), bf16[16,320,512]{2,1,0:T(8,128)(2,1)}, u32[]{:S(2)}, u32[]{:S(2)}) async-start(bf16[16,320,512]{2,1,0:T(8,128)(2,1)} %broadcast_in_dim.160), calls=%async_computation.3 | async-start | bytes 10485760 | tf_op jit(solution)/shard_map/all_to_all | solution.py:50
  171.5 12.0 %copy-start.7 = (f32[1280]{0:T(1024)S(1)}, f32[1280]{0:T(1024)}, u32[]{:S(2)}) copy-start(f32[1280]{0:T(1024)} %param.22) | copy-start | bytes 15364
  171.5 12.0 %copy-start.8 = (f32[1280]{0:T(1024)S(1)}, f32[1280]{0:T(1024)}, u32[]{:S(2)}) copy-start(f32[1280]{0:T(1024)} %param.21) | copy-start | bytes 15364
  171.5 13.2 %copy-start.9 = (s32[128]{0:T(128)S(1)}, s32[128]{0:T(128)}, u32[]{:S(2)}) copy-start(s32[128]{0:T(128)} %param.14) | copy-start | bytes 1540
  171.5 77.6 %all-gather.12.cloned.1.call-start = ((), (), s32[]{:S(2)}) async-start(), calls=%async_computation.9 | async-start | bytes 2949120 | tf_op jit(solution)/shard_map/all_gather | solution.py:139
  256.6 7.4 %copy-start.12 = (u32[128]{0:T(128)S(1)}, u32[128]{0:T(128)}, u32[]{:S(2)}) copy-start(u32[128]{0:T(128)} %constant.292) | copy-start | bytes 1540
  257.7 17.7 %all-to-all-start.3 = ((bf16[16,48,512]{2,1,0:T(8,128)(2,1)}), bf16[16,48,512]{2,1,0:T(8,128)(2,1)S(1)}, u32[]{:S(2)}, u32[]{:S(2)}) async-start(bf16[16,48,512]{2,1,0:T(8,128)(2,1)} %broadcast_select_fusion), calls=%async_computation.4 | async-start | bytes 1572864 | tf_op jit(solution)/shard_map/all_to_all | solution.py:161
  (3 other events, 3.6 us)
Sparse Core Ops, SparseCore 0:
  12.5 29.6 all-gather.5
  45.8 29.1 all-gather.7
  85.0 28.9 all-gather.9
  148.5 33.5 reduce-scatter.1
  184.8 26.5 all-gather.11

commit v7 on v6

--- a/solution.py
+++ b/solution.py
@@ -119,20 +119,14 @@
         hidden, down_t, contract_t, preferred_element_type=jnp.float32
     )
     mlp_terms = mlp_terms.astype(jnp.bfloat16)
-    split = D // 2
-    head_sum = lax.psum_scatter(
-        mlp_terms[:, :split], "col", scatter_dimension=0, tiled=True
-    ).astype(jnp.float32)
-    tail_terms = mlp_terms[:, split:]
-    tail_sum = jnp.zeros((tok_dev, D - split), jnp.float32)
+    mlp_out = jnp.zeros((tok_dev, D), jnp.float32)
     for shift in range(n_col):
         target = (col_index + shift) % n_col
-        block = lax.dynamic_slice_in_dim(tail_terms, target * tok_dev, tok_dev, 0)
+        block = lax.dynamic_slice_in_dim(mlp_terms, target * tok_dev, tok_dev, 0)
         if shift:
             pairs = [(i, (i + shift) % n_col) for i in range(n_col)]
             block = lax.ppermute(block, "col", pairs)
-        tail_sum = tail_sum + block.astype(jnp.float32)
-    mlp_out = jnp.concatenate([head_sum, tail_sum], axis=1)
+        mlp_out = mlp_out + block.astype(jnp.float32)
     stream = (stream.astype(jnp.float32) + mlp_out).astype(jnp.bfloat16)
     merged = layer_norm(stream.astype(jnp.float32), merge_gain, merge_bias).astype(jnp.bfloat16)
     merged = merged.reshape(tok_dev // 4, 4 * D)

time: 302 us -> 308 us (1.020)
  waiting for transfers between devices: 89.7 us -> 101 us
    all_to_all x1, waiting for transfers between devices: 63.8 us -> 72.3 us  [row_gather(): received = lax.all_to_all(send, 'row', 0, 0, tiled=True)]
    ppermute x14, waiting for transfers between devices: 8.33 us -> 16 us  [local(): block = lax.ppermute(block, 'col', pairs)]
    reduce_scatter x1 -> x0, waiting for transfers between devices: 7.31 us -> none  [local(): lax.psum_scatter(mlp_terms[:, :split], 'col', scatter_dimension=0, tiled=...]
  transfers between devices with their start and end apart: 21 -> 20, of which waited for: 8 -> 8; matrix products, arithmetic and copies ran while one was open for 12% -> 11% of each run, Pallas kernels for 0% -> 0%
where the time goes in v7:
time: 308 us; the launch traced here: 307 us
  waiting for transfers between devices  101 us (33%)
  blocking collectives  94 us (31%)
  matrix products  38.7 us (13%)
  starting transfers between devices  29.6 us (10%)
  between operations  15.2 us (5%)
  local copies, waits for them, and re-layouts  14.9 us (5%)
  other arithmetic  13.9 us (5%)
    all_to_all x2, blocking collectives, row_gather(): received = lax.all_to_all(send, 'row', 0, 0, tiled=True)  77.7 us
    all_to_all x1, waiting for transfers between devices, row_gather(): received = lax.all_to_all(send, 'row', 0, 0, tiled=True)  72.3 us
    ppermute x14, starting transfers between devices, local(): block = lax.ppermute(block, 'col', pairs)  21.2 us
    unnamed x1, blocking collectives  16.3 us
    ppermute x14, waiting for transfers between devices, local(): block = lax.ppermute(block, 'col', pairs)  16 us
    dot_general x1, matrix products, local(): lax.dot_general(hidden, down_t, contract_t, preferred_element_type=jnp.fl...  11.7 us
    all_to_all x1, waiting for transfers between devices, local(): recv = lax.all_to_all(send, 'row', 0, 0, tiled=True)  10.5 us
    sub x2, matrix products, attend(): expo = jnp.exp(scores - peak)  8.43 us
  transfers between devices with their start and end apart: 20, of which 8 were waited for; matrix products, arithmetic and copies ran while one was open for 11% of the time, Pallas kernels for 0%

profile of v7, /device:TPU:1, one launch (start us, length us, event | category | flops | bytes accessed | tf_op | source)
XLA Modules:
  0.0 306.7 jit_solution(17571797988658651779)
XLA Ops:
  10.4 2.0 fusion.89
  14.4 29.9 %all_to_all.20 = bf16[16,80,640]{2,1,0:T(8,128)(2,1)S(1)} all-to-all(bf16[16,80,640]{2,1,0:T(8,128)(2,1)S(1)} %broadcast_in_dim.155), channel_id=1, replica_groups=mesh['row'=16,'col'=8] {'row'}, dimensions={0} | all-to-all | bytes 3276800 | tf_op jit(solution)/shard_map/all_to_all | solution.py:50
  47.2 4.2 %convolution_convert_fusion.9 = bf16[1024,480]{0,1:T(8,128)(2,1)} fusion(bf16[1024,1280]{1,0:T(8,128)(2,1)} %all-gather.6.cloned.1.call-done, bf16[1280,640]{1,0:T(8,128)(2,1)S(1)} %bitcast.97), kind=kOutput, calls=%fused_computation.70 | convolution fusion | flops 1258782720 | bytes 4915200 | tf_op jit(solution)/shard_map/dot_general | solution.py:94
  51.3 4.8 %fusion.169 = (f32[2,512]{1,0:T(2,128)S(1)}, f32[2,512,1024]{2,1,0:T(8,128)}) fusion(pred[512,1024]{1,0:T(8,128)(4,1)S(1)} %get-tuple-element.28, bf16[1024,2,3,80]{0,3,2,1:T(8,128)(2,1)} %bitcast.111), kind=kOutput, calls=%fused_computation.281 | convolution fusion | flops 171967488 | bytes 5214208 | tf_op jit(solution)/shard_map/sub | solution.py:40
  56.1 3.7 %fusion.168 = (f32[2,512]{1,0:T(2,128)S(1)}, f32[2,512,1024]{2,1,0:T(8,128)}) fusion(pred[512,1024]{1,0:T(8,128)(4,1)S(1)} %get-tuple-element.29, bf16[1024,2,3,80]{0,3,2,1:T(8,128)(2,1)S(1)} %bitcast.112), kind=kOutput, calls=%fused_computation.280 | convolution fusion | flops 171967488 | bytes 5214208 | tf_op jit(solution)/shard_map/sub | solution.py:40
  59.8 3.2 %fusion.78 = bf16[2,80,512]{2,1,0:T(8,128)(2,1)S(1)} fusion(f32[2,512,1024]{2,1,0:T(8,128)} %get-tuple-element.35, f32[2,512]{1,0:T(2,128)S(1)} %get-tuple-element.34, bf16[1024,2,3,80]{0,3,2,1:T(8,128)(2,1)S(1)} %bitcast.113), kind=kOutput, calls=%fused_computation.103 | convolution fusion | flops 169951232 | bytes 4689920 | tf_op jit(solution)/shard_map/hqk,khd->qhd/dot_general | solution.py:42
  64.4 3.4 %collective-permute-start = (bf16[128,160]{0,1:T(8,128)(2,1)S(1)}, bf16[128,160]{0,1:T(8,128)(2,1)S(1)}, u32[]{:S(2)}, u32[]{:S(2)}) collective-permute-start(bf16[128,160]{0,1:T(8,128)(2,1)S(1)} %get-tuple-element.23), channel_id=1, source_target_pairs={{0,1},{1,2},{2,3},{3,4},{4,5},{5,6},{6,7},{7,0},{8,9},{9,10},{10,1... | collective-permute-start | bytes 122888 | tf_op jit(solution)/shard_map/ppermute | solution.py:106
  67.8 2.1 collective-permute-start.2
  71.2 2.6 collective-permute-start.4
  73.8 1.6 all-gather.8.cloned.1.call-done
  75.4 1.4 fusion.31
  77.6 1.3 fusion.30
  79.5 1.3 fusion.18
  84.6 47.8 %all_to_all.21 = bf16[16,80,1280]{2,1,0:T(8,128)(2,1)} all-to-all(bf16[16,80,1280]{2,1,0:T(8,128)(2,1)S(1)} %broadcast_in_dim.159), channel_id=1, replica_groups=mesh['row'=16,'col'=8] {'row'}, dimensions={0} | all-to-all | bytes 6553600 | tf_op jit(solution)/shard_map/all_to_all | solution.py:50
  132.4 11.7 %convolution_convert_fusion = bf16[1024,1280]{1,0:T(8,128)(2,1)S(1)} fusion(bf16[1280,1280]{1,0:T(8,128)(2,1)} %bitcast.95, bf16[1024,1280]{1,0:T(8,128)(2,1)} %all-gather.10.cloned.1.call-done), kind=kOutput, calls=%fused_computation.12 | convolution fusion | flops 3399352320 | bytes 8519680 | tf_op jit(solution)/shard_map/dot_general | solution.py:118
  145.3 3.6 %collective-permute-start.10 = (bf16[128,1280]{1,0:T(8,128)(2,1)S(1)}, bf16[128,1280]{1,0:T(8,128)(2,1)}, u32[]{:S(2)}, u32[]{:S(2)}) collective-permute-start(bf16[128,1280]{1,0:T(8,128)(2,1)S(1)} %get-tuple-element.19), channel_id=1, source_target_pairs={{0,4},{1,5},{2,6},{3,7},{4,0},{5,1},{6,2},{7,3},{8,12},{9,13},{10,... | collective-permute-start | bytes 983048 | tf_op jit(solution)/shard_map/ppermute | solution.py:128
  149.0 2.3 collective-permute-start.11
  151.3 1.6 collective-permute-start.13
  153.0 2.0 collective-permute-done.10
  155.0 2.8 collective-permute-start.8
  157.8 9.7 %collective-permute-done.11 = bf16[128,1280]{1,0:T(8,128)(2,1)S(1)} collective-permute-done((bf16[128,1280]{1,0:T(8,128)(2,1)S(1)}, bf16[128,1280]{1,0:T(8,128)(2,1)S(1)}, u32[]{:S(2)}, u32[]{:S(2)}) %collective-permute-start.11) | collective-permute-done | bytes 327712 | tf_op jit(solution)/shard_map/ppermute | solution.py:128
  168.2 2.9 broadcast_in_dim.160
  171.1 4.6 %all-to-all-start.2 = ((bf16[16,320,512]{2,1,0:T(8,128)(2,1)}), bf16[16,320,512]{2,1,0:T(8,128)(2,1)}, u32[]{:S(2)}, u32[]{:S(2)}) async-start(bf16[16,320,512]{2,1,0:T(8,128)(2,1)} %broadcast_in_dim.160), calls=%async_computation.2 | async-start | bytes 10485760 | tf_op jit(solution)/shard_map/all_to_all | solution.py:50
  175.8 1.7 collective-permute-done.13
  177.5 1.8 collective-permute-done.9
  179.3 2.0 convert_reduce_fusion.1
  183.4 72.3 %all-to-all-done.2 = bf16[16,320,512]{2,1,0:T(8,128)(2,1)} async-done(((bf16[16,320,512]{2,1,0:T(8,128)(2,1)}), bf16[16,320,512]{2,1,0:T(8,128)(2,1)}, u32[]{:S(2)}, u32[]{:S(2)}) %all-to-all-start.2) | async-done | bytes 5242912 | tf_op jit(solution)/shard_map/all_to_all | solution.py:50
  255.7 4.8 %convolution_convert_fusion.10 = bf16[256,512]{1,0:T(8,128)(2,1)S(1)} fusion(bf16[256,5120]{1,0:T(8,128)(2,1)} %all-gather.12.cloned.1.call-done, bf16[5120,512]{1,0:T(8,128)(2,1)} %bitcast.19), kind=kOutput, calls=%fused_computation.102 | convolution fusion | flops 1342308352 | bytes 8126464 | tf_op jit(solution)/shard_map/dot_general | solution.py:135
  260.6 2.7 gather_fusion.1
  264.3 3.6 %all-to-all-start.3 = ((bf16[16,48,512]{2,1,0:T(8,128)(2,1)}), bf16[16,48,512]{2,1,0:T(8,128)(2,1)S(1)}, u32[]{:S(2)}, u32[]{:S(2)}) async-start(bf16[16,48,512]{2,1,0:T(8,128)(2,1)} %broadcast_select_fusion), calls=%async_computation.3 | async-start | bytes 1572864 | tf_op jit(solution)/shard_map/all_to_all | solution.py:155
  270.4 10.5 %all-to-all-done.3 = bf16[16,48,512]{2,1,0:T(8,128)(2,1)S(1)} async-done(((bf16[16,48,512]{2,1,0:T(8,128)(2,1)}), bf16[16,48,512]{2,1,0:T(8,128)(2,1)S(1)}, u32[]{:S(2)}, u32[]{:S(2)}) %all-to-all-start.3) | async-done | bytes 786464 | tf_op jit(solution)/shard_map/all_to_all | solution.py:155
  282.1 16.3 %all-reduce.1 = f32[128]{0:T(128)S(1)} all-reduce(f32[128]{0:T(128)S(1)} %maximum_dynamic-update-slice_fusion), channel_id=2, replica_groups=mesh['row'=16,'col'=8] {'col'}, use_global_device_ids=true, to_apply=%add.1 | all-reduce | flops 128 | bytes 1024
  (125 shorter events, 25.4 us)
Async XLA Ops:
  7.2 40.0 %all-gather.6.cloned.1.call-start = ((), (), s32[]{:S(2)}) async-start(), calls=%async_computation.4 | async-start | bytes 2949120 | tf_op jit(solution)/shard_map/all_gather | solution.py:93
  12.4 63.0 %all-gather.8.cloned.1.call-start = ((), (), s32[]{:S(2)}) async-start(), calls=%async_computation.5 | async-start | bytes 3686400 | tf_op jit(solution)/shard_map/all_gather | solution.py:99
  14.4 31.5 %copy-start.6 = (s32[16,8]{0,1:T(8,128)S(1)}, s32[16,8]{0,1:T(8,128)}, u32[]{:S(2)}) copy-start(s32[16,8]{0,1:T(8,128)} %param.13) | copy-start | bytes 1540
  45.6 86.8 %all-gather.10.cloned.1.call-start = ((), (), s32[]{:S(2)}) async-start(), calls=%async_computation.6 | async-start | bytes 2949120 | tf_op jit(solution)/shard_map/all_gather | solution.py:115
  51.3 4.8 %copy-start.11 = (bf16[1024,480]{0,1:T(8,128)(2,1)S(1)}, bf16[1024,480]{0,1:T(8,128)(2,1)}, u32[]{:S(2)}) copy-start(bf16[1024,480]{0,1:T(8,128)(2,1)} %convolution_convert_fusion.9) | copy-start | bytes 2949124
  59.8 3.6 %copy-start.13 = (f32[2,512,1024]{2,1,0:T(8,128)S(1)}, f32[2,512,1024]{2,1,0:T(8,128)}, u32[]{:S(2)}) copy-start(f32[2,512,1024]{2,1,0:T(8,128)} %get-tuple-element.33) | copy-start | bytes 12582916
  64.4 12.5 %collective-permute-start = (bf16[128,160]{0,1:T(8,128)(2,1)S(1)}, bf16[128,160]{0,1:T(8,128)(2,1)S(1)}, u32[]{:S(2)}, u32[]{:S(2)}) collective-permute-start(bf16[128,160]{0,1:T(8,128)(2,1)S(1)} %get-tuple-element.23), channel_id=1, source_target_pairs={{0,1},{1,2},{2,3},{3,4},{4,5},{5,6},{6,7},{7,0},{8,9},{9,10},{10,1... | collective-permute-start | bytes 122888 | tf_op jit(solution)/shard_map/ppermute | solution.py:106
  67.8 11.1 %collective-permute-start.2 = (bf16[128,160]{0,1:T(8,128)(2,1)S(1)}, bf16[128,160]{0,1:T(8,128)(2,1)S(1)}, u32[]{:S(2)}, u32[]{:S(2)}) collective-permute-start(bf16[128,160]{0,1:T(8,128)(2,1)S(1)} %get-tuple-element.24), channel_id=1, source_target_pairs={{0,3},{1,4},{2,5},{3,6},{4,7},{5,0},{6,1},{7,2},{8,11},{9,12},{10,... | collective-permute-start | bytes 122888 | tf_op jit(solution)/shard_map/ppermute | solution.py:106
  69.9 10.8 %collective-permute-start.3 = (bf16[128,160]{0,1:T(8,128)(2,1)S(1)}, bf16[128,160]{0,1:T(8,128)(2,1)S(1)}, u32[]{:S(2)}, u32[]{:S(2)}) collective-permute-start(bf16[128,160]{0,1:T(8,128)(2,1)S(1)} %get-tuple-element.25), channel_id=1, source_target_pairs={{0,4},{1,5},{2,6},{3,7},{4,0},{5,1},{6,2},{7,3},{8,12},{9,13},{10,... | collective-permute-start | bytes 122888 | tf_op jit(solution)/shard_map/ppermute | solution.py:106
  71.2 9.9 %collective-permute-start.4 = (bf16[128,160]{0,1:T(8,128)(2,1)S(1)}, bf16[128,160]{0,1:T(8,128)(2,1)S(1)}, u32[]{:S(2)}, u32[]{:S(2)}) collective-permute-start(bf16[128,160]{0,1:T(8,128)(2,1)S(1)} %get-tuple-element.26), channel_id=1, source_target_pairs={{0,5},{1,6},{2,7},{3,0},{4,1},{5,2},{6,3},{7,4},{8,13},{9,14},{10,... | collective-permute-start | bytes 122888 | tf_op jit(solution)/shard_map/ppermute | solution.py:106
  73.8 7.5 %collective-permute-start.5 = (bf16[128,160]{0,1:T(8,128)(2,1)S(1)}, bf16[128,160]{0,1:T(8,128)(2,1)S(1)}, u32[]{:S(2)}, u32[]{:S(2)}) collective-permute-start(bf16[128,160]{0,1:T(8,128)(2,1)S(1)} %get-tuple-element.27), channel_id=1, source_target_pairs={{0,6},{1,7},{2,0},{3,1},{4,2},{5,3},{6,4},{7,5},{8,14},{9,15},{10,... | collective-permute-start | bytes 122888 | tf_op jit(solution)/shard_map/ppermute | solution.py:106
  75.4 5.3 %copy-start.1 = (bf16[1280,1280]{1,0:T(8,128)(2,1)S(1)}, bf16[1280,1280]{1,0:T(8,128)(2,1)}, u32[]{:S(2)}) copy-start(bf16[1280,1280]{1,0:T(8,128)(2,1)} %all-gather.8.cloned.1.call-done) | copy-start | bytes 9830404
  76.9 5.8 %collective-permute-start.1 = (bf16[128,160]{0,1:T(8,128)(2,1)S(1)}, bf16[128,160]{0,1:T(8,128)(2,1)S(1)}, u32[]{:S(2)}, u32[]{:S(2)}) collective-permute-start(bf16[128,160]{0,1:T(8,128)(2,1)S(1)} %get-tuple-element.22), channel_id=1, source_target_pairs={{0,2},{1,3},{2,4},{3,5},{4,6},{5,7},{6,0},{7,1},{8,10},{9,11},{10,... | collective-permute-start | bytes 122888 | tf_op jit(solution)/shard_map/ppermute | solution.py:106
  78.9 3.8 %copy-start = (bf16[128,1280]{1,0:T(8,128)(2,1)S(1)}, bf16[128,1280]{1,0:T(8,128)(2,1)}, u32[]{:S(2)}) copy-start(bf16[128,1280]{1,0:T(8,128)(2,1)} %param.12) | copy-start | bytes 983044
  78.9 3.4 %collective-permute-start.6 = (bf16[128,160]{0,1:T(8,128)(2,1)S(1)}, bf16[128,160]{0,1:T(8,128)(2,1)S(1)}, u32[]{:S(2)}, u32[]{:S(2)}) collective-permute-start(bf16[128,160]{0,1:T(8,128)(2,1)S(1)} %fusion.109), channel_id=1, source_target_pairs={{0,7},{1,0},{2,1},{3,2},{4,3},{5,4},{6,5},{7,6},{8,15},{9,8},{10,9... | collective-permute-start | bytes 122888 | tf_op jit(solution)/shard_map/ppermute | solution.py:106
  82.6 1.7 copy-start.4
  82.6 1.7 copy-start.5
  144.1 24.1 %copy-start.2 = (bf16[320,512]{1,0:T(8,128)(2,1)S(1)}, bf16[320,512]{1,0:T(8,128)(2,1)}, u32[]{:S(2)}) copy-start(bf16[320,512]{1,0:T(8,128)(2,1)} %param.23) | copy-start | bytes 983044
  145.3 9.7 %collective-permute-start.10 = (bf16[128,1280]{1,0:T(8,128)(2,1)S(1)}, bf16[128,1280]{1,0:T(8,128)(2,1)}, u32[]{:S(2)}, u32[]{:S(2)}) collective-permute-start(bf16[128,1280]{1,0:T(8,128)(2,1)S(1)} %get-tuple-element.19), channel_id=1, source_target_pairs={{0,4},{1,5},{2,6},{3,7},{4,0},{5,1},{6,2},{7,3},{8,12},{9,13},{10,... | collective-permute-start | bytes 983048 | tf_op jit(solution)/shard_map/ppermute | solution.py:128
  149.0 18.5 %collective-permute-start.11 = (bf16[128,1280]{1,0:T(8,128)(2,1)S(1)}, bf16[128,1280]{1,0:T(8,128)(2,1)S(1)}, u32[]{:S(2)}, u32[]{:S(2)}) collective-permute-start(bf16[128,1280]{1,0:T(8,128)(2,1)S(1)} %get-tuple-element.18), channel_id=1, source_target_pairs={{0,5},{1,6},{2,7},{3,0},{4,1},{5,2},{6,3},{7,4},{8,13},{9,14},{10,... | collective-permute-start | bytes 983048 | tf_op jit(solution)/shard_map/ppermute | solution.py:128
  151.2 24.5 %collective-permute-start.12 = (bf16[128,1280]{1,0:T(8,128)(2,1)}, bf16[128,1280]{1,0:T(8,128)(2,1)}, u32[]{:S(2)}, u32[]{:S(2)}) collective-permute-start(bf16[128,1280]{1,0:T(8,128)(2,1)} %get-tuple-element.17), channel_id=1, source_target_pairs={{0,6},{1,7},{2,0},{3,1},{4,2},{5,3},{6,4},{7,5},{8,14},{9,15},{10,... | collective-permute-start | bytes 983048 | tf_op jit(solution)/shard_map/ppermute | solution.py:128
  151.3 26.2 %collective-permute-start.13 = (bf16[128,1280]{1,0:T(8,128)(2,1)}, bf16[128,1280]{1,0:T(8,128)(2,1)}, u32[]{:S(2)}, u32[]{:S(2)}) collective-permute-start(bf16[128,1280]{1,0:T(8,128)(2,1)} %get-tuple-element.16), channel_id=1, source_target_pairs={{0,7},{1,0},{2,1},{3,2},{4,3},{5,4},{6,5},{7,6},{8,15},{9,8},{10,9... | collective-permute-start | bytes 983048 | tf_op jit(solution)/shard_map/ppermute | solution.py:128
  152.9 24.6 %collective-permute-start.7 = (bf16[128,1280]{1,0:T(8,128)(2,1)}, bf16[128,1280]{1,0:T(8,128)(2,1)}, u32[]{:S(2)}, u32[]{:S(2)}) collective-permute-start(bf16[128,1280]{1,0:T(8,128)(2,1)} %get-tuple-element.15), channel_id=1, source_target_pairs={{0,1},{1,2},{2,3},{3,4},{4,5},{5,6},{6,7},{7,0},{8,9},{9,10},{10,1... | collective-permute-start | bytes 983048 | tf_op jit(solution)/shard_map/ppermute | solution.py:128
  155.0 22.5 %collective-permute-start.8 = (bf16[128,1280]{1,0:T(8,128)(2,1)}, bf16[128,1280]{1,0:T(8,128)(2,1)}, u32[]{:S(2)}, u32[]{:S(2)}) collective-permute-start(bf16[128,1280]{1,0:T(8,128)(2,1)} %get-tuple-element.21), channel_id=1, source_target_pairs={{0,2},{1,3},{2,4},{3,5},{4,6},{5,7},{6,0},{7,1},{8,10},{9,11},{10,... | collective-permute-start | bytes 983048 | tf_op jit(solution)/shard_map/ppermute | solution.py:128
  168.2 11.1 %collective-permute-start.9 = (bf16[128,1280]{1,0:T(8,128)(2,1)}, bf16[128,1280]{1,0:T(8,128)(2,1)}, u32[]{:S(2)}, u32[]{:S(2)}) collective-permute-start(bf16[128,1280]{1,0:T(8,128)(2,1)} %get-tuple-element.20), channel_id=1, source_target_pairs={{0,3},{1,4},{2,5},{3,6},{4,7},{5,0},{6,1},{7,2},{8,11},{9,12},{10,... | collective-permute-start | bytes 983048 | tf_op jit(solution)/shard_map/ppermute | solution.py:128
  171.1 84.6 %all-to-all-start.2 = ((bf16[16,320,512]{2,1,0:T(8,128)(2,1)}), bf16[16,320,512]{2,1,0:T(8,128)(2,1)}, u32[]{:S(2)}, u32[]{:S(2)}) async-start(bf16[16,320,512]{2,1,0:T(8,128)(2,1)} %broadcast_in_dim.160), calls=%async_computation.2 | async-start | bytes 10485760 | tf_op jit(solution)/shard_map/all_to_all | solution.py:50
  175.7 5.9 %copy-start.7 = (f32[1280]{0:T(1024)S(1)}, f32[1280]{0:T(1024)}, u32[]{:S(2)}) copy-start(f32[1280]{0:T(1024)} %param.22) | copy-start | bytes 15364
  175.7 5.9 %copy-start.8 = (f32[1280]{0:T(1024)S(1)}, f32[1280]{0:T(1024)}, u32[]{:S(2)}) copy-start(f32[1280]{0:T(1024)} %param.21) | copy-start | bytes 15364
  175.7 7.1 %copy-start.9 = (s32[128]{0:T(128)S(1)}, s32[128]{0:T(128)}, u32[]{:S(2)}) copy-start(s32[128]{0:T(128)} %param.14) | copy-start | bytes 1540
  175.7 80.0 %all-gather.12.cloned.1.call-start = ((), (), s32[]{:S(2)}) async-start(), calls=%async_computation.7 | async-start | bytes 2949120 | tf_op jit(solution)/shard_map/all_gather | solution.py:133
  263.2 5.9 %copy-start.12 = (u32[128]{0:T(128)S(1)}, u32[128]{0:T(128)}, u32[]{:S(2)}) copy-start(u32[128]{0:T(128)} %constant.292) | copy-start | bytes 1540
  264.3 16.6 %all-to-all-start.3 = ((bf16[16,48,512]{2,1,0:T(8,128)(2,1)}), bf16[16,48,512]{2,1,0:T(8,128)(2,1)S(1)}, u32[]{:S(2)}, u32[]{:S(2)}) async-start(bf16[16,48,512]{2,1,0:T(8,128)(2,1)} %broadcast_select_fusion), calls=%async_computation.3 | async-start | bytes 1572864 | tf_op jit(solution)/shard_map/all_to_all | solution.py:155
  (2 other events, 1.9 us)
Sparse Core Ops, SparseCore 0:
  12.5 29.6 all-gather.5
  45.7 29.6 all-gather.7
  84.5 29.4 all-gather.9
  182.9 25.4 all-gather.11

commit v8 on v7

--- a/solution.py
+++ b/solution.py
@@ -161,7 +161,14 @@
     blocks = jnp.where(valid[:, :, None], taken, jnp.zeros_like(taken)).astype(jnp.float32)
     squares = jnp.sum(blocks * blocks, axis=(1, 2))
     peaks = jnp.max(jnp.abs(blocks), axis=(1, 2))
-    stats = lax.all_gather(jnp.concatenate([squares, peaks]), "col", axis=0, tiled=False)
+    mine = jnp.concatenate([squares, peaks])
+    shares = [mine]
+    for shift in range(1, n_col):
+        pairs = [(i, (i + shift) % n_col) for i in range(n_col)]
+        shares.append(lax.ppermute(mine, "col", pairs))
+    by_shift = jnp.stack(shares)
+    order = (col_index - jnp.arange(n_col, dtype=jnp.int32)) % n_col
+    stats = jnp.take(by_shift, order, axis=0)
     squares = jnp.sum(stats[:, :IMG_ROW], axis=0)
     peaks = jnp.max(stats[:, IMG_ROW:], axis=0)
     slot_size = sizes_flat[request].astype(jnp.float32)

time: 308 us -> 306 us (level)
  blocking collectives: 94 us -> 77.7 us
  starting transfers between devices: 29.6 us -> 42.1 us
    unnamed x1 -> x0, blocking collectives: 16.3 us -> none
    ppermute x0 -> x7, starting transfers between devices: none -> 12.6 us  [local(): shares.append(lax.ppermute(mine, 'col', pairs))]
  transfers between devices with their start and end apart: 20 -> 27, of which waited for: 8 -> 10; matrix products, arithmetic and copies ran while one was open for 11% -> 11% of each run, Pallas kernels for 0% -> 0%
where the time goes in v8:
time: 306 us
  waiting for transfers between devices  104 us (34%)
  blocking collectives  77.7 us (25%)
  starting transfers between devices  42.1 us (14%)
  matrix products  38.7 us (13%)
  local copies, waits for them, and re-layouts  14.8 us (5%)
  between operations  14.5 us (5%)
  other arithmetic  13.9 us (5%)
    all_to_all x2, blocking collectives, row_gather(): received = lax.all_to_all(send, 'row', 0, 0, tiled=True)  77.7 us
    all_to_all x1, waiting for transfers between devices, row_gather(): received = lax.all_to_all(send, 'row', 0, 0, tiled=True)  71.5 us
    ppermute x14, starting transfers between devices, local(): block = lax.ppermute(block, 'col', pairs)  21.2 us
    ppermute x14, waiting for transfers between devices, local(): block = lax.ppermute(block, 'col', pairs)  16 us
    ppermute x7, starting transfers between devices, local(): shares.append(lax.ppermute(mine, 'col', pairs))  12.6 us
    all_to_all x1, waiting for transfers between devices, local(): recv = lax.all_to_all(send, 'row', 0, 0, tiled=True)  12.5 us
    dot_general x1, matrix products, local(): lax.dot_general(hidden, down_t, contract_t, preferred_element_type=jnp.fl...  11.7 us
    sub x2, matrix products, attend(): expo = jnp.exp(scores - peak)  8.43 us
  transfers between devices with their start and end apart: 27, of which 10 were waited for; matrix products, arithmetic and copies ran while one was open for 11% of the time, Pallas kernels for 0%

profile of v8, /device:TPU:1, one launch (start us, length us, event | category | flops | bytes accessed | tf_op | source)
XLA Modules:
  0.0 305.6 jit_solution(9406439697963113330)
XLA Ops:
  10.4 2.0 fusion.89
  14.4 29.9 %all_to_all.20 = bf16[16,80,640]{2,1,0:T(8,128)(2,1)S(1)} all-to-all(bf16[16,80,640]{2,1,0:T(8,128)(2,1)S(1)} %broadcast_in_dim.165), channel_id=1, replica_groups=mesh['row'=16,'col'=8] {'row'}, dimensions={0} | all-to-all | bytes 3276800 | tf_op jit(solution)/shard_map/all_to_all | solution.py:50
  47.2 4.2 %convolution_convert_fusion.9 = bf16[1024,480]{0,1:T(8,128)(2,1)} fusion(bf16[1024,1280]{1,0:T(8,128)(2,1)} %all-gather.5.cloned.1.call-done, bf16[1280,640]{1,0:T(8,128)(2,1)S(1)} %bitcast.106), kind=kOutput, calls=%fused_computation.71 | convolution fusion | flops 1258782720 | bytes 4915200 | tf_op jit(solution)/shard_map/dot_general | solution.py:94
  51.3 4.8 %fusion.172 = (f32[2,512]{1,0:T(2,128)S(1)}, f32[2,512,1024]{2,1,0:T(8,128)}) fusion(pred[512,1024]{1,0:T(8,128)(4,1)S(1)} %get-tuple-element.28, bf16[1024,2,3,80]{0,3,2,1:T(8,128)(2,1)} %bitcast.128), kind=kOutput, calls=%fused_computation.296 | convolution fusion | flops 171967488 | bytes 5214208 | tf_op jit(solution)/shard_map/sub | solution.py:40
  56.1 3.7 %fusion.171 = (f32[2,512]{1,0:T(2,128)S(1)}, f32[2,512,1024]{2,1,0:T(8,128)}) fusion(pred[512,1024]{1,0:T(8,128)(4,1)S(1)} %get-tuple-element.29, bf16[1024,2,3,80]{0,3,2,1:T(8,128)(2,1)S(1)} %bitcast.129), kind=kOutput, calls=%fused_computation.295 | convolution fusion | flops 171967488 | bytes 5214208 | tf_op jit(solution)/shard_map/sub | solution.py:40
  59.8 3.2 %fusion.78 = bf16[2,80,512]{2,1,0:T(8,128)(2,1)S(1)} fusion(f32[2,512,1024]{2,1,0:T(8,128)} %get-tuple-element.35, f32[2,512]{1,0:T(2,128)S(1)} %get-tuple-element.34, bf16[1024,2,3,80]{0,3,2,1:T(8,128)(2,1)S(1)} %bitcast.130), kind=kOutput, calls=%fused_computation.104 | convolution fusion | flops 169951232 | bytes 4689920 | tf_op jit(solution)/shard_map/hqk,khd->qhd/dot_general | solution.py:42
  64.4 3.4 %collective-permute-start = (bf16[128,160]{0,1:T(8,128)(2,1)S(1)}, bf16[128,160]{0,1:T(8,128)(2,1)S(1)}, u32[]{:S(2)}, u32[]{:S(2)}) collective-permute-start(bf16[128,160]{0,1:T(8,128)(2,1)S(1)} %get-tuple-element.23), channel_id=1, source_target_pairs={{0,1},{1,2},{2,3},{3,4},{4,5},{5,6},{6,7},{7,0},{8,9},{9,10},{10,1... | collective-permute-start | bytes 122888 | tf_op jit(solution)/shard_map/ppermute | solution.py:106
  67.8 2.1 collective-permute-start.2
  71.2 2.6 collective-permute-start.4
  73.8 1.6 all-gather.7.cloned.1.call-done
  75.4 1.4 fusion.31
  84.6 47.8 %all_to_all.21 = bf16[16,80,1280]{2,1,0:T(8,128)(2,1)} all-to-all(bf16[16,80,1280]{2,1,0:T(8,128)(2,1)S(1)} %broadcast_in_dim.169), channel_id=1, replica_groups=mesh['row'=16,'col'=8] {'row'}, dimensions={0} | all-to-all | bytes 6553600 | tf_op jit(solution)/shard_map/all_to_all | solution.py:50
  132.4 11.7 %convolution_convert_fusion = bf16[1024,1280]{1,0:T(8,128)(2,1)S(1)} fusion(bf16[1280,1280]{1,0:T(8,128)(2,1)} %bitcast.104, bf16[1024,1280]{1,0:T(8,128)(2,1)} %all-gather.9.cloned.1.call-done), kind=kOutput, calls=%fused_computation.13 | convolution fusion | flops 3399352320 | bytes 8519680 | tf_op jit(solution)/shard_map/dot_general | solution.py:118
  145.3 3.7 %collective-permute-start.10 = (bf16[128,1280]{1,0:T(8,128)(2,1)S(1)}, bf16[128,1280]{1,0:T(8,128)(2,1)}, u32[]{:S(2)}, u32[]{:S(2)}) collective-permute-start(bf16[128,1280]{1,0:T(8,128)(2,1)S(1)} %get-tuple-element.19), channel_id=1, source_target_pairs={{0,4},{1,5},{2,6},{3,7},{4,0},{5,1},{6,2},{7,3},{8,12},{9,13},{10,... | collective-permute-start | bytes 983048 | tf_op jit(solution)/shard_map/ppermute | solution.py:128
  149.0 2.3 collective-permute-start.11
  151.3 1.6 collective-permute-start.13
  153.0 2.0 collective-permute-done.10
  155.1 2.7 collective-permute-start.8
  157.8 9.7 %collective-permute-done.11 = bf16[128,1280]{1,0:T(8,128)(2,1)S(1)} collective-permute-done((bf16[128,1280]{1,0:T(8,128)(2,1)S(1)}, bf16[128,1280]{1,0:T(8,128)(2,1)S(1)}, u32[]{:S(2)}, u32[]{:S(2)}) %collective-permute-start.11) | collective-permute-done | bytes 327712 | tf_op jit(solution)/shard_map/ppermute | solution.py:128
  168.2 2.9 broadcast_in_dim.170
  171.1 4.6 %all-to-all-start.2 = ((bf16[16,320,512]{2,1,0:T(8,128)(2,1)}), bf16[16,320,512]{2,1,0:T(8,128)(2,1)}, u32[]{:S(2)}, u32[]{:S(2)}) async-start(bf16[16,320,512]{2,1,0:T(8,128)(2,1)} %broadcast_in_dim.170), calls=%async_computation.2 | async-start | bytes 10485760 | tf_op jit(solution)/shard_map/all_to_all | solution.py:50
  175.8 1.7 collective-permute-done.13
  177.5 1.8 collective-permute-done.9
  179.3 2.0 convert_reduce_fusion.1
  184.2 71.5 %all-to-all-done.2 = bf16[16,320,512]{2,1,0:T(8,128)(2,1)} async-done(((bf16[16,320,512]{2,1,0:T(8,128)(2,1)}), bf16[16,320,512]{2,1,0:T(8,128)(2,1)}, u32[]{:S(2)}, u32[]{:S(2)}) %all-to-all-start.2) | async-done | bytes 5242912 | tf_op jit(solution)/shard_map/all_to_all | solution.py:50
  255.7 4.8 %convolution_convert_fusion.10 = bf16[256,512]{1,0:T(8,128)(2,1)S(1)} fusion(bf16[256,5120]{1,0:T(8,128)(2,1)} %all-gather.11.cloned.1.call-done, bf16[5120,512]{1,0:T(8,128)(2,1)} %bitcast.19), kind=kOutput, calls=%fused_computation.103 | convolution fusion | flops 1342308352 | bytes 8126464 | tf_op jit(solution)/shard_map/dot_general | solution.py:135
  260.6 2.7 gather_fusion.1
  264.3 3.6 %all-to-all-start.3 = ((bf16[16,48,512]{2,1,0:T(8,128)(2,1)}), bf16[16,48,512]{2,1,0:T(8,128)(2,1)S(1)}, u32[]{:S(2)}, u32[]{:S(2)}) async-start(bf16[16,48,512]{2,1,0:T(8,128)(2,1)} %broadcast_select_fusion), calls=%async_computation.3 | async-start | bytes 1572864 | tf_op jit(solution)/shard_map/all_to_all | solution.py:155
  268.4 12.5 %all-to-all-done.3 = bf16[16,48,512]{2,1,0:T(8,128)(2,1)S(1)} async-done(((bf16[16,48,512]{2,1,0:T(8,128)(2,1)}), bf16[16,48,512]{2,1,0:T(8,128)(2,1)S(1)}, u32[]{:S(2)}, u32[]{:S(2)}) %all-to-all-start.3) | async-done | bytes 786464 | tf_op jit(solution)/shard_map/all_to_all | solution.py:155
  282.0 6.3 %collective-permute-start.14 = (f32[16]{0:T(128)S(1)}, f32[16]{0:T(128)S(1)}, u32[]{:S(2)}, u32[]{:S(2)}) collective-permute-start(f32[16]{0:T(128)S(1)} %pad_maximum_fusion.2), channel_id=1, source_target_pairs={{0,1},{1,2},{2,3},{3,4},{4,5},{5,6},{6,7},{7,0},{8,9},{9,10},{10,1... | collective-permute-start | bytes 200 | tf_op jit(solution)/shard_map/ppermute | solution.py:168
  288.3 2.2 collective-permute-start.16
  294.6 1.5 collective-permute-done.18
  (139 shorter events, 32.6 us)
Async XLA Ops:
  7.2 40.0 %all-gather.5.cloned.1.call-start = ((), (), s32[]{:S(2)}) async-start(), calls=%async_computation.4 | async-start | bytes 2949120 | tf_op jit(solution)/shard_map/all_gather | solution.py:93
  12.4 63.0 %all-gather.7.cloned.1.call-start = ((), (), s32[]{:S(2)}) async-start(), calls=%async_computation.5 | async-start | bytes 3686400 | tf_op jit(solution)/shard_map/all_gather | solution.py:99
  14.4 31.5 %copy-start.6 = (s32[16,8]{0,1:T(8,128)S(1)}, s32[16,8]{0,1:T(8,128)}, u32[]{:S(2)}) copy-start(s32[16,8]{0,1:T(8,128)} %param.13) | copy-start | bytes 1540
  45.6 86.8 %all-gather.9.cloned.1.call-start = ((), (), s32[]{:S(2)}) async-start(), calls=%async_computation.6 | async-start | bytes 2949120 | tf_op jit(solution)/shard_map/all_gather | solution.py:115
  64.4 12.5 %collective-permute-start = (bf16[128,160]{0,1:T(8,128)(2,1)S(1)}, bf16[128,160]{0,1:T(8,128)(2,1)S(1)}, u32[]{:S(2)}, u32[]{:S(2)}) collective-permute-start(bf16[128,160]{0,1:T(8,128)(2,1)S(1)} %get-tuple-element.23), channel_id=1, source_target_pairs={{0,1},{1,2},{2,3},{3,4},{4,5},{5,6},{6,7},{7,0},{8,9},{9,10},{10,1... | collective-permute-start | bytes 122888 | tf_op jit(solution)/shard_map/ppermute | solution.py:106
  67.8 11.1 %collective-permute-start.2 = (bf16[128,160]{0,1:T(8,128)(2,1)S(1)}, bf16[128,160]{0,1:T(8,128)(2,1)S(1)}, u32[]{:S(2)}, u32[]{:S(2)}) collective-permute-start(bf16[128,160]{0,1:T(8,128)(2,1)S(1)} %get-tuple-element.24), channel_id=1, source_target_pairs={{0,3},{1,4},{2,5},{3,6},{4,7},{5,0},{6,1},{7,2},{8,11},{9,12},{10,... | collective-permute-start | bytes 122888 | tf_op jit(solution)/shard_map/ppermute | solution.py:106
  69.9 10.8 %collective-permute-start.3 = (bf16[128,160]{0,1:T(8,128)(2,1)S(1)}, bf16[128,160]{0,1:T(8,128)(2,1)S(1)}, u32[]{:S(2)}, u32[]{:S(2)}) collective-permute-start(bf16[128,160]{0,1:T(8,128)(2,1)S(1)} %get-tuple-element.25), channel_id=1, source_target_pairs={{0,4},{1,5},{2,6},{3,7},{4,0},{5,1},{6,2},{7,3},{8,12},{9,13},{10,... | collective-permute-start | bytes 122888 | tf_op jit(solution)/shard_map/ppermute | solution.py:106
  71.2 9.9 %collective-permute-start.4 = (bf16[128,160]{0,1:T(8,128)(2,1)S(1)}, bf16[128,160]{0,1:T(8,128)(2,1)S(1)}, u32[]{:S(2)}, u32[]{:S(2)}) collective-permute-start(bf16[128,160]{0,1:T(8,128)(2,1)S(1)} %get-tuple-element.26), channel_id=1, source_target_pairs={{0,5},{1,6},{2,7},{3,0},{4,1},{5,2},{6,3},{7,4},{8,13},{9,14},{10,... | collective-permute-start | bytes 122888 | tf_op jit(solution)/shard_map/ppermute | solution.py:106
  73.8 7.5 %collective-permute-start.5 = (bf16[128,160]{0,1:T(8,128)(2,1)S(1)}, bf16[128,160]{0,1:T(8,128)(2,1)S(1)}, u32[]{:S(2)}, u32[]{:S(2)}) collective-permute-start(bf16[128,160]{0,1:T(8,128)(2,1)S(1)} %get-tuple-element.27), channel_id=1, source_target_pairs={{0,6},{1,7},{2,0},{3,1},{4,2},{5,3},{6,4},{7,5},{8,14},{9,15},{10,... | collective-permute-start | bytes 122888 | tf_op jit(solution)/shard_map/ppermute | solution.py:106
  76.9 5.8 %collective-permute-start.1 = (bf16[128,160]{0,1:T(8,128)(2,1)S(1)}, bf16[128,160]{0,1:T(8,128)(2,1)S(1)}, u32[]{:S(2)}, u32[]{:S(2)}) collective-permute-start(bf16[128,160]{0,1:T(8,128)(2,1)S(1)} %get-tuple-element.22), channel_id=1, source_target_pairs={{0,2},{1,3},{2,4},{3,5},{4,6},{5,7},{6,0},{7,1},{8,10},{9,11},{10,... | collective-permute-start | bytes 122888 | tf_op jit(solution)/shard_map/ppermute | solution.py:106
  78.9 3.4 %collective-permute-start.6 = (bf16[128,160]{0,1:T(8,128)(2,1)S(1)}, bf16[128,160]{0,1:T(8,128)(2,1)S(1)}, u32[]{:S(2)}, u32[]{:S(2)}) collective-permute-start(bf16[128,160]{0,1:T(8,128)(2,1)S(1)} %fusion.109), channel_id=1, source_target_pairs={{0,7},{1,0},{2,1},{3,2},{4,3},{5,4},{6,5},{7,6},{8,15},{9,8},{10,9... | collective-permute-start | bytes 122888 | tf_op jit(solution)/shard_map/ppermute | solution.py:106
  144.1 24.1 %copy-start.2 = (bf16[320,512]{1,0:T(8,128)(2,1)S(1)}, bf16[320,512]{1,0:T(8,128)(2,1)}, u32[]{:S(2)}) copy-start(bf16[320,512]{1,0:T(8,128)(2,1)} %param.23) | copy-start | bytes 983044
  145.3 9.8 %collective-permute-start.10 = (bf16[128,1280]{1,0:T(8,128)(2,1)S(1)}, bf16[128,1280]{1,0:T(8,128)(2,1)}, u32[]{:S(2)}, u32[]{:S(2)}) collective-permute-start(bf16[128,1280]{1,0:T(8,128)(2,1)S(1)} %get-tuple-element.19), channel_id=1, source_target_pairs={{0,4},{1,5},{2,6},{3,7},{4,0},{5,1},{6,2},{7,3},{8,12},{9,13},{10,... | collective-permute-start | bytes 983048 | tf_op jit(solution)/shard_map/ppermute | solution.py:128
  149.0 18.5 %collective-permute-start.11 = (bf16[128,1280]{1,0:T(8,128)(2,1)S(1)}, bf16[128,1280]{1,0:T(8,128)(2,1)S(1)}, u32[]{:S(2)}, u32[]{:S(2)}) collective-permute-start(bf16[128,1280]{1,0:T(8,128)(2,1)S(1)} %get-tuple-element.18), channel_id=1, source_target_pairs={{0,5},{1,6},{2,7},{3,0},{4,1},{5,2},{6,3},{7,4},{8,13},{9,14},{10,... | collective-permute-start | bytes 983048 | tf_op jit(solution)/shard_map/ppermute | solution.py:128
  151.2 24.5 %collective-permute-start.12 = (bf16[128,1280]{1,0:T(8,128)(2,1)}, bf16[128,1280]{1,0:T(8,128)(2,1)}, u32[]{:S(2)}, u32[]{:S(2)}) collective-permute-start(bf16[128,1280]{1,0:T(8,128)(2,1)} %get-tuple-element.17), channel_id=1, source_target_pairs={{0,6},{1,7},{2,0},{3,1},{4,2},{5,3},{6,4},{7,5},{8,14},{9,15},{10,... | collective-permute-start | bytes 983048 | tf_op jit(solution)/shard_map/ppermute | solution.py:128
  151.3 26.2 %collective-permute-start.13 = (bf16[128,1280]{1,0:T(8,128)(2,1)}, bf16[128,1280]{1,0:T(8,128)(2,1)}, u32[]{:S(2)}, u32[]{:S(2)}) collective-permute-start(bf16[128,1280]{1,0:T(8,128)(2,1)} %get-tuple-element.16), channel_id=1, source_target_pairs={{0,7},{1,0},{2,1},{3,2},{4,3},{5,4},{6,5},{7,6},{8,15},{9,8},{10,9... | collective-permute-start | bytes 983048 | tf_op jit(solution)/shard_map/ppermute | solution.py:128
  152.9 24.6 %collective-permute-start.7 = (bf16[128,1280]{1,0:T(8,128)(2,1)}, bf16[128,1280]{1,0:T(8,128)(2,1)}, u32[]{:S(2)}, u32[]{:S(2)}) collective-permute-start(bf16[128,1280]{1,0:T(8,128)(2,1)} %get-tuple-element.15), channel_id=1, source_target_pairs={{0,1},{1,2},{2,3},{3,4},{4,5},{5,6},{6,7},{7,0},{8,9},{9,10},{10,1... | collective-permute-start | bytes 983048 | tf_op jit(solution)/shard_map/ppermute | solution.py:128
  155.1 22.4 %collective-permute-start.8 = (bf16[128,1280]{1,0:T(8,128)(2,1)}, bf16[128,1280]{1,0:T(8,128)(2,1)}, u32[]{:S(2)}, u32[]{:S(2)}) collective-permute-start(bf16[128,1280]{1,0:T(8,128)(2,1)} %get-tuple-element.21), channel_id=1, source_target_pairs={{0,2},{1,3},{2,4},{3,5},{4,6},{5,7},{6,0},{7,1},{8,10},{9,11},{10,... | collective-permute-start | bytes 983048 | tf_op jit(solution)/shard_map/ppermute | solution.py:128
  168.2 11.1 %collective-permute-start.9 = (bf16[128,1280]{1,0:T(8,128)(2,1)}, bf16[128,1280]{1,0:T(8,128)(2,1)}, u32[]{:S(2)}, u32[]{:S(2)}) collective-permute-start(bf16[128,1280]{1,0:T(8,128)(2,1)} %get-tuple-element.20), channel_id=1, source_target_pairs={{0,3},{1,4},{2,5},{3,6},{4,7},{5,0},{6,1},{7,2},{8,11},{9,12},{10,... | collective-permute-start | bytes 983048 | tf_op jit(solution)/shard_map/ppermute | solution.py:128
  171.1 84.6 %all-to-all-start.2 = ((bf16[16,320,512]{2,1,0:T(8,128)(2,1)}), bf16[16,320,512]{2,1,0:T(8,128)(2,1)}, u32[]{:S(2)}, u32[]{:S(2)}) async-start(bf16[16,320,512]{2,1,0:T(8,128)(2,1)} %broadcast_in_dim.170), calls=%async_computation.2 | async-start | bytes 10485760 | tf_op jit(solution)/shard_map/all_to_all | solution.py:50
  175.7 5.9 %copy-start.7 = (f32[1280]{0:T(1024)S(1)}, f32[1280]{0:T(1024)}, u32[]{:S(2)}) copy-start(f32[1280]{0:T(1024)} %param.22) | copy-start | bytes 15364
  175.7 5.9 %copy-start.8 = (f32[1280]{0:T(1024)S(1)}, f32[1280]{0:T(1024)}, u32[]{:S(2)}) copy-start(f32[1280]{0:T(1024)} %param.21) | copy-start | bytes 15364
  175.7 7.2 %copy-start.9 = (s32[128]{0:T(128)S(1)}, s32[128]{0:T(128)}, u32[]{:S(2)}) copy-start(s32[128]{0:T(128)} %param.14) | copy-start | bytes 1540
  175.7 80.0 %all-gather.11.cloned.1.call-start = ((), (), s32[]{:S(2)}) async-start(), calls=%async_computation.7 | async-start | bytes 2949120 | tf_op jit(solution)/shard_map/all_gather | solution.py:133
  264.3 16.6 %all-to-all-start.3 = ((bf16[16,48,512]{2,1,0:T(8,128)(2,1)}), bf16[16,48,512]{2,1,0:T(8,128)(2,1)S(1)}, u32[]{:S(2)}, u32[]{:S(2)}) async-start(bf16[16,48,512]{2,1,0:T(8,128)(2,1)} %broadcast_select_fusion), calls=%async_computation.3 | async-start | bytes 1572864 | tf_op jit(solution)/shard_map/all_to_all | solution.py:155
  282.0 10.8 %collective-permute-start.14 = (f32[16]{0:T(128)S(1)}, f32[16]{0:T(128)S(1)}, u32[]{:S(2)}, u32[]{:S(2)}) collective-permute-start(f32[16]{0:T(128)S(1)} %pad_maximum_fusion.2), channel_id=1, source_target_pairs={{0,1},{1,2},{2,3},{3,4},{4,5},{5,6},{6,7},{7,0},{8,9},{9,10},{10,1... | collective-permute-start | bytes 200 | tf_op jit(solution)/shard_map/ppermute | solution.py:168
  288.3 5.4 %collective-permute-start.15 = (f32[16]{0:T(128)S(1)}, f32[16]{0:T(128)S(1)}, u32[]{:S(2)}, u32[]{:S(2)}) collective-permute-start(f32[16]{0:T(128)S(1)} %pad_maximum_fusion.2), channel_id=1, source_target_pairs={{0,2},{1,3},{2,4},{3,5},{4,6},{5,7},{6,0},{7,1},{8,10},{9,11},{10,... | collective-permute-start | bytes 200 | tf_op jit(solution)/shard_map/ppermute | solution.py:168
  288.3 6.3 %collective-permute-start.16 = (f32[16]{0:T(128)S(1)}, f32[16]{0:T(128)S(1)}, u32[]{:S(2)}, u32[]{:S(2)}) collective-permute-start(f32[16]{0:T(128)S(1)} %pad_maximum_fusion.2), channel_id=1, source_target_pairs={{0,3},{1,4},{2,5},{3,6},{4,7},{5,0},{6,1},{7,2},{8,11},{9,12},{10,... | collective-permute-start | bytes 200 | tf_op jit(solution)/shard_map/ppermute | solution.py:168
  290.4 4.2 %collective-permute-start.17 = (f32[16]{0:T(128)S(1)}, f32[16]{0:T(128)S(1)}, u32[]{:S(2)}, u32[]{:S(2)}) collective-permute-start(f32[16]{0:T(128)S(1)} %pad_maximum_fusion.2), channel_id=1, source_target_pairs={{0,4},{1,5},{2,6},{3,7},{4,0},{5,1},{6,2},{7,3},{8,12},{9,13},{10,... | collective-permute-start | bytes 200 | tf_op jit(solution)/shard_map/ppermute | solution.py:168
  291.6 4.5 %collective-permute-start.18 = (f32[16]{0:T(128)S(1)}, f32[16]{0:T(128)S(1)}, u32[]{:S(2)}, u32[]{:S(2)}) collective-permute-start(f32[16]{0:T(128)S(1)} %pad_maximum_fusion.2), channel_id=1, source_target_pairs={{0,5},{1,6},{2,7},{3,0},{4,1},{5,2},{6,3},{7,4},{8,13},{9,14},{10,... | collective-permute-start | bytes 200 | tf_op jit(solution)/shard_map/ppermute | solution.py:168
  292.8 3.4 %collective-permute-start.19 = (f32[16]{0:T(128)S(1)}, f32[16]{0:T(128)S(1)}, u32[]{:S(2)}, u32[]{:S(2)}) collective-permute-start(f32[16]{0:T(128)S(1)} %pad_maximum_fusion.2), channel_id=1, source_target_pairs={{0,6},{1,7},{2,0},{3,1},{4,2},{5,3},{6,4},{7,5},{8,14},{9,15},{10,... | collective-permute-start | bytes 200 | tf_op jit(solution)/shard_map/ppermute | solution.py:168
  293.6 3.1 %collective-permute-start.20 = (f32[16]{0:T(128)S(1)}, f32[16]{0:T(128)S(1)}, u32[]{:S(2)}, u32[]{:S(2)}) collective-permute-start(f32[16]{0:T(128)S(1)} %pad_maximum_fusion.2), channel_id=1, source_target_pairs={{0,7},{1,0},{2,1},{3,2},{4,3},{5,4},{6,5},{7,6},{8,15},{9,8},{10,9... | collective-permute-start | bytes 200 | tf_op jit(solution)/shard_map/ppermute | solution.py:168
  (8 other events, 22.8 us)
Sparse Core Ops, SparseCore 0:
  12.5 29.6 all-gather.4
  45.7 29.6 all-gather.6
  84.5 29.4 all-gather.8
  182.9 25.4 all-gather.10

commit v9 on v8

--- a/solution.py
+++ b/solution.py
@@ -130,7 +130,12 @@
     stream = (stream.astype(jnp.float32) + mlp_out).astype(jnp.bfloat16)
     merged = layer_norm(stream.astype(jnp.float32), merge_gain, merge_bias).astype(jnp.bfloat16)
     merged = merged.reshape(tok_dev // 4, 4 * D)
-    merged_all = lax.all_gather(merged, "col", axis=0, tiled=True)
+    gathered = [merged]
+    for shift in range(1, n_col):
+        pairs = [(i, (i + shift) % n_col) for i in range(n_col)]
+        gathered.append(lax.ppermute(merged, "col", pairs))
+    merged_order = (col_index - jnp.arange(n_col, dtype=jnp.int32)) % n_col
+    merged_all = jnp.take(jnp.stack(gathered), merged_order, axis=0).reshape(-1, merged.shape[1])
     out_dev = w_merge.shape[1]
     projected = jnp.dot(merged_all, merge_full, preferred_element_type=jnp.float32).astype(
         jnp.bfloat16

time: 306 us -> 288 us (0.941)
  blocking collectives: 77.7 us -> 29.9 us
  starting transfers between devices: 42.1 us -> 57.8 us
  local copies, waits for them, and re-layouts: 14.8 us -> 22.7 us
  waiting for transfers between devices: 104 us -> 109 us
    all_to_all x2 -> x1, blocking collectives: 77.7 us -> 29.9 us  [row_gather(): received = lax.all_to_all(send, 'row', 0, 0, tiled=True)]
    all_to_all x1 -> x2, waiting for transfers between devices: 71.5 us -> 46.7 us  [row_gather(): received = lax.all_to_all(send, 'row', 0, 0, tiled=True)]
    ppermute x0 -> x7, waiting for transfers between devices: none -> 22.7 us  [local(): gathered.append(lax.ppermute(merged, 'col', pairs))]
    ppermute x14, waiting for transfers between devices: 16 us -> 25 us  [local(): block = lax.ppermute(block, 'col', pairs)]
    all_to_all x1 -> x2, starting transfers between devices: 4.57 us -> 13 us  [row_gather(): received = lax.all_to_all(send, 'row', 0, 0, tiled=True)]
    ppermute x0 -> x7, starting transfers between devices: none -> 6.43 us  [local(): gathered.append(lax.ppermute(merged, 'col', pairs))]
    unnamed x27 -> x32, local copies, waits for them, and re-layouts: 1.21 us -> 5.72 us
  transfers between devices with their start and end apart: 27 -> 34, of which waited for: 10 -> 14; matrix products, arithmetic and copies ran while one was open for 11% -> 20% of each run, Pallas kernels for 0% -> 0%
where the time goes in v9:
time: 288 us; the launch traced here: 287 us
  waiting for transfers between devices  109 us (38%)
  starting transfers between devices  57.8 us (20%)
  matrix products  38.7 us (13%)
  blocking collectives  29.9 us (10%)
  local copies, waits for them, and re-layouts  22.7 us (8%)
  between operations  14.6 us (5%)
  other arithmetic  14.2 us (5%)
    all_to_all x2, waiting for transfers between devices, row_gather(): received = lax.all_to_all(send, 'row', 0, 0, tiled=True)  46.7 us
    all_to_all x1, blocking collectives, row_gather(): received = lax.all_to_all(send, 'row', 0, 0, tiled=True)  29.9 us
    ppermute x14, waiting for transfers between devices, local(): block = lax.ppermute(block, 'col', pairs)  25 us
    ppermute x7, waiting for transfers between devices, local(): gathered.append(lax.ppermute(merged, 'col', pairs))  22.7 us
    ppermute x14, starting transfers between devices, local(): block = lax.ppermute(block, 'col', pairs)  21.9 us
    all_to_all x2, starting transfers between devices, row_gather(): received = lax.all_to_all(send, 'row', 0, 0, tiled=True)  13 us
    all_to_all x1, waiting for transfers between devices, local(): recv = lax.all_to_all(send, 'row', 0, 0, tiled=True)  12.3 us
    dot_general x1, matrix products, local(): lax.dot_general(hidden, down_t, contract_t, preferred_element_type=jnp.fl...  11.7 us
  transfers between devices with their start and end apart: 34, of which 14 were waited for; matrix products, arithmetic and copies ran while one was open for 20% of the time, Pallas kernels for 0%

profile of v9, /device:TPU:1, one launch (start us, length us, event | category | flops | bytes accessed | tf_op | source)
XLA Modules:
  0.0 287.0 jit_solution(1105688887915909217)
XLA Ops:
  10.4 2.0 fusion.89
  14.4 29.9 %all_to_all.20 = bf16[16,80,640]{2,1,0:T(8,128)(2,1)S(1)} all-to-all(bf16[16,80,640]{2,1,0:T(8,128)(2,1)S(1)} %broadcast_in_dim.176), channel_id=1, replica_groups=mesh['row'=16,'col'=8] {'row'}, dimensions={0} | all-to-all | bytes 3276800 | tf_op jit(solution)/shard_map/all_to_all | solution.py:50
  47.2 4.2 %convolution_convert_fusion.9 = bf16[1024,480]{0,1:T(8,128)(2,1)} fusion(bf16[1024,1280]{1,0:T(8,128)(2,1)} %all-gather.4.cloned.1.call-done, bf16[1280,640]{1,0:T(8,128)(2,1)S(1)} %bitcast.120), kind=kOutput, calls=%fused_computation.73 | convolution fusion | flops 1258782720 | bytes 4915200 | tf_op jit(solution)/shard_map/dot_general | solution.py:94
  51.3 4.8 %fusion.172 = (f32[2,512]{1,0:T(2,128)S(1)}, f32[2,512,1024]{2,1,0:T(8,128)}) fusion(pred[512,1024]{1,0:T(8,128)(4,1)S(1)} %get-tuple-element.28, bf16[1024,2,3,80]{0,3,2,1:T(8,128)(2,1)} %bitcast.143), kind=kOutput, calls=%fused_computation.306 | convolution fusion | flops 171967488 | bytes 5214208 | tf_op jit(solution)/shard_map/sub | solution.py:40
  56.1 3.7 %fusion.171 = (f32[2,512]{1,0:T(2,128)S(1)}, f32[2,512,1024]{2,1,0:T(8,128)}) fusion(pred[512,1024]{1,0:T(8,128)(4,1)S(1)} %get-tuple-element.29, bf16[1024,2,3,80]{0,3,2,1:T(8,128)(2,1)S(1)} %bitcast.144), kind=kOutput, calls=%fused_computation.305 | convolution fusion | flops 171967488 | bytes 5214208 | tf_op jit(solution)/shard_map/sub | solution.py:40
  59.8 3.2 %fusion.78 = bf16[2,80,512]{2,1,0:T(8,128)(2,1)S(1)} fusion(f32[2,512,1024]{2,1,0:T(8,128)} %get-tuple-element.35, f32[2,512]{1,0:T(2,128)S(1)} %get-tuple-element.34, bf16[1024,2,3,80]{0,3,2,1:T(8,128)(2,1)S(1)} %bitcast.145), kind=kOutput, calls=%fused_computation.106 | convolution fusion | flops 169951232 | bytes 4689920 | tf_op jit(solution)/shard_map/hqk,khd->qhd/dot_general | solution.py:42
  64.4 3.4 %collective-permute-start = (bf16[128,160]{0,1:T(8,128)(2,1)S(1)}, bf16[128,160]{0,1:T(8,128)(2,1)S(1)}, u32[]{:S(2)}, u32[]{:S(2)}) collective-permute-start(bf16[128,160]{0,1:T(8,128)(2,1)S(1)} %get-tuple-element.23), channel_id=1, source_target_pairs={{0,1},{1,2},{2,3},{3,4},{4,5},{5,6},{6,7},{7,0},{8,9},{9,10},{10,1... | collective-permute-start | bytes 122888 | tf_op jit(solution)/shard_map/ppermute | solution.py:106
  67.8 2.1 collective-permute-start.2
  71.2 2.6 collective-permute-start.4
  86.3 8.4 %all-to-all-start.1 = ((bf16[16,80,1280]{2,1,0:T(8,128)(2,1)}), bf16[16,80,1280]{2,1,0:T(8,128)(2,1)}, u32[]{:S(2)}, u32[]{:S(2)}) async-start(bf16[16,80,1280]{2,1,0:T(8,128)(2,1)} %broadcast_in_dim.180), calls=%async_computation.1 | async-start | bytes 6553600 | tf_op jit(solution)/shard_map/all_to_all | solution.py:50
  95.2 46.7 %all-to-all-done.1 = bf16[16,80,1280]{2,1,0:T(8,128)(2,1)} async-done(((bf16[16,80,1280]{2,1,0:T(8,128)(2,1)}), bf16[16,80,1280]{2,1,0:T(8,128)(2,1)}, u32[]{:S(2)}, u32[]{:S(2)}) %all-to-all-start.1) | async-done | bytes 3276832 | tf_op jit(solution)/shard_map/all_to_all | solution.py:50
  141.9 2.9 broadcast_in_dim.182
  144.7 4.6 %all-to-all-start.2 = ((bf16[16,320,512]{2,1,0:T(8,128)(2,1)}), bf16[16,320,512]{2,1,0:T(8,128)(2,1)}, u32[]{:S(2)}, u32[]{:S(2)}) async-start(bf16[16,320,512]{2,1,0:T(8,128)(2,1)} %broadcast_in_dim.182), calls=%async_computation.2 | async-start | bytes 10485760 | tf_op jit(solution)/shard_map/all_to_all | solution.py:50
  149.3 11.7 %convolution_convert_fusion = bf16[1024,1280]{1,0:T(8,128)(2,1)S(1)} fusion(bf16[1280,1280]{1,0:T(8,128)(2,1)} %bitcast.18, bf16[1024,1280]{1,0:T(8,128)(2,1)} %all-gather.8.cloned.1.call-done), kind=kOutput, calls=%fused_computation.14 | convolution fusion | flops 3399352320 | bytes 8519680 | tf_op jit(solution)/shard_map/dot_general | solution.py:118
  161.3 6.1 %collective-permute-start.10 = (bf16[128,1280]{1,0:T(8,128)(2,1)S(1)}, bf16[128,1280]{1,0:T(8,128)(2,1)S(1)}, u32[]{:S(2)}, u32[]{:S(2)}) collective-permute-start(bf16[128,1280]{1,0:T(8,128)(2,1)S(1)} %get-tuple-element.19), channel_id=1, source_target_pairs={{0,4},{1,5},{2,6},{3,7},{4,0},{5,1},{6,2},{7,3},{8,12},{9,13},{10,... | collective-permute-start | bytes 983048 | tf_op jit(solution)/shard_map/ppermute | solution.py:128
  167.4 2.0 collective-permute-start.11
  171.3 3.5 %collective-permute-done.10 = bf16[128,1280]{1,0:T(8,128)(2,1)S(1)} collective-permute-done((bf16[128,1280]{1,0:T(8,128)(2,1)S(1)}, bf16[128,1280]{1,0:T(8,128)(2,1)S(1)}, u32[]{:S(2)}, u32[]{:S(2)}) %collective-permute-start.10) | collective-permute-done | bytes 327712 | tf_op jit(solution)/shard_map/ppermute | solution.py:128
  176.0 9.0 %collective-permute-done.11 = bf16[128,1280]{1,0:T(8,128)(2,1)S(1)} collective-permute-done((bf16[128,1280]{1,0:T(8,128)(2,1)S(1)}, bf16[128,1280]{1,0:T(8,128)(2,1)S(1)}, u32[]{:S(2)}, u32[]{:S(2)}) %collective-permute-start.11) | collective-permute-done | bytes 327712 | tf_op jit(solution)/shard_map/ppermute | solution.py:128
  185.2 9.0 %collective-permute-done.12 = bf16[128,1280]{1,0:T(8,128)(2,1)S(1)} collective-permute-done((bf16[128,1280]{1,0:T(8,128)(2,1)S(1)}, bf16[128,1280]{1,0:T(8,128)(2,1)S(1)}, u32[]{:S(2)}, u32[]{:S(2)}) %collective-permute-start.12) | collective-permute-done | bytes 327712 | tf_op jit(solution)/shard_map/ppermute | solution.py:128
  194.1 1.9 collective-permute-done.13
  200.1 2.4 collective-permute-start.16
  207.6 6.3 %collective-permute-done.15 = bf16[32,5120]{1,0:T(8,128)(2,1)S(1)} collective-permute-done((bf16[32,5120]{1,0:T(8,128)(2,1)S(1)}, bf16[32,5120]{1,0:T(8,128)(2,1)S(1)}, u32[]{:S(2)}, u32[]{:S(2)}) %collective-permute-start.15) | collective-permute-done | bytes 327712 | tf_op jit(solution)/shard_map/ppermute | solution.py:136
  214.7 6.3 %collective-permute-done.16 = bf16[32,5120]{1,0:T(8,128)(2,1)S(1)} collective-permute-done((bf16[32,5120]{1,0:T(8,128)(2,1)S(1)}, bf16[32,5120]{1,0:T(8,128)(2,1)S(1)}, u32[]{:S(2)}, u32[]{:S(2)}) %collective-permute-start.16) | collective-permute-done | bytes 327712 | tf_op jit(solution)/shard_map/ppermute | solution.py:136
  221.7 8.8 %collective-permute-done.17 = bf16[32,5120]{1,0:T(8,128)(2,1)S(1)} collective-permute-done((bf16[32,5120]{1,0:T(8,128)(2,1)S(1)}, bf16[32,5120]{1,0:T(8,128)(2,1)S(1)}, u32[]{:S(2)}, u32[]{:S(2)}) %collective-permute-start.17) | collective-permute-done | bytes 327712 | tf_op jit(solution)/shard_map/ppermute | solution.py:136
  233.5 2.5 gather_fusion.1
  237.8 4.8 %convolution_convert_fusion.10 = bf16[256,512]{1,0:T(8,128)(2,1)S(1)} fusion(bf16[256,5120]{1,0:T(8,128)(2,1)} %bitcast.122, bf16[5120,512]{1,0:T(8,128)(2,1)} %bitcast.28), kind=kOutput, calls=%fused_computation.105 | convolution fusion | flops 1342308352 | bytes 8126464 | tf_op jit(solution)/shard_map/dot_general | solution.py:140
  242.6 2.7 gather_fusion.2
  246.3 6.5 %all-to-all-start.3 = ((bf16[16,48,512]{2,1,0:T(8,128)(2,1)}), bf16[16,48,512]{2,1,0:T(8,128)(2,1)S(1)}, u32[]{:S(2)}, u32[]{:S(2)}) async-start(bf16[16,48,512]{2,1,0:T(8,128)(2,1)} %broadcast_select_fusion.1), calls=%async_computation.3 | async-start | bytes 1572864 | tf_op jit(solution)/shard_map/all_to_all | solution.py:160
  254.1 12.3 %all-to-all-done.3 = bf16[16,48,512]{2,1,0:T(8,128)(2,1)S(1)} async-done(((bf16[16,48,512]{2,1,0:T(8,128)(2,1)}), bf16[16,48,512]{2,1,0:T(8,128)(2,1)S(1)}, u32[]{:S(2)}, u32[]{:S(2)}) %all-to-all-start.3) | async-done | bytes 786464 | tf_op jit(solution)/shard_map/all_to_all | solution.py:160
  267.5 3.4 %collective-permute-start.22 = (f32[16]{0:T(128)S(1)}, f32[16]{0:T(128)S(1)}, u32[]{:S(2)}, u32[]{:S(2)}) collective-permute-start(f32[16]{0:T(128)S(1)} %pad_maximum_fusion.2), channel_id=1, source_target_pairs={{0,2},{1,3},{2,4},{3,5},{4,6},{5,7},{6,0},{7,1},{8,10},{9,11},{10,... | collective-permute-start | bytes 200 | tf_op jit(solution)/shard_map/ppermute | solution.py:173
  271.7 2.2 collective-permute-start.25
  274.7 2.5 collective-permute-start.27
  (160 shorter events, 50.1 us)
Async XLA Ops:
  7.2 40.0 %all-gather.4.cloned.1.call-start = ((), (), s32[]{:S(2)}) async-start(), calls=%async_computation.4 | async-start | bytes 2949120 | tf_op jit(solution)/shard_map/all_gather | solution.py:93
  12.4 63.0 %all-gather.6.cloned.1.call-start = ((), (), s32[]{:S(2)}) async-start(), calls=%async_computation.5 | async-start | bytes 3686400 | tf_op jit(solution)/shard_map/all_gather | solution.py:99
  45.6 103.7 %all-gather.8.cloned.1.call-start = ((), (), s32[]{:S(2)}) async-start(), calls=%async_computation.6 | async-start | bytes 2949120 | tf_op jit(solution)/shard_map/all_gather | solution.py:115
  64.4 12.5 %collective-permute-start = (bf16[128,160]{0,1:T(8,128)(2,1)S(1)}, bf16[128,160]{0,1:T(8,128)(2,1)S(1)}, u32[]{:S(2)}, u32[]{:S(2)}) collective-permute-start(bf16[128,160]{0,1:T(8,128)(2,1)S(1)} %get-tuple-element.23), channel_id=1, source_target_pairs={{0,1},{1,2},{2,3},{3,4},{4,5},{5,6},{6,7},{7,0},{8,9},{9,10},{10,1... | collective-permute-start | bytes 122888 | tf_op jit(solution)/shard_map/ppermute | solution.py:106
  67.8 11.1 %collective-permute-start.2 = (bf16[128,160]{0,1:T(8,128)(2,1)S(1)}, bf16[128,160]{0,1:T(8,128)(2,1)S(1)}, u32[]{:S(2)}, u32[]{:S(2)}) collective-permute-start(bf16[128,160]{0,1:T(8,128)(2,1)S(1)} %get-tuple-element.24), channel_id=1, source_target_pairs={{0,3},{1,4},{2,5},{3,6},{4,7},{5,0},{6,1},{7,2},{8,11},{9,12},{10,... | collective-permute-start | bytes 122888 | tf_op jit(solution)/shard_map/ppermute | solution.py:106
  69.9 10.8 %collective-permute-start.3 = (bf16[128,160]{0,1:T(8,128)(2,1)S(1)}, bf16[128,160]{0,1:T(8,128)(2,1)S(1)}, u32[]{:S(2)}, u32[]{:S(2)}) collective-permute-start(bf16[128,160]{0,1:T(8,128)(2,1)S(1)} %get-tuple-element.25), channel_id=1, source_target_pairs={{0,4},{1,5},{2,6},{3,7},{4,0},{5,1},{6,2},{7,3},{8,12},{9,13},{10,... | collective-permute-start | bytes 122888 | tf_op jit(solution)/shard_map/ppermute | solution.py:106
  71.2 9.9 %collective-permute-start.4 = (bf16[128,160]{0,1:T(8,128)(2,1)S(1)}, bf16[128,160]{0,1:T(8,128)(2,1)S(1)}, u32[]{:S(2)}, u32[]{:S(2)}) collective-permute-start(bf16[128,160]{0,1:T(8,128)(2,1)S(1)} %get-tuple-element.26), channel_id=1, source_target_pairs={{0,5},{1,6},{2,7},{3,0},{4,1},{5,2},{6,3},{7,4},{8,13},{9,14},{10,... | collective-permute-start | bytes 122888 | tf_op jit(solution)/shard_map/ppermute | solution.py:106
  73.8 7.5 %collective-permute-start.5 = (bf16[128,160]{0,1:T(8,128)(2,1)S(1)}, bf16[128,160]{0,1:T(8,128)(2,1)S(1)}, u32[]{:S(2)}, u32[]{:S(2)}) collective-permute-start(bf16[128,160]{0,1:T(8,128)(2,1)S(1)} %get-tuple-element.27), channel_id=1, source_target_pairs={{0,6},{1,7},{2,0},{3,1},{4,2},{5,3},{6,4},{7,5},{8,14},{9,15},{10,... | collective-permute-start | bytes 122888 | tf_op jit(solution)/shard_map/ppermute | solution.py:106
  76.9 5.8 %collective-permute-start.1 = (bf16[128,160]{0,1:T(8,128)(2,1)S(1)}, bf16[128,160]{0,1:T(8,128)(2,1)S(1)}, u32[]{:S(2)}, u32[]{:S(2)}) collective-permute-start(bf16[128,160]{0,1:T(8,128)(2,1)S(1)} %get-tuple-element.22), channel_id=1, source_target_pairs={{0,2},{1,3},{2,4},{3,5},{4,6},{5,7},{6,0},{7,1},{8,10},{9,11},{10,... | collective-permute-start | bytes 122888 | tf_op jit(solution)/shard_map/ppermute | solution.py:106
  78.9 3.4 %collective-permute-start.6 = (bf16[128,160]{0,1:T(8,128)(2,1)S(1)}, bf16[128,160]{0,1:T(8,128)(2,1)S(1)}, u32[]{:S(2)}, u32[]{:S(2)}) collective-permute-start(bf16[128,160]{0,1:T(8,128)(2,1)S(1)} %fusion.109), channel_id=1, source_target_pairs={{0,7},{1,0},{2,1},{3,2},{4,3},{5,4},{6,5},{7,6},{8,15},{9,8},{10,9... | collective-permute-start | bytes 122888 | tf_op jit(solution)/shard_map/ppermute | solution.py:106
  86.3 55.6 %all-to-all-start.1 = ((bf16[16,80,1280]{2,1,0:T(8,128)(2,1)}), bf16[16,80,1280]{2,1,0:T(8,128)(2,1)}, u32[]{:S(2)}, u32[]{:S(2)}) async-start(bf16[16,80,1280]{2,1,0:T(8,128)(2,1)} %broadcast_in_dim.180), calls=%async_computation.1 | async-start | bytes 6553600 | tf_op jit(solution)/shard_map/all_to_all | solution.py:50
  144.7 93.0 %all-to-all-start.2 = ((bf16[16,320,512]{2,1,0:T(8,128)(2,1)}), bf16[16,320,512]{2,1,0:T(8,128)(2,1)}, u32[]{:S(2)}, u32[]{:S(2)}) async-start(bf16[16,320,512]{2,1,0:T(8,128)(2,1)} %broadcast_in_dim.182), calls=%async_computation.2 | async-start | bytes 10485760 | tf_op jit(solution)/shard_map/all_to_all | solution.py:50
  161.3 13.5 %collective-permute-start.10 = (bf16[128,1280]{1,0:T(8,128)(2,1)S(1)}, bf16[128,1280]{1,0:T(8,128)(2,1)S(1)}, u32[]{:S(2)}, u32[]{:S(2)}) collective-permute-start(bf16[128,1280]{1,0:T(8,128)(2,1)S(1)} %get-tuple-element.19), channel_id=1, source_target_pairs={{0,4},{1,5},{2,6},{3,7},{4,0},{5,1},{6,2},{7,3},{8,12},{9,13},{10,... | collective-permute-start | bytes 983048 | tf_op jit(solution)/shard_map/ppermute | solution.py:128
  167.4 17.7 %collective-permute-start.11 = (bf16[128,1280]{1,0:T(8,128)(2,1)S(1)}, bf16[128,1280]{1,0:T(8,128)(2,1)S(1)}, u32[]{:S(2)}, u32[]{:S(2)}) collective-permute-start(bf16[128,1280]{1,0:T(8,128)(2,1)S(1)} %get-tuple-element.18), channel_id=1, source_target_pairs={{0,5},{1,6},{2,7},{3,0},{4,1},{5,2},{6,3},{7,4},{8,13},{9,14},{10,... | collective-permute-start | bytes 983048 | tf_op jit(solution)/shard_map/ppermute | solution.py:128
  169.5 24.7 %collective-permute-start.12 = (bf16[128,1280]{1,0:T(8,128)(2,1)S(1)}, bf16[128,1280]{1,0:T(8,128)(2,1)S(1)}, u32[]{:S(2)}, u32[]{:S(2)}) collective-permute-start(bf16[128,1280]{1,0:T(8,128)(2,1)S(1)} %get-tuple-element.17), channel_id=1, source_target_pairs={{0,6},{1,7},{2,0},{3,1},{4,2},{5,3},{6,4},{7,5},{8,14},{9,15},{10,... | collective-permute-start | bytes 983048 | tf_op jit(solution)/shard_map/ppermute | solution.py:128
  169.5 26.5 %collective-permute-start.13 = (bf16[128,1280]{1,0:T(8,128)(2,1)S(1)}, bf16[128,1280]{1,0:T(8,128)(2,1)S(1)}, u32[]{:S(2)}, u32[]{:S(2)}) collective-permute-start(bf16[128,1280]{1,0:T(8,128)(2,1)S(1)} %get-tuple-element.16), channel_id=1, source_target_pairs={{0,7},{1,0},{2,1},{3,2},{4,3},{5,4},{6,5},{7,6},{8,15},{9,8},{10,9... | collective-permute-start | bytes 983048 | tf_op jit(solution)/shard_map/ppermute | solution.py:128
  170.6 25.5 %collective-permute-start.7 = (bf16[128,1280]{1,0:T(8,128)(2,1)S(1)}, bf16[128,1280]{1,0:T(8,128)(2,1)S(1)}, u32[]{:S(2)}, u32[]{:S(2)}) collective-permute-start(bf16[128,1280]{1,0:T(8,128)(2,1)S(1)} %get-tuple-element.15), channel_id=1, source_target_pairs={{0,1},{1,2},{2,3},{3,4},{4,5},{5,6},{6,7},{7,0},{8,9},{9,10},{10,1... | collective-permute-start | bytes 983048 | tf_op jit(solution)/shard_map/ppermute | solution.py:128
  174.8 21.2 %collective-permute-start.8 = (bf16[128,1280]{1,0:T(8,128)(2,1)S(1)}, bf16[128,1280]{1,0:T(8,128)(2,1)S(1)}, u32[]{:S(2)}, u32[]{:S(2)}) collective-permute-start(bf16[128,1280]{1,0:T(8,128)(2,1)S(1)} %get-tuple-element.21), channel_id=1, source_target_pairs={{0,2},{1,3},{2,4},{3,5},{4,6},{5,7},{6,0},{7,1},{8,10},{9,11},{10,... | collective-permute-start | bytes 983048 | tf_op jit(solution)/shard_map/ppermute | solution.py:128
  185.1 11.8 %collective-permute-start.9 = (bf16[128,1280]{1,0:T(8,128)(2,1)S(1)}, bf16[128,1280]{1,0:T(8,128)(2,1)S(1)}, u32[]{:S(2)}, u32[]{:S(2)}) collective-permute-start(bf16[128,1280]{1,0:T(8,128)(2,1)S(1)} %get-tuple-element.20), channel_id=1, source_target_pairs={{0,3},{1,4},{2,5},{3,6},{4,7},{5,0},{6,1},{7,2},{8,11},{9,12},{10,... | collective-permute-start | bytes 983048 | tf_op jit(solution)/shard_map/ppermute | solution.py:128
  198.3 8.6 %collective-permute-start.14 = (bf16[32,5120]{1,0:T(8,128)(2,1)S(1)}, bf16[32,5120]{1,0:T(8,128)(2,1)S(1)}, u32[]{:S(2)}, u32[]{:S(2)}) collective-permute-start(bf16[32,5120]{1,0:T(8,128)(2,1)S(1)} %reshape.361), channel_id=1, source_target_pairs={{0,1},{1,2},{2,3},{3,4},{4,5},{5,6},{6,7},{7,0},{8,9},{9,10},{10,1... | collective-permute-start | bytes 983048 | tf_op jit(solution)/shard_map/ppermute | solution.py:136
  200.1 13.8 %collective-permute-start.15 = (bf16[32,5120]{1,0:T(8,128)(2,1)S(1)}, bf16[32,5120]{1,0:T(8,128)(2,1)S(1)}, u32[]{:S(2)}, u32[]{:S(2)}) collective-permute-start(bf16[32,5120]{1,0:T(8,128)(2,1)S(1)} %reshape.361), channel_id=1, source_target_pairs={{0,2},{1,3},{2,4},{3,5},{4,6},{5,7},{6,0},{7,1},{8,10},{9,11},{10,... | collective-permute-start | bytes 983048 | tf_op jit(solution)/shard_map/ppermute | solution.py:136
  200.1 20.9 %collective-permute-start.16 = (bf16[32,5120]{1,0:T(8,128)(2,1)S(1)}, bf16[32,5120]{1,0:T(8,128)(2,1)S(1)}, u32[]{:S(2)}, u32[]{:S(2)}) collective-permute-start(bf16[32,5120]{1,0:T(8,128)(2,1)S(1)} %reshape.361), channel_id=1, source_target_pairs={{0,3},{1,4},{2,5},{3,6},{4,7},{5,0},{6,1},{7,2},{8,11},{9,12},{10,... | collective-permute-start | bytes 983048 | tf_op jit(solution)/shard_map/ppermute | solution.py:136
  202.5 28.0 %collective-permute-start.17 = (bf16[32,5120]{1,0:T(8,128)(2,1)S(1)}, bf16[32,5120]{1,0:T(8,128)(2,1)S(1)}, u32[]{:S(2)}, u32[]{:S(2)}) collective-permute-start(bf16[32,5120]{1,0:T(8,128)(2,1)S(1)} %reshape.361), channel_id=1, source_target_pairs={{0,4},{1,5},{2,6},{3,7},{4,0},{5,1},{6,2},{7,3},{8,12},{9,13},{10,... | collective-permute-start | bytes 983048 | tf_op jit(solution)/shard_map/ppermute | solution.py:136
  203.4 27.8 %collective-permute-start.18 = (bf16[32,5120]{1,0:T(8,128)(2,1)S(1)}, bf16[32,5120]{1,0:T(8,128)(2,1)S(1)}, u32[]{:S(2)}, u32[]{:S(2)}) collective-permute-start(bf16[32,5120]{1,0:T(8,128)(2,1)S(1)} %reshape.361), channel_id=1, source_target_pairs={{0,5},{1,6},{2,7},{3,0},{4,1},{5,2},{6,3},{7,4},{8,13},{9,14},{10,... | collective-permute-start | bytes 983048 | tf_op jit(solution)/shard_map/ppermute | solution.py:136
  206.9 25.1 %collective-permute-start.19 = (bf16[32,5120]{1,0:T(8,128)(2,1)S(1)}, bf16[32,5120]{1,0:T(8,128)(2,1)S(1)}, u32[]{:S(2)}, u32[]{:S(2)}) collective-permute-start(bf16[32,5120]{1,0:T(8,128)(2,1)S(1)} %reshape.361), channel_id=1, source_target_pairs={{0,6},{1,7},{2,0},{3,1},{4,2},{5,3},{6,4},{7,5},{8,14},{9,15},{10,... | collective-permute-start | bytes 983048 | tf_op jit(solution)/shard_map/ppermute | solution.py:136
  213.9 18.8 %collective-permute-start.20 = (bf16[32,5120]{1,0:T(8,128)(2,1)S(1)}, bf16[32,5120]{1,0:T(8,128)(2,1)S(1)}, u32[]{:S(2)}, u32[]{:S(2)}) collective-permute-start(bf16[32,5120]{1,0:T(8,128)(2,1)S(1)} %reshape.361), channel_id=1, source_target_pairs={{0,7},{1,0},{2,1},{3,2},{4,3},{5,4},{6,5},{7,6},{8,15},{9,8},{10,9... | collective-permute-start | bytes 983048 | tf_op jit(solution)/shard_map/ppermute | solution.py:136
  246.3 20.1 %all-to-all-start.3 = ((bf16[16,48,512]{2,1,0:T(8,128)(2,1)}), bf16[16,48,512]{2,1,0:T(8,128)(2,1)S(1)}, u32[]{:S(2)}, u32[]{:S(2)}) async-start(bf16[16,48,512]{2,1,0:T(8,128)(2,1)} %broadcast_select_fusion.1), calls=%async_computation.3 | async-start | bytes 1572864 | tf_op jit(solution)/shard_map/all_to_all | solution.py:160
  267.5 6.4 %collective-permute-start.21 = (f32[16]{0:T(128)S(1)}, f32[16]{0:T(128)S(1)}, u32[]{:S(2)}, u32[]{:S(2)}) collective-permute-start(f32[16]{0:T(128)S(1)} %pad_maximum_fusion.2), channel_id=1, source_target_pairs={{0,1},{1,2},{2,3},{3,4},{4,5},{5,6},{6,7},{7,0},{8,9},{9,10},{10,1... | collective-permute-start | bytes 200 | tf_op jit(solution)/shard_map/ppermute | solution.py:173
  267.5 7.2 %collective-permute-start.22 = (f32[16]{0:T(128)S(1)}, f32[16]{0:T(128)S(1)}, u32[]{:S(2)}, u32[]{:S(2)}) collective-permute-start(f32[16]{0:T(128)S(1)} %pad_maximum_fusion.2), channel_id=1, source_target_pairs={{0,2},{1,3},{2,4},{3,5},{4,6},{5,7},{6,0},{7,1},{8,10},{9,11},{10,... | collective-permute-start | bytes 200 | tf_op jit(solution)/shard_map/ppermute | solution.py:173
  270.9 6.4 %collective-permute-start.23 = (f32[16]{0:T(128)S(1)}, f32[16]{0:T(128)S(1)}, u32[]{:S(2)}, u32[]{:S(2)}) collective-permute-start(f32[16]{0:T(128)S(1)} %pad_maximum_fusion.2), channel_id=1, source_target_pairs={{0,3},{1,4},{2,5},{3,6},{4,7},{5,0},{6,1},{7,2},{8,11},{9,12},{10,... | collective-permute-start | bytes 200 | tf_op jit(solution)/shard_map/ppermute | solution.py:173
  271.7 5.6 %collective-permute-start.24 = (f32[16]{0:T(128)S(1)}, f32[16]{0:T(128)S(1)}, u32[]{:S(2)}, u32[]{:S(2)}) collective-permute-start(f32[16]{0:T(128)S(1)} %pad_maximum_fusion.2), channel_id=1, source_target_pairs={{0,4},{1,5},{2,6},{3,7},{4,0},{5,1},{6,2},{7,3},{8,12},{9,13},{10,... | collective-permute-start | bytes 200 | tf_op jit(solution)/shard_map/ppermute | solution.py:173
  271.7 5.6 %collective-permute-start.25 = (f32[16]{0:T(128)S(1)}, f32[16]{0:T(128)S(1)}, u32[]{:S(2)}, u32[]{:S(2)}) collective-permute-start(f32[16]{0:T(128)S(1)} %pad_maximum_fusion.2), channel_id=1, source_target_pairs={{0,5},{1,6},{2,7},{3,0},{4,1},{5,2},{6,3},{7,4},{8,13},{9,14},{10,... | collective-permute-start | bytes 200 | tf_op jit(solution)/shard_map/ppermute | solution.py:173
  (14 other events, 197.0 us)
Sparse Core Ops, SparseCore 0:
  12.5 29.6 all-gather.3
  45.7 29.6 all-gather.5
  84.5 29.6 all-gather.7
